TPU v7x, 512 devices: a whole 4x8x8 slice. The times are simulated.
512 devices in a mesh: slab: 128 (over z, y, core), chan: 4 (over x).
Axes of the slice: x: 4, y: 8, z: 8, core: 2. Of those that a mesh axis runs over, the one named last changes fastest.
Arguments:
- field: bfloat16 [64, 256, 4096], P(None, 'slab'), may hold values from -6 to 6
- cotangent: bfloat16 [64, 256, 4096], P(None, 'slab'), may hold values from -10 to 10
- spectral_weight: bfloat16 [2, 64, 64, 512, 32], P(None, 'chan', None, 'slab'), may hold values from -4 to 4
- point_weight: bfloat16 [64, 64], replicated, may hold values from -0.75 to 0.75
- point_bias: bfloat16 [64], replicated, may hold values from -2 to 2
Outputs:
- grad_input: bfloat16 [64, 256, 4096], P('chan', 'slab')
- grad_spectral: float32 [2, 64, 64, 512, 32], P(None, 'chan', None, 'slab')
- grad_pointwise: float32 [64, 64], P('chan')
- grad_bias: float32 [64], replicated
All inputs are finite; a program needn't handle non-finite values.
Results may differ from a plain program's by a relative error of at most 0.023.
Values may be sent and summed in bfloat16 or wider, within the bound.
No kernel may reach another device: no remote copies, remote signals or barrier semaphores. Data moves between devices by JAX's collectives and lax.ppermute only.
A program may use at most 64 MiB of HBM per device.

v0:
```python
import math

import jax
import jax.numpy as jnp
from jax import lax
from jax.sharding import PartitionSpec as P

MX = 32
MY = 32
MZ = 16
NX = 256
NY = 64
NZ = 64


def kept_modes(total, length):
    mode_index = jnp.arange(total, dtype=jnp.int32)
    return jnp.where(mode_index < total // 2, mode_index, mode_index - total + length)


def phases(frequency, length):
    positions = jnp.arange(length, dtype=jnp.int32)
    wound_up = frequency[:, None] * positions[None, :] % length
    return 2.0 * math.pi / length * wound_up.astype(jnp.float32)


def make_tables():
    angle_z = phases(jnp.arange(MZ, dtype=jnp.int32), NZ)
    cosine_z = jnp.cos(angle_z)
    sine_z = jnp.sin(angle_z)
    forward_z = jnp.stack([cosine_z.T, -sine_z.T], 1).astype(jnp.bfloat16)
    weight_z = (jnp.where(jnp.arange(MZ) == 0, 1.0, 2.0) / (NX * NY * NZ)).astype(jnp.float32)
    scaled_z = jnp.stack([weight_z[:, None] * cosine_z, -weight_z[:, None] * sine_z], 1).astype(
        jnp.bfloat16
    )
    plain_z = jnp.stack([cosine_z, -sine_z], 1).astype(jnp.bfloat16)
    angle_y = phases(kept_modes(MY, NY), NY)
    cosine_y = jnp.cos(angle_y)
    sine_y = jnp.sin(angle_y)
    upper_rows = jnp.stack([cosine_y.T, -sine_y.T], -1)
    lower_rows = jnp.stack([sine_y.T, cosine_y.T], -1)
    forward_y = jnp.stack([upper_rows, lower_rows], 0).reshape(2 * NY, 2 * MY).astype(jnp.bfloat16)
    real_rows = jnp.stack([cosine_y, sine_y], 1)
    imag_rows = jnp.stack([-sine_y, cosine_y], 1)
    inverse_y = jnp.stack([real_rows, imag_rows], 1).reshape(2 * MY, 2 * NY).astype(jnp.bfloat16)
    angle_x = phases(kept_modes(MX, NX), NX)
    cosine_x = jnp.cos(angle_x).T.astype(jnp.bfloat16)
    sine_x = jnp.sin(angle_x).T.astype(jnp.bfloat16)
    return (forward_z, scaled_z, plain_z, forward_y, inverse_y, cosine_x, sine_x)


def to_modes(field_part, tables):
    forward_z, scaled_z, plain_z, forward_y, inverse_y, cosine_x, sine_x = tables
    channels = field_part.shape[0]
    planes = field_part.shape[1]
    grid_view = field_part.reshape(channels, planes, NY, NZ)
    section_one = jnp.einsum(
        "cxyz,zpk->cxkpy", grid_view, forward_z, preferred_element_type=jnp.float32
    ).astype(jnp.bfloat16)
    section_one = section_one.reshape(channels, planes, MZ, 2 * NY)
    section_two = jnp.einsum(
        "cxkm,mn->cxkn", section_one, forward_y, preferred_element_type=jnp.float32
    ).astype(jnp.bfloat16)
    section_two = section_two.reshape(channels, planes, 2 * MZ * MY)
    pencils = lax.all_to_all(section_two, "slab", split_axis=2, concat_axis=1, tiled=True)
    pencils = pencils.reshape(channels, NX, -1, 2)
    along_cos = jnp.einsum("cxmq,xk->cmqk", pencils, cosine_x, preferred_element_type=jnp.float32)
    along_sin = jnp.einsum("cxmq,xk->cmqk", pencils, sine_x, preferred_element_type=jnp.float32)
    real_part = along_cos[:, :, 0] + along_sin[:, :, 1]
    imag_part = along_cos[:, :, 1] - along_sin[:, :, 0]
    return jnp.stack([real_part, imag_part], 2)


def to_grid(spectra, tables, table_z):
    forward_z, scaled_z, plain_z, forward_y, inverse_y, cosine_x, sine_x = tables
    channels = spectra.shape[0]
    back_cos = jnp.einsum("cmqk,xk->cxmq", spectra, cosine_x, preferred_element_type=jnp.float32)
    back_sin = jnp.einsum("cmqk,xk->cxmq", spectra, sine_x, preferred_element_type=jnp.float32)
    real_part = back_cos[..., 0] - back_sin[..., 1]
    imag_part = back_cos[..., 1] + back_sin[..., 0]
    pencil_rows = jnp.stack([real_part, imag_part], -1).astype(jnp.bfloat16)
    pencil_rows = pencil_rows.reshape(channels, NX, -1)
    slabs = lax.all_to_all(pencil_rows, "slab", split_axis=1, concat_axis=2, tiled=True)
    channels = slabs.shape[0]
    planes = slabs.shape[1]
    slabs = slabs.reshape(channels, planes, MZ, 2 * MY)
    section_two = jnp.einsum(
        "cxkn,nm->cxkm", slabs, inverse_y, preferred_element_type=jnp.float32
    ).astype(jnp.bfloat16)
    section_two = section_two.reshape(channels, planes, MZ, 2, NY)
    grid_view = jnp.einsum(
        "cxkpy,kpz->cxyz", section_two, table_z, preferred_element_type=jnp.float32
    )
    return grid_view.reshape(channels, planes, NY * NZ)


def gelu_grad(pre_act):
    normal_cdf = 0.5 * (1.0 + jax.scipy.special.erf(pre_act / math.sqrt(2.0)))
    normal_pdf = jnp.exp(-0.5 * pre_act * pre_act) / math.sqrt(2.0 * math.pi)
    return normal_cdf + pre_act * normal_pdf


def body(field, cotangent, spectral_weight, point_weight, point_bias):
    tables = make_tables()
    scaled_z = tables[1]
    plain_z = tables[2]
    group_size = spectral_weight.shape[1]
    modes_dev = spectral_weight.shape[3]
    chan_start = lax.axis_index("chan") * group_size
    own_field = lax.dynamic_slice_in_dim(field, chan_start, group_size, 0)
    coeff = to_modes(own_field, tables).astype(jnp.bfloat16)
    coeff_real = coeff[:, :, 0]
    coeff_imag = coeff[:, :, 1]
    real_weight = spectral_weight[0]
    imag_weight = spectral_weight[1]
    spec_real = jnp.einsum(
        "imk,iomk->omk", coeff_real, real_weight, preferred_element_type=jnp.float32
    ) - jnp.einsum("imk,iomk->omk", coeff_imag, imag_weight, preferred_element_type=jnp.float32)
    spec_imag = jnp.einsum(
        "imk,iomk->omk", coeff_real, imag_weight, preferred_element_type=jnp.float32
    ) + jnp.einsum("imk,iomk->omk", coeff_imag, real_weight, preferred_element_type=jnp.float32)
    partial_spectra = jnp.stack([spec_real, spec_imag], 2)
    spectra = lax.psum(partial_spectra.astype(jnp.bfloat16), "chan")
    shaped = to_grid(spectra, tables, scaled_z)
    mixed = jnp.einsum("io,ixc->oxc", point_weight, field, preferred_element_type=jnp.float32)
    pre_act = shaped + mixed + point_bias.astype(jnp.float32)[:, None, None]
    grad_pre = (cotangent.astype(jnp.float32) * gelu_grad(pre_act)).astype(jnp.bfloat16)
    mode_index = lax.axis_index("slab") * modes_dev + jnp.arange(modes_dev, dtype=jnp.int32)
    mode_scale = (jnp.where(mode_index // MY == 0, 1.0, 2.0) / (NX * NY * NZ)).astype(jnp.float32)
    grad_hat = (to_modes(grad_pre, tables) * mode_scale[None, :, None, None]).astype(jnp.bfloat16)
    grad_real = grad_hat[:, :, 0]
    grad_imag = grad_hat[:, :, 1]
    outer_real = jnp.einsum(
        "imk,omk->iomk", coeff_real, grad_real, preferred_element_type=jnp.float32
    ) + jnp.einsum("imk,omk->iomk", coeff_imag, grad_imag, preferred_element_type=jnp.float32)
    outer_imag = jnp.einsum(
        "imk,omk->iomk", coeff_real, grad_imag, preferred_element_type=jnp.float32
    ) - jnp.einsum("imk,omk->iomk", coeff_imag, grad_real, preferred_element_type=jnp.float32)
    grad_spectral = jnp.stack([outer_real, outer_imag], 0)
    adj_real = jnp.einsum(
        "omk,iomk->imk", grad_real, real_weight, preferred_element_type=jnp.float32
    ) + jnp.einsum("omk,iomk->imk", grad_imag, imag_weight, preferred_element_type=jnp.float32)
    adj_imag = jnp.einsum(
        "omk,iomk->imk", grad_imag, real_weight, preferred_element_type=jnp.float32
    ) - jnp.einsum("omk,iomk->imk", grad_real, imag_weight, preferred_element_type=jnp.float32)
    adjoint = jnp.stack([adj_real, adj_imag], 2).astype(jnp.bfloat16)
    spectral_back = to_grid(adjoint, tables, plain_z)
    own_rows = lax.dynamic_slice_in_dim(point_weight, chan_start, group_size, 0)
    point_back = jnp.einsum("io,oxc->ixc", own_rows, grad_pre, preferred_element_type=jnp.float32)
    grad_input = (spectral_back + point_back).astype(jnp.bfloat16)
    inverse_root = 1.0 / math.sqrt(NX * NY * NZ)
    weight_part = (
        jnp.einsum("ixc,oxc->io", own_field, grad_pre, preferred_element_type=jnp.float32)
        * inverse_root
    )
    bias_part = jnp.sum(grad_pre, axis=(1, 2), dtype=jnp.float32) * inverse_root
    grad_pointwise, grad_bias = lax.psum((weight_part, bias_part), "slab")
    return (grad_input, grad_spectral, grad_pointwise, grad_bias)


def solution(mesh):
    placed = (
        P(None, "slab", None),
        P(None, "slab", None),
        P(None, "chan", None, "slab", None),
        P(),
        P(),
    )
    return jax.shard_map(
        body,
        mesh=mesh,
        in_specs=placed,
        out_specs=(
            P("chan", "slab", None),
            P(None, "chan", None, "slab", None),
            P("chan", None),
            P(),
        ),
        check_vma=False,
    )
```

profile of v0, /device:TPU:1, one launch (start us, length us, event | category | flops | bytes accessed | tf_op | source)
XLA Modules:
  0.0 397.6 jit_solution(5632324393416578759)
XLA Ops:
  1.1 1.8 copy.125
  3.2 0.3 reshape.577
  3.6 0.6 fusion.17
  4.8 0.5 copy.181
  5.2 1.0 reshape.605
  6.2 18.4 %all-to-all-start = ((bf16[128,2,128]{2,1,0:T(2,128)(2,1)}), bf16[128,2,128]{2,1,0:T(2,128)(2,1)S(1)}, u32[]{:S(2)}, u32[]{:S(2)}) async-start(bf16[128,2,128]{2,1,0:T(2,128)(2,1)} %reshape.605), calls=%async_computation | async-start | bytes 131072 | tf_op jit(solution)/shard_map/all_to_all | solution.py:65
  25.2 10.9 %all-to-all-done = bf16[128,2,128]{2,1,0:T(2,128)(2,1)S(1)} async-done(((bf16[128,2,128]{2,1,0:T(2,128)(2,1)}), bf16[128,2,128]{2,1,0:T(2,128)(2,1)S(1)}, u32[]{:S(2)}, u32[]{:S(2)}) %all-to-all-start) | async-done | bytes 65568 | tf_op jit(solution)/shard_map/all_to_all | solution.py:65
  36.0 0.4 reshape.606
  36.6 0.4 copy.132
  37.9 0.4 fusion.34
  38.4 0.4 fusion.24
  38.8 0.4 fusion.26
  39.2 0.4 fusion.32
  39.8 13.8 %psum.21 = bf16[64,4,2,32]{0,3,2,1:T(8,128)(2,1)S(1)} all-reduce(bf16[64,4,2,32]{0,3,2,1:T(8,128)(2,1)S(1)} %pad_maximum_fusion.2), channel_id=1, replica_groups=mesh['slab'=128,'chan'=4] {'chan'}, use_global_device_ids=true, to_apply=%region_0.1 | all-reduce | flops 16384 | bytes 65536 | tf_op jit(solution)/shard_map/psum | solution.py:123
  53.5 0.4 convolution_bitcast_fusion.3
  53.9 0.4 convolution_bitcast_fusion.2
  54.8 1.0 reshape.607
  55.8 9.5 %all-to-all-start.1 = ((bf16[128,2,512]{2,1,0:T(2,128)(2,1)}), bf16[128,2,512]{2,1,0:T(2,128)(2,1)S(1)}, u32[]{:S(2)}, u32[]{:S(2)}) async-start(bf16[128,2,512]{2,1,0:T(2,128)(2,1)} %reshape.607), calls=%async_computation.1 | async-start | bytes 524288 | tf_op jit(solution)/shard_map/all_to_all | solution.py:83
  65.5 15.2 %all-to-all-done.1 = bf16[128,2,512]{2,1,0:T(2,128)(2,1)S(1)} async-done(((bf16[128,2,512]{2,1,0:T(2,128)(2,1)}), bf16[128,2,512]{2,1,0:T(2,128)(2,1)S(1)}, u32[]{:S(2)}, u32[]{:S(2)}) %all-to-all-start.1) | async-done | bytes 262176 | tf_op jit(solution)/shard_map/all_to_all | solution.py:83
  81.0 0.8 copy.137
  82.1 0.4 reshape.567
  82.5 2.7 convolution_bitcast_fusion
  85.2 4.2 %reshape.568 = f32[64,2,4096]{2,1,0:T(2,128)S(1)} reshape(f32[64,2,64,64]{3,2,1,0:T(8,128)} %convolution_bitcast_fusion) | data formatting | bytes 4194304 | tf_op jit(solution)/shard_map/reshape | solution.py:94
  89.4 5.7 %convert_reduce_fusion = (f32[64]{0:T(128)S(1)}, bf16[64,2,4096]{2,0,1:T(8,128)(2,1)S(1)}) fusion(f32[64]{0:T(128)S(1)} %convert_element_type.232, bf16[64,2,4096]{2,1,0:T(2,128)(2,1)} %param.5, bf16[64,64]{1,0:T(8,128)(2,1)S(1)} %copy-done, f32[64,2,4096]{2,1,0:T(2,128)S(1)} %reshape.568, bf16[64,2,4096]{2,1,0:T(2,128)(2,1)} %param.6), kind=kOutput, calls=%fused_computation.16 | convolution fusion | flops 74973120 | bytes 5251584 | tf_op jit(solution)/shard_map/io,ixc->oxc/dot_general | solution.py:125
  95.1 2.3 reshape.569
  97.4 2.0 fusion.14
  99.4 1.6 copy.143
  101.1 0.5 reshape.570
  101.9 0.7 copy.183
  102.6 1.0 reshape.609
  103.6 5.8 %all-to-all-start.2 = ((bf16[128,2,512]{2,1,0:T(2,128)(2,1)}), bf16[128,2,512]{2,1,0:T(2,128)(2,1)S(1)}, u32[]{:S(2)}, u32[]{:S(2)}) async-start(bf16[128,2,512]{2,1,0:T(2,128)(2,1)} %reshape.609), calls=%async_computation.2 | async-start | bytes 524288 | tf_op jit(solution)/shard_map/all_to_all | solution.py:65
  109.4 0.4 fusion.18
  109.8 256.7 %all-reduce = (f32[16,64]{1,0:T(8,128)}, f32[64]{0:T(128)}) all-reduce(f32[16,64]{1,0:T(8,128)S(1)} %fusion.18, f32[64]{0:T(128)S(1)} %broadcast_multiply_fusion), channel_id=1, replica_groups=mesh['slab'=128,'chan'=4] {'slab'}, use_global_device_ids=true, to_apply=%region_1.2 | all-reduce | flops 1088 | bytes 8704 | tf_op jit(solution)/shard_map/psum | solution.py:157
  367.0 0.5 copy.147
  368.4 0.4 fusion.22
  368.8 0.4 fusion.28
  369.2 0.4 fusion.30
  369.7 0.4 fusion.20
  371.5 1.0 reshape.611
  372.5 10.4 %all-to-all-start.3 = ((bf16[128,2,128]{2,1,0:T(2,128)(2,1)}), bf16[128,2,128]{2,1,0:T(2,128)(2,1)S(1)}, u32[]{:S(2)}, u32[]{:S(2)}) async-start(bf16[128,2,128]{2,1,0:T(2,128)(2,1)} %reshape.611), calls=%async_computation.3 | async-start | bytes 131072 | tf_op jit(solution)/shard_map/all_to_all | solution.py:83
  382.9 0.6 add_bitcast_fusion
  383.5 1.6 pad_maximum_fusion
  385.1 9.2 %all-to-all-done.3 = bf16[128,2,128]{2,1,0:T(2,128)(2,1)S(1)} async-done(((bf16[128,2,128]{2,1,0:T(2,128)(2,1)}), bf16[128,2,128]{2,1,0:T(2,128)(2,1)S(1)}, u32[]{:S(2)}, u32[]{:S(2)}) %all-to-all-start.3) | async-done | bytes 65568 | tf_op jit(solution)/shard_map/all_to_all | solution.py:83
  394.3 0.4 reshape.612
  395.3 0.3 convolution_bitcast_fusion.1
  395.7 0.5 reshape.575
  396.2 0.4 fusion.1
  396.6 1.0 copy.156
  (83 shorter events, 7.7 us)
Async XLA Ops:
  0.6 88.8 %copy-start = (bf16[64,64]{1,0:T(8,128)(2,1)S(1)}, bf16[64,64]{1,0:T(8,128)(2,1)}, u32[]{:S(2)}) copy-start(bf16[64,64]{1,0:T(8,128)(2,1)} %param.8) | copy-start | bytes 24580
  3.2 21.6 %copy-start.1 = (bf16[2,16,64,4,32]{2,4,3,1,0:T(8,128)(2,1)S(1)}, bf16[2,16,64,4,32]{2,4,3,1,0:T(8,128)(2,1)}, u32[]{:S(2)}) copy-start(bf16[2,16,64,4,32]{2,4,3,1,0:T(8,128)(2,1)} %param.7) | copy-start | bytes 1572868
  4.6 20.5 %copy-start.6 = (bf16[64]{0:T(256)(128)(2,1)S(1)}, bf16[64]{0:T(256)(128)(2,1)}, u32[]{:S(2)}) copy-start(bf16[64]{0:T(256)(128)(2,1)} %param.9) | copy-start | bytes 388
  6.2 29.8 %all-to-all-start = ((bf16[128,2,128]{2,1,0:T(2,128)(2,1)}), bf16[128,2,128]{2,1,0:T(2,128)(2,1)S(1)}, u32[]{:S(2)}, u32[]{:S(2)}) async-start(bf16[128,2,128]{2,1,0:T(2,128)(2,1)} %reshape.605), calls=%async_computation | async-start | bytes 131072 | tf_op jit(solution)/shard_map/all_to_all | solution.py:65
  24.9 13.9 %copy-start.2 = (bf16[16,64,4,32]{1,3,2,0:T(8,128)(2,1)}, bf16[16,64,4,32]{1,3,2,0:T(8,128)(2,1)S(1)}, u32[]{:S(2)}) copy-start(bf16[16,64,4,32]{1,3,2,0:T(8,128)(2,1)S(1)} %get-tuple-element.33) | copy-start | bytes 786436
  24.9 14.3 %copy-start.4 = (bf16[16,64,4,32]{1,3,2,0:T(8,128)(2,1)}, bf16[16,64,4,32]{1,3,2,0:T(8,128)(2,1)S(1)}, u32[]{:S(2)}) copy-start(bf16[16,64,4,32]{1,3,2,0:T(8,128)(2,1)S(1)} %get-tuple-element.32) | copy-start | bytes 786436
  55.8 24.8 %all-to-all-start.1 = ((bf16[128,2,512]{2,1,0:T(2,128)(2,1)}), bf16[128,2,512]{2,1,0:T(2,128)(2,1)S(1)}, u32[]{:S(2)}, u32[]{:S(2)}) async-start(bf16[128,2,512]{2,1,0:T(2,128)(2,1)} %reshape.607), calls=%async_computation.1 | async-start | bytes 524288 | tf_op jit(solution)/shard_map/all_to_all | solution.py:83
  103.6 262.9 %all-to-all-start.2 = ((bf16[128,2,512]{2,1,0:T(2,128)(2,1)}), bf16[128,2,512]{2,1,0:T(2,128)(2,1)S(1)}, u32[]{:S(2)}, u32[]{:S(2)}) async-start(bf16[128,2,512]{2,1,0:T(2,128)(2,1)} %reshape.609), calls=%async_computation.2 | async-start | bytes 524288 | tf_op jit(solution)/shard_map/all_to_all | solution.py:65
  366.8 1.5 copy-start.3
  366.9 1.9 copy-start.5
  372.5 21.8 %all-to-all-start.3 = ((bf16[128,2,128]{2,1,0:T(2,128)(2,1)}), bf16[128,2,128]{2,1,0:T(2,128)(2,1)S(1)}, u32[]{:S(2)}, u32[]{:S(2)}) async-start(bf16[128,2,128]{2,1,0:T(2,128)(2,1)} %reshape.611), calls=%async_computation.3 | async-start | bytes 131072 | tf_op jit(solution)/shard_map/all_to_all | solution.py:83
where the time goes:
time: 398 us
  blocking collectives  270 us (68%)
  starting transfers between devices  44.1 us (11%)
  waiting for transfers between devices  35.3 us (9%)
  local copies, waits for them, and re-layouts  24 us (6%)
  matrix products  19.2 us (5%)
    psum x1, blocking collectives, body(): grad_pointwise, grad_bias = lax.psum((weight_part, bias_part), 'slab')  257 us
    all_to_all x2, waiting for transfers between devices, to_grid(): lax.all_to_all(pencil_rows, 'slab', split_axis=1, concat_axis=2, tiled=True)  24.4 us
    all_to_all x2, starting transfers between devices, to_modes(): lax.all_to_all(section_two, 'slab', split_axis=2, concat_axis=1, tiled=True)  24.2 us
    all_to_all x2, starting transfers between devices, to_grid(): lax.all_to_all(pencil_rows, 'slab', split_axis=1, concat_axis=2, tiled=True)  19.9 us
    psum x1, blocking collectives, body(): spectra = lax.psum(partial_spectra.astype(jnp.bfloat16), 'chan')  13.8 us
    all_to_all x2, waiting for transfers between devices, to_modes(): lax.all_to_all(section_two, 'slab', split_axis=2, concat_axis=1, tiled=True)  10.9 us
    unnamed x24, local copies, waits for them, and re-layouts  8.16 us
  transfers between devices with their start and end apart: 4, of which 3 were waited for; matrix products, arithmetic and copies ran while one was open for 1% of the time, Pallas kernels for 0%

commit v1 on v0

v1 whole, which is shorter than its diff:
```python
import math

import jax
import jax.numpy as jnp
import numpy as np
from jax import lax
from jax.experimental import pallas as pl
from jax.experimental.pallas import tpu as pltpu
from jax.sharding import PartitionSpec as P

MX = 32
MY = 32
MZ = 16
NX = 256
NY = 64
NZ = 64
C = 64
OWN = 16
SLAB = 128
PLANES = 2
LOW = 4
HIGH = 8
CELLS = NY * NZ
LANES = 128
HALF = 64
CHUNK = 10
BACK = 4
SHARE = 7
INVERSE_ROOT = 1.0 / math.sqrt(NX * NY * NZ)
F32 = jnp.float32
BF16 = jnp.bfloat16


def kept(total, length):
    index = np.arange(total)
    return np.where(index < total // 2, index, index - total + length)


def waves(frequency, length):
    wound = (frequency[:, None] * np.arange(length)[None, :]) % length
    angle = np.float32(2.0 * math.pi / length) * wound.astype(np.float32)
    return np.cos(angle), np.sin(angle)


def table(values):
    return jnp.asarray(np.asarray(values, np.float32)).astype(BF16)


def axis_tables():
    cos_z, sin_z = waves(np.arange(MZ), NZ)
    cos_y, sin_y = waves(kept(MY, NY), NY)
    cos_x, sin_x = waves(kept(MX, NX), NX)
    return cos_z, sin_z, cos_y, sin_y, cos_x, sin_x


def rows_of_ky(real, imag):
    both = np.stack([real, imag], 1).reshape(HIGH, LOW, 2, -1)
    return np.transpose(both, (0, 2, 1, 3))


def middle_tables():
    cos_z, sin_z, cos_y, sin_y, _, _ = axis_tables()
    weight = (np.where(np.arange(MZ) == 0, 1.0, 2.0) / (NX * NY * NZ))[:, None]
    to_z = np.stack([weight * cos_z, -weight * sin_z], 1).reshape(2 * MZ, NZ).T
    from_z = np.concatenate([cos_z, -sin_z], 0)
    real = np.stack([cos_y, sin_y], 1).reshape(MY, 2 * NY)
    imag = np.stack([-sin_y, cos_y], 1).reshape(MY, 2 * NY)
    to_y = rows_of_ky(real, imag).reshape(2 * MY, 2 * NY).T
    real = np.stack([cos_y, sin_y], 2).reshape(MY, 2 * NY)
    imag = np.stack([-sin_y, cos_y], 2).reshape(MY, 2 * NY)
    from_y = rows_of_ky(real, imag).reshape(HIGH, 8, 2 * NY)
    from_y = np.concatenate([from_y, np.zeros((HIGH, CHUNK - 8, 2 * NY))], 1)
    from_y = from_y.reshape(HIGH * CHUNK, 2 * NY)
    pick = np.zeros((SLAB, CHUNK, 32))
    owner = np.arange(SLAB)
    pick[owner, 8, np.minimum(owner // SHARE, OWN)] = 1.0
    return to_y, to_z, from_z, from_y, pick.reshape(SLAB * CHUNK, 32)


def pencil_tables():
    _, _, _, _, cos_x, sin_x = axis_tables()
    along = np.concatenate([cos_x, sin_x], 0)
    split = along.reshape(2 * MX, SLAB, PLANES)
    spread = np.transpose(split, (2, 0, 1)).reshape(2 * PLANES * MX, SLAB)
    back = np.transpose(split, (2, 1, 0)).reshape(NX, 2 * MX)
    return along, spread, spread.T, back


def mm(left, right):
    return jnp.dot(left, right, preferred_element_type=F32)


def swap(values):
    return pltpu.roll(values, HALF, 1)


def lane_of(shape):
    return lax.broadcasted_iota(jnp.int32, shape, 1)


def gelu_grad(pre_act):
    normal_cdf = 0.5 * (1.0 + lax.erf(pre_act * (1.0 / math.sqrt(2.0))))
    normal_pdf = jnp.exp(-0.5 * pre_act * pre_act) * (1.0 / math.sqrt(2.0 * math.pi))
    return normal_cdf + pre_act * normal_pdf


def two_words(values):
    head = values.astype(BF16).astype(F32)
    rest = values - head
    return jnp.where(lane_of(values.shape) < HALF, head, swap(rest))


def middle_kernel(
    modes, base, cot, own, to_y, to_z, from_z, from_y, pick, grad, out, up, flat, down
):
    @pl.loop(0, MZ, unroll=4)
    def _(kz):
        start = pl.multiple_of(kz * 64, 64)
        up[pl.ds(pl.multiple_of(kz * 128, 128), 128), :] = mm(
            to_y[...], modes[pl.ds(start, 64), :]
        )

    @pl.loop(0, NY // 2, unroll=4)
    def _(pair):
        left = up[pl.ds(pair * 2, 2 * MZ, stride=NY), :]
        right = up[pl.ds(pair * 2 + 1, 2 * MZ, stride=NY), :]
        both = jnp.concatenate([left, right], 1).astype(BF16)
        grid = mm(to_z[...], both)
        start = pl.multiple_of(pair * 128, 128)
        flat[pl.ds(start, 64), :] = grid[:, :LANES] + base[pl.ds(start, 64), :]
        start = pl.multiple_of(pair * 128 + 64, 64)
        flat[pl.ds(start, 64), :] = grid[:, LANES:] + base[pl.ds(start, 64), :]

    @pl.loop(0, CELLS // 64, unroll=2)
    def _(block):
        rows = pl.ds(pl.multiple_of(block * 64, 64), 64)
        grad[rows, :] = (cot[rows, :].astype(F32) * gelu_grad(flat[rows, :])).astype(BF16)

    @pl.loop(0, NY // 2, unroll=4)
    def _(pair):
        start = pl.multiple_of(pair * 128, 128)
        left = grad[pl.ds(start, 64), :]
        right = grad[pl.ds(pl.multiple_of(start + 64, 64), 64), :]
        lines = mm(from_z[...], jnp.concatenate([left, right], 1))
        start = pl.multiple_of(pair * 64, 64)
        down[pl.ds(start, 32), :] = lines[:, :LANES]
        down[pl.ds(pl.multiple_of(start + 32, 32), 32), :] = lines[:, LANES:]

    sums = mm(own[...], grad[...])
    lower = sums[:OWN] + swap(sums[OWN : 2 * OWN])
    bias = sums[2 * OWN : 2 * OWN + 8] + swap(sums[2 * OWN : 2 * OWN + 8])
    words = two_words(jnp.concatenate([lower, bias, jnp.zeros_like(bias)], 0)).astype(BF16)

    @pl.loop(0, MZ, unroll=4)
    def _(kz):
        lines = down[pl.ds(kz, 2 * NY, stride=MZ), :].astype(BF16)
        rows = pl.ds(pl.multiple_of(kz * HIGH * CHUNK, HIGH * CHUNK), HIGH * CHUNK)
        out[rows, :] = (mm(from_y[...], lines) + mm(pick[rows, :], words)).astype(BF16)


def in_vmem(count):
    return [pl.BlockSpec(memory_space=pltpu.VMEM)] * count


def call(kernel, shapes, scratch, flops, *operands):
    moved = sum(s.size * s.dtype.itemsize for s in list(operands) + list(shapes))
    return pl.pallas_call(
        kernel,
        out_shape=shapes,
        in_specs=in_vmem(len(operands)),
        out_specs=in_vmem(len(shapes)),
        scratch_shapes=scratch,
        cost_estimate=pl.CostEstimate(flops=flops, bytes_accessed=moved, transcendentals=0),
        compiler_params=pltpu.CompilerParams(vmem_limit_bytes=40 * 2**20),
    )(*operands)


def middle(modes, base, cot, own):
    tables = [table(t) for t in middle_tables()]
    shapes = (
        jax.ShapeDtypeStruct((CELLS, LANES), BF16),
        jax.ShapeDtypeStruct((SLAB * CHUNK, LANES), BF16),
    )
    scratch = [
        pltpu.VMEM((2 * NY * MZ, LANES), F32),
        pltpu.VMEM((CELLS, LANES), F32),
        pltpu.VMEM((2 * NY * MZ, LANES), F32),
    ]
    return call(middle_kernel, shapes, scratch, 400_000_000, modes, base, cot, own, *tables)


def mix_kernel(pencils, weight, along, coeff, out):
    both = mm(along[...], pencils[...])
    lane = lane_of((MX, LANES))
    turned = swap(both[MX:])
    modes = both[:MX] + jnp.where(lane < HALF, turned, -turned)
    modes = modes.astype(BF16).astype(F32)
    coeff[...] = modes
    for m in range(LOW):
        rows = pl.ds(m * MX, MX)
        real = jnp.zeros((MX, C), F32)
        imag = jnp.zeros((MX, C), F32)
        for i in range(OWN):
            at = m * OWN + i
            left = jnp.broadcast_to(modes[:, at : at + 1], (MX, C))
            right = jnp.broadcast_to(modes[:, HALF + at : HALF + at + 1], (MX, C))
            weight_real = weight[0, i, rows, :].astype(F32)
            weight_imag = weight[1, i, rows, :].astype(F32)
            real += left * weight_real - right * weight_imag
            imag += left * weight_imag + right * weight_real
        part = jnp.concatenate([real, imag], 1).astype(BF16)
        for peer in range(4):
            out[peer, rows, :] = part


def mix(pencils, weight):
    along = table(pencil_tables()[0])
    shapes = (
        jax.ShapeDtypeStruct((MX, LANES), F32),
        jax.ShapeDtypeStruct((4, LOW * MX, LANES), BF16),
    )
    return call(mix_kernel, shapes, [], 4_000_000, pencils, weight, along)


def spread_kernel(parts, spread, out, rows):
    total = parts[0].astype(F32)
    for peer in range(1, 4):
        total += parts[peer].astype(F32)
    lane = lane_of((MX, LANES))
    for m in range(LOW):
        here = total[m * MX : (m + 1) * MX]
        there = swap(here)
        zero = jnp.zeros_like(here)
        a = jnp.where(lane < HALF, here, zero)
        b = jnp.where(lane < HALF, there, zero)
        c = jnp.where(lane < HALF, zero, there)
        d = jnp.where(lane < HALF, zero, here)
        top = jnp.concatenate([a, b], 1)
        second = jnp.concatenate([-b, a], 1)
        third = jnp.concatenate([c, d], 1)
        last = jnp.concatenate([-d, c], 1)
        block = jnp.concatenate([top, second, third, last], 0).astype(BF16)
        planes = mm(spread[...], block)
        rows[pl.ds(m, SLAB, stride=8), :] = planes[:, :LANES]
        rows[pl.ds(LOW + m, SLAB, stride=8), :] = planes[:, LANES:]
    out[...] = rows[...].astype(BF16)


def spread_planes(parts):
    shapes = (jax.ShapeDtypeStruct((SLAB * 8, LANES), BF16),)
    scratch = [pltpu.VMEM((SLAB * 8, LANES), F32)]
    spread = table(pencil_tables()[2])
    return call(spread_kernel, shapes, scratch, 40_000_000, parts, spread)[0]


def adjoint_kernel(pencils, weight, gather, back, scale, hat, out, wide, rows):
    wide[...] = pencils[...].astype(F32)
    lane = lane_of((MX, LANES))
    adjoint = jnp.zeros((MX, LANES), F32)
    factor = scale[0:1, :]
    for m in range(LOW):
        left = wide[pl.ds(m, SLAB, stride=CHUNK), :]
        right = wide[pl.ds(LOW + m, SLAB, stride=CHUNK), :]
        both = mm(gather[...], jnp.concatenate([left, right], 1).astype(BF16))
        first = both[: 2 * MX, :LANES] + swap(both[2 * MX :, :LANES])
        second = both[: 2 * MX, LANES:] + swap(both[2 * MX :, LANES:])
        real = (first[:MX] + second[MX:]) * factor
        imag = (second[:MX] - first[MX:]) * factor
        real = real.astype(BF16).astype(F32)[:, :C]
        imag = imag.astype(BF16).astype(F32)[:, :C]
        at_m = pl.ds(m * MX, MX)
        hat[0, at_m, :] = real
        hat[1, at_m, :] = imag
        for i in range(OWN):
            weight_real = weight[0, i, at_m, :].astype(F32)
            weight_imag = weight[1, i, at_m, :].astype(F32)
            sum_real = jnp.sum(real * weight_real + imag * weight_imag, 1, keepdims=True)
            sum_imag = jnp.sum(imag * weight_real - real * weight_imag, 1, keepdims=True)
            adjoint = jnp.where(lane == m * OWN + i, sum_real, adjoint)
            adjoint = jnp.where(lane == HALF + m * OWN + i, sum_imag, adjoint)
    turned = swap(adjoint)
    lower = jnp.where(lane < HALF, -turned, turned)
    planes = mm(back[...], jnp.concatenate([adjoint, lower], 0).astype(BF16))
    for plane in range(PLANES):
        rows[pl.ds(plane, SLAB, stride=BACK), :] = planes[plane * SLAB : (plane + 1) * SLAB]
    rider = wide[pl.ds(8, SLAB, stride=CHUNK), :]
    total = jnp.sum(rider, 0, keepdims=True)
    total = jnp.broadcast_to(total, (8, LANES))
    total = two_words((total + swap(total)) * INVERSE_ROOT)
    rows[pl.ds(2, SLAB, stride=BACK), :] = jnp.broadcast_to(total[:1], (SLAB, LANES))
    rows[pl.ds(3, SLAB, stride=BACK), :] = jnp.zeros((SLAB, LANES), F32)
    out[...] = rows[...].astype(BF16)


def adjoint_planes(pencils, weight, scale):
    _, gather, _, back = pencil_tables()
    shapes = (
        jax.ShapeDtypeStruct((2, LOW * MX, C), F32),
        jax.ShapeDtypeStruct((SLAB * BACK, LANES), BF16),
    )
    scratch = [
        pltpu.VMEM((SLAB * CHUNK, LANES), F32),
        pltpu.VMEM((SLAB * BACK, LANES), F32),
    ]
    return call(
        adjoint_kernel, shapes, scratch, 40_000_000,
        pencils, weight, table(gather), table(back), scale,
    )


def outer_kernel(coeff, hat, out):
    modes = coeff[...]
    for m in range(LOW):
        rows = pl.ds(m * MX, MX)
        real = hat[0, rows, :]
        imag = hat[1, rows, :]
        for i in range(OWN):
            at = m * OWN + i
            left = jnp.broadcast_to(modes[:, at : at + 1], (MX, C))
            right = jnp.broadcast_to(modes[:, HALF + at : HALF + at + 1], (MX, C))
            out[0, i, rows, :] = left * real + right * imag
            out[1, i, rows, :] = left * imag - right * real


def outer(coeff, hat):
    shapes = (jax.ShapeDtypeStruct((2, OWN, LOW * MX, C), F32),)
    return call(outer_kernel, shapes, [], 8_000_000, coeff, hat)[0]


def own_modes(own_field):
    cos_z, sin_z, cos_y, sin_y, _, _ = axis_tables()
    forward_z = table(np.stack([cos_z.T, -sin_z.T], 1))
    upper = np.stack([cos_y.T, -sin_y.T], -1)
    lower = np.stack([sin_y.T, cos_y.T], -1)
    forward_y = table(np.stack([upper, lower], 0).reshape(2 * NY, 2 * MY))
    grid_view = own_field.reshape(OWN, PLANES, NY, NZ)
    lines = jnp.einsum("cxyz,zpk->cxkpy", grid_view, forward_z, preferred_element_type=F32)
    lines = lines.astype(BF16).reshape(OWN, PLANES, MZ, 2 * NY)
    modes = jnp.einsum("cxkm,mn->cxkn", lines, forward_y, preferred_element_type=F32)
    modes = modes.astype(BF16).reshape(OWN, PLANES, SLAB, LOW, 2)
    return jnp.transpose(modes, (2, 1, 4, 3, 0)).reshape(SLAB, PLANES, LANES)


def own_grid(planes):
    cos_z, sin_z, cos_y, sin_y, _, _ = axis_tables()
    plain_z = table(np.stack([cos_z, -sin_z], 1))
    real = np.stack([cos_y, sin_y], 1)
    imag = np.stack([-sin_y, cos_y], 1)
    inverse_y = table(np.stack([real, imag], 1).reshape(2 * MY, 2 * NY))
    modes = planes.reshape(SLAB, PLANES, 2, LOW, OWN)
    modes = jnp.transpose(modes, (4, 1, 0, 3, 2)).reshape(OWN, PLANES, MZ, 2 * MY)
    lines = jnp.einsum("cxkn,nm->cxkm", modes, inverse_y, preferred_element_type=F32)
    lines = lines.astype(BF16).reshape(OWN, PLANES, MZ, 2, NY)
    grid = jnp.einsum("cxkpy,kpz->cxyz", lines, plain_z, preferred_element_type=F32)
    return grid.reshape(OWN, PLANES, CELLS)


def over(values, axis):
    return lax.all_to_all(values, axis, split_axis=0, concat_axis=0, tiled=True)


def paired(matrix):
    zero = jnp.zeros_like(matrix)
    upper = jnp.concatenate([matrix, zero], 1)
    lower = jnp.concatenate([zero, matrix], 1)
    return jnp.concatenate([upper, lower], 0)


def body(field, cotangent, spectral_weight, point_weight, point_bias):
    chan_start = lax.axis_index("chan") * OWN
    own_field = lax.dynamic_slice_in_dim(field, chan_start, OWN, 0)
    own_rows = lax.dynamic_slice_in_dim(point_weight, chan_start, OWN, 0)
    weight = jnp.transpose(spectral_weight, (0, 1, 3, 4, 2)).reshape(2, OWN, LOW * MX, C)
    first = own_modes(own_field)
    field, cotangent, own_field, first = lax.optimization_barrier(
        (field, cotangent, own_field, first)
    )
    pencils = over(first, "slab").reshape(NX, LANES)

    cells = jnp.transpose(field, (2, 1, 0)).reshape(CELLS, LANES)
    cot = jnp.transpose(cotangent, (2, 1, 0)).reshape(CELLS, LANES)
    bias = jnp.tile(point_bias.astype(F32), 2)[None]
    base = mm(cells, paired(point_weight)) + bias
    own = jnp.transpose(own_field, (1, 0, 2)).reshape(2 * OWN, CELLS)
    own = jnp.concatenate([own, jnp.ones((8, CELLS), BF16)], 0)

    coeff, parts = mix(pencils, weight)
    parts = over(parts, "chan")
    planes = spread_planes(parts)
    modes = over(planes.reshape(SLAB, 8, LANES), "slab").reshape(SLAB * 8, LANES)
    grad, rows = middle(modes, base, cot, own)
    arrived = over(rows.reshape(SLAB * CHUNK // 2, 2, LANES), "slab").reshape(SLAB * CHUNK, LANES)
    point_back = mm(paired(own_rows), grad.T)
    kz_weight = jnp.where(lax.axis_index("slab") < HIGH, 1.0, 2.0) / (NX * NY * NZ)
    scale = jnp.full((8, LANES), kz_weight, F32)
    hat, rows = adjoint_planes(arrived, weight, scale)
    final = over(rows.reshape(SLAB, BACK, LANES), "slab")
    outer_part = outer(coeff, hat).reshape(2, OWN, LOW, MX, C)
    grad_spectral = jnp.transpose(outer_part, (0, 1, 4, 2, 3))
    point_back = jnp.transpose(point_back.reshape(PLANES, OWN, CELLS), (1, 0, 2))
    grad_input = (own_grid(final[:, :PLANES]) + point_back).astype(BF16)
    words = final[: SHARE * (OWN + 1) : SHARE, 2].astype(F32)
    totals = words[:, :HALF] + words[:, HALF:]
    return grad_input, grad_spectral, totals[:OWN], totals[OWN]


def solution(mesh):
    placed = (
        P(None, "slab", None),
        P(None, "slab", None),
        P(None, "chan", None, "slab", None),
        P(),
        P(),
    )
    return jax.shard_map(
        body,
        mesh=mesh,
        in_specs=placed,
        out_specs=(
            P("chan", "slab", None),
            P(None, "chan", None, "slab", None),
            P("chan", None),
            P(),
        ),
        check_vma=False,
    )
```

time: 398 us -> 131 us (0.33)
  blocking collectives: 270 us -> 38.5 us
  starting transfers between devices: 44.1 us -> 19.3 us
  matrix products: 19.2 us -> 4.12 us
  Pallas kernels: 0 us -> 13.3 us
  local copies, waits for them, and re-layouts: 24 us -> 16.6 us
    psum x2 -> x0, blocking collectives: 270 us -> none  [the longest x1 257 us: body(): grad_pointwise, grad_bias = lax.psum((weight_part, bias_part), 'slab')]
    all_to_all x0 -> x2, blocking collectives: none -> 38.5 us  [over(): return lax.all_to_all(values, axis, split_axis=0, concat_axis=0, tiled=True)]
    all_to_all x4 -> x3, starting transfers between devices: 44.1 us -> 19.3 us  [over(): return lax.all_to_all(values, axis, split_axis=0, concat_axis=0, tiled=True)]
    dot_general x27 -> x6, matrix products: 19.2 us -> 4.12 us  [the longest x2 2.17 us: mm(): return jnp.dot(left, right, preferred_element_type=F32)]
    pallas_call x0 -> x5, Pallas kernels: none -> 13.3 us  [call(): pl.pallas_call(kernel, out_shape=shapes, in_specs=in_vmem(len(operands)),...]
    reshape x14 -> x6, local copies, waits for them, and re-layouts: 11.7 us -> 2.08 us  [the longest x1 0.66 us: body(): cot = jnp.transpose(cotangent, (2, 1, 0)).reshape(CELLS, LANES)]
    all_to_all x4 -> x3, waiting for transfers between devices: 35.3 us -> 36.3 us  [over(): return lax.all_to_all(values, axis, split_axis=0, concat_axis=0, tiled=True)]
    unnamed x24 -> x44, local copies, waits for them, and re-layouts: 8.16 us -> 7.74 us
  transfers between devices with their start and end apart: 4 -> 3, of which waited for: 3 -> 3; matrix products, arithmetic and copies ran while one was open for 1% -> 5% of each run, Pallas kernels for 0% -> 2%
where the time goes in v1:
time: 131 us; the launch traced here: 130 us
  blocking collectives  38.5 us (29%)
  waiting for transfers between devices  36.3 us (28%)
  starting transfers between devices  19.3 us (15%)
  local copies, waits for them, and re-layouts  16.6 us (13%)
  Pallas kernels  13.3 us (10%)
  matrix products  4.12 us (3%)
  other arithmetic  1.32 us (1%)
    all_to_all x2, blocking collectives, over(): return lax.all_to_all(values, axis, split_axis=0, concat_axis=0, tiled=True)  38.5 us
    all_to_all x3, waiting for transfers between devices, over(): return lax.all_to_all(values, axis, split_axis=0, concat_axis=0, tiled=True)  36.3 us
    all_to_all x3, starting transfers between devices, over(): return lax.all_to_all(values, axis, split_axis=0, concat_axis=0, tiled=True)  19.3 us
    pallas_call x5, Pallas kernels, call(): pl.pallas_call(kernel, out_shape=shapes, in_specs=in_vmem(len(operands)),...  13.3 us
    unnamed x44, local copies, waits for them, and re-layouts  7.74 us
  transfers between devices with their start and end apart: 3, of which 3 were waited for; matrix products, arithmetic and copies ran while one was open for 5% of the time, Pallas kernels for 2%

profile of v1, /device:TPU:1, one launch (start us, length us, event | category | flops | bytes accessed | tf_op | source)
XLA Modules:
  0.0 130.4 jit_solution(4379150208876099416)
XLA Ops:
  0.6 1.1 constant_dynamic-slice_fusion.1
  1.8 0.3 reshape.93
  2.2 1.3 fusion
  3.5 0.2 copy.57
  3.7 0.1 reshape.73
  3.9 0.2 convolution_convert_fusion.2
  4.1 0.3 copy.58
  4.4 0.4 copy.59
  4.8 0.1 copy.60
  4.9 29.7 %all_to_all.25 = bf16[128,2,128]{2,1,0:T(2,128)(2,1)S(1)} all-to-all(bf16[128,2,128]{2,1,0:T(2,128)(2,1)S(1)} %copy.60), channel_id=1, replica_groups=mesh['slab'=128,'chan'=4] {'slab'}, dimensions={0} | all-to-all | bytes 131072 | tf_op jit(solution)/shard_map/all_to_all | solution.py:359
  34.6 1.0 shard_map.201
  35.6 8.8 %all_to_all.26.parts = bf16[4,128,128]{2,1,0:T(8,128)(2,1)S(1)} all-to-all(bf16[4,128,128]{2,1,0:T(8,128)(2,1)S(1)} %get-tuple-element.15), channel_id=1, replica_groups=mesh['slab'=128,'chan'=4] {'chan'}, dimensions={0} | all-to-all | bytes 262144 | tf_op jit(solution)/shard_map/all_to_all | solution.py:359
  44.3 1.0 shard_map.202
  45.4 8.2 %all-to-all-start.2 = ((bf16[128,8,128]{2,1,0:T(8,128)(2,1)}), bf16[128,8,128]{2,1,0:T(8,128)(2,1)}, u32[]{:S(2)}, u32[]{:S(2)}) async-start(bf16[128,8,128]{2,1,0:T(8,128)(2,1)} %bitcast.12), calls=%async_computation.2 | async-start | bytes 524288 | tf_op jit(solution)/shard_map/all_to_all | solution.py:359
  53.6 1.6 %copy.61 = bf16[64,2,4096]{2,0,1:T(8,128)(2,1)} copy(bf16[64,2,4096]{2,1,0:T(2,128)(2,1)S(1)} %copy-done.14) | data formatting | bytes 2097152 | tf_op jit(solution)/shard_map/optimization_barrier | solution.py:375
  55.2 0.6 copy.62
  55.8 0.7 copy.64.cot
  56.5 0.2 copy.63
  56.7 1.7 %convolution_add_fusion.base = f32[4096,128]{1,0:T(8,128)S(1)} fusion(bf16[4096,128]{0,1:T(8,128)(2,1)} %bitcast.75, f32[128]{0:T(128)S(1)} %add.31, bf16[64,64]{1,0:T(8,128)(2,1)S(1)} %copy-done.16), kind=kOutput, calls=%fused_computation | convolution fusion | flops 134873088 | bytes 3154432 | tf_op jit(solution)/shard_map/dot_general | solution.py:90
  58.4 10.1 %all-to-all-done.2 = bf16[128,8,128]{2,1,0:T(8,128)(2,1)} async-done(((bf16[128,8,128]{2,1,0:T(8,128)(2,1)}), bf16[128,8,128]{2,1,0:T(8,128)(2,1)}, u32[]{:S(2)}, u32[]{:S(2)}) %all-to-all-start.2) | async-done | bytes 262176 | tf_op jit(solution)/shard_map/all_to_all | solution.py:359
  68.6 1.0 copy-done.4
  69.5 0.8 copy-done.7
  70.3 0.7 copy-done.11
  71.0 0.7 copy-done.12
  71.7 0.7 copy-done.13
  72.4 7.3 %shard_map.203 = (bf16[4096,128]{1,0:T(8,128)(2,1)S(1)}, bf16[1280,128]{1,0:T(8,128)(2,1)S(1)}) custom-call(bf16[1024,128]{1,0:T(8,128)(2,1)} %bitcast.13.modes, f32[4096,128]{1,0:T(8,128)S(1)} %convolution_add_fusion.base, bf16[4096,128]{1,0:T(8,128)(2,1)S(1)} %copy.64.cot, bf16[40,4096]{1,0:T(8,128)(2,1)S(1)} %concatenate.24.own, ...), custom_call_target="tpu_custom_call" | custom-call | flops 400000000 | bytes 5238784 | tf_op jit(solution)/shard_map/pallas_call | solution.py:167
  79.7 1.0 copy-done.2
  80.7 0.7 copy-done.5
  81.4 5.5 %all-to-all-start.3 = ((bf16[640,2,128]{2,1,0:T(2,128)(2,1)}), bf16[640,2,128]{2,1,0:T(2,128)(2,1)S(1)}, u32[]{:S(2)}, u32[]{:S(2)}) async-start(bf16[640,2,128]{2,1,0:T(2,128)(2,1)} %bitcast.73), calls=%async_computation.3 | async-start | bytes 655360 | tf_op jit(solution)/shard_map/all_to_all | solution.py:359
  87.0 0.7 constant_dynamic-slice_fusion
  87.7 16.0 %all-to-all-done.3 = bf16[640,2,128]{2,1,0:T(2,128)(2,1)S(1)} async-done(((bf16[640,2,128]{2,1,0:T(2,128)(2,1)}), bf16[640,2,128]{2,1,0:T(2,128)(2,1)S(1)}, u32[]{:S(2)}, u32[]{:S(2)}) %all-to-all-start.3) | async-done | bytes 327712 | tf_op jit(solution)/shard_map/all_to_all | solution.py:359
  103.6 1.2 copy-done.1
  104.9 0.8 copy-done.8
  105.6 1.9 %shard_map.204 = (f32[2,128,64]{2,1,0:T(8,128)S(1)}, bf16[512,128]{1,0:T(8,128)(2,1)}) custom-call(bf16[1280,128]{1,0:T(8,128)(2,1)S(1)} %bitcast.72, bf16[2,16,128,64]{3,2,1,0:T(8,128)(2,1)S(1)} %bitcast.71, bf16[128,128]{1,0:T(8,128)(2,1)S(1)} %copy-done.8, bf16[256,64]{1,0:T(8,128)(2,1)S(1)} %copy-done.6, f32[8,128]{1,0:T(8,128)S(1)} %broadcast_in_dim.2.scale), custom_call_target="tpu_custom_call" | custom-call | flops 40000000 | bytes 1118208 | tf_op jit(solution)/shard_map/pallas_call | solution.py:167
  107.6 5.5 %all-to-all-start.4 = ((bf16[128,4,128]{2,1,0:T(4,128)(2,1)}), bf16[128,4,128]{2,1,0:T(4,128)(2,1)S(1)}, u32[]{:S(2)}, u32[]{:S(2)}) async-start(bf16[128,4,128]{2,1,0:T(4,128)(2,1)} %bitcast.22), calls=%async_computation.4 | async-start | bytes 262144 | tf_op jit(solution)/shard_map/all_to_all | solution.py:359
  113.1 0.4 fusion.16
  113.5 2.1 %shard_map.205 = f32[2,16,128,64]{3,2,1,0:T(8,128)} custom-call(f32[32,128]{1,0:T(8,128)S(1)} %get-tuple-element.22.coeff, f32[2,128,64]{2,1,0:T(8,128)S(1)} %get-tuple-element.23.hat), custom_call_target="tpu_custom_call" | custom-call | flops 8000000 | bytes 1130496 | tf_op jit(solution)/shard_map/pallas_call | solution.py:167
  115.7 10.2 %all-to-all-done.4 = bf16[128,4,128]{2,1,0:T(4,128)(2,1)S(1)} async-done(((bf16[128,4,128]{2,1,0:T(4,128)(2,1)}), bf16[128,4,128]{2,1,0:T(4,128)(2,1)S(1)}, u32[]{:S(2)}, u32[]{:S(2)}) %all-to-all-start.4) | async-done | bytes 131104 | tf_op jit(solution)/shard_map/all_to_all | solution.py:359
  126.0 0.6 slice.27
  126.6 0.5 slice_bitcast_fusion
  127.2 0.1 copy.77
  127.3 0.4 copy.66
  127.7 0.3 copy.67
  128.0 0.2 convolution_convert_fusion.1
  128.2 0.1 reshape.88
  128.3 0.3 convolution_bitcast_fusion
  128.7 0.5 reshape.89
  129.2 1.2 fusion.1
  (41 shorter events, 0.3 us)
Async XLA Ops:
  0.6 3.3 %copy-start.18 = (bf16[128,64,1,1]{0,1,3,2:T(8,128)(2,1)S(1)}, bf16[128,64,1,1]{0,1,3,2:T(8,128)(2,1)}, u32[]{:S(2)}) copy-start(bf16[128,64,1,1]{0,1,3,2:T(8,128)(2,1)} %constant.95) | copy-start | bytes 49156
  1.8 32.8 %copy-start = (bf16[2,16,64,4,32]{2,4,3,1,0:T(8,128)(2,1)S(1)}, bf16[2,16,64,4,32]{2,4,3,1,0:T(8,128)(2,1)}, u32[]{:S(2)}) copy-start(bf16[2,16,64,4,32]{2,4,3,1,0:T(8,128)(2,1)} %param.20) | copy-start | bytes 1572868
  1.8 32.8 %copy-start.9 = (bf16[64,256]{1,0:T(8,128)(2,1)S(1)}, bf16[64,256]{1,0:T(8,128)(2,1)}, u32[]{:S(2)}) copy-start(bf16[64,256]{1,0:T(8,128)(2,1)} %constant.83.along) | copy-start | bytes 98308
  3.5 40.9 %copy-start.10 = (bf16[128,128]{1,0:T(8,128)(2,1)S(1)}, bf16[128,128]{1,0:T(8,128)(2,1)}, u32[]{:S(2)}) copy-start(bf16[128,128]{1,0:T(8,128)(2,1)} %constant.84.spread) | copy-start | bytes 98308
  3.9 49.7 %copy-start.14 = (bf16[64,2,4096]{2,1,0:T(2,128)(2,1)S(1)}, bf16[64,2,4096]{2,1,0:T(2,128)(2,1)}, u32[]{:S(2)}) copy-start(bf16[64,2,4096]{2,1,0:T(2,128)(2,1)} %param.18) | copy-start | bytes 3145732
  34.6 20.5 %copy-start.20 = (bf16[64]{0:T(256)(128)(2,1)S(1)}, bf16[64]{0:T(256)(128)(2,1)}, u32[]{:S(2)}) copy-start(bf16[64]{0:T(256)(128)(2,1)} %param.22) | copy-start | bytes 388
  35.6 19.7 %copy-start.15 = (bf16[64,2,4096]{2,1,0:T(2,128)(2,1)S(1)}, bf16[64,2,4096]{2,1,0:T(2,128)(2,1)}, u32[]{:S(2)}) copy-start(bf16[64,2,4096]{2,1,0:T(2,128)(2,1)} %param.19) | copy-start | bytes 3145732
  45.4 23.2 %all-to-all-start.2 = ((bf16[128,8,128]{2,1,0:T(8,128)(2,1)}), bf16[128,8,128]{2,1,0:T(8,128)(2,1)}, u32[]{:S(2)}, u32[]{:S(2)}) async-start(bf16[128,8,128]{2,1,0:T(8,128)(2,1)} %bitcast.12), calls=%async_computation.2 | async-start | bytes 524288 | tf_op jit(solution)/shard_map/all_to_all | solution.py:359
  55.8 0.9 copy-start.16
  68.6 1.0 copy-start.4
  69.5 0.8 copy-start.7
  70.3 0.7 copy-start.11
  71.0 0.7 copy-start.12
  71.7 0.7 copy-start.13
  72.4 31.2 %copy-start.6 = (bf16[256,64]{1,0:T(8,128)(2,1)S(1)}, bf16[256,64]{1,0:T(8,128)(2,1)}, u32[]{:S(2)}) copy-start(bf16[256,64]{1,0:T(8,128)(2,1)} %constant.91.back) | copy-start | bytes 98308
  79.7 1.0 copy-start.2
  80.7 0.7 copy-start.5
  81.4 22.2 %all-to-all-start.3 = ((bf16[640,2,128]{2,1,0:T(2,128)(2,1)}), bf16[640,2,128]{2,1,0:T(2,128)(2,1)S(1)}, u32[]{:S(2)}, u32[]{:S(2)}) async-start(bf16[640,2,128]{2,1,0:T(2,128)(2,1)} %bitcast.73), calls=%async_computation.3 | async-start | bytes 655360 | tf_op jit(solution)/shard_map/all_to_all | solution.py:359
  103.6 1.2 copy-start.1
  104.9 0.8 copy-start.8
  105.6 7.5 %copy-start.3 = (bf16[4096,128]{1,0:T(8,128)(2,1)S(1)}, bf16[4096,128]{1,0:T(8,128)(2,1)}, u32[]{:S(2)}) copy-start(bf16[4096,128]{1,0:T(8,128)(2,1)} %copy-done.2) | copy-start | bytes 3145732
  107.6 18.4 %all-to-all-start.4 = ((bf16[128,4,128]{2,1,0:T(4,128)(2,1)}), bf16[128,4,128]{2,1,0:T(4,128)(2,1)S(1)}, u32[]{:S(2)}, u32[]{:S(2)}) async-start(bf16[128,4,128]{2,1,0:T(4,128)(2,1)} %bitcast.22), calls=%async_computation.4 | async-start | bytes 262144 | tf_op jit(solution)/shard_map/all_to_all | solution.py:359
  113.5 14.4 %copy-start.17 = (bf16[64,128,1,1]{1,0,3,2:T(8,128)(2,1)S(1)}, bf16[64,128,1,1]{1,0,3,2:T(8,128)(2,1)}, u32[]{:S(2)}) copy-start(bf16[64,128,1,1]{1,0,3,2:T(8,128)(2,1)} %constant.96) | copy-start | bytes 49156
  113.5 14.8 %copy-start.19 = (bf16[16,2,64,1,1]{2,0,1,4,3:T(8,128)(2,1)S(1)}, bf16[16,2,64,1,1]{2,0,1,4,3:T(8,128)(2,1)}, u32[]{:S(2)}) copy-start(bf16[16,2,64,1,1]{2,0,1,4,3:T(8,128)(2,1)} %constant.97) | copy-start | bytes 12292

commit v2 on v1

v2 whole, which is shorter than its diff:
```python
import math

import jax
import jax.numpy as jnp
import numpy as np
from jax import lax
from jax.experimental import pallas as pl
from jax.experimental.pallas import tpu as pltpu
from jax.sharding import PartitionSpec as P

MX = 32
MY = 32
MZ = 16
NX = 256
NY = 64
NZ = 64
C = 64
OWN = 16
SLAB = 128
PLANES = 2
LOW = 4
HIGH = 8
CELLS = NY * NZ
LANES = 128
HALF = 64
CHUNK = 10
BACK = 4
SHARE = 7
INVERSE_ROOT = 1.0 / math.sqrt(NX * NY * NZ)
F32 = jnp.float32
BF16 = jnp.bfloat16


def kept(total, length):
    index = np.arange(total)
    return np.where(index < total // 2, index, index - total + length)


def waves(frequency, length):
    wound = (frequency[:, None] * np.arange(length)[None, :]) % length
    angle = np.float32(2.0 * math.pi / length) * wound.astype(np.float32)
    return np.cos(angle), np.sin(angle)


def table(values):
    return jnp.asarray(np.asarray(values, np.float32)).astype(BF16)


def axis_tables():
    cos_z, sin_z = waves(np.arange(MZ), NZ)
    cos_y, sin_y = waves(kept(MY, NY), NY)
    cos_x, sin_x = waves(kept(MX, NX), NX)
    return cos_z, sin_z, cos_y, sin_y, cos_x, sin_x


def rows_of_ky(real, imag):
    both = np.stack([real, imag], 1).reshape(HIGH, LOW, 2, -1)
    return np.transpose(both, (0, 2, 1, 3))


def pack_tables():
    cos_z, sin_z, cos_y, sin_y, cos_x, sin_x = axis_tables()
    weight = (np.where(np.arange(MZ) == 0, 1.0, 2.0) / (NX * NY * NZ))[:, None]
    to_z = np.stack([weight * cos_z, -weight * sin_z], 1).reshape(2 * MZ, NZ).T
    from_z = np.concatenate([cos_z, -sin_z], 0)
    real = np.stack([cos_y, sin_y], 1).reshape(MY, 2 * NY)
    imag = np.stack([-sin_y, cos_y], 1).reshape(MY, 2 * NY)
    to_y = rows_of_ky(real, imag).reshape(2 * MY, 2 * NY).T
    real = np.stack([cos_y, sin_y], 2).reshape(MY, 2 * NY)
    imag = np.stack([-sin_y, cos_y], 2).reshape(MY, 2 * NY)
    from_y = rows_of_ky(real, imag).reshape(HIGH, 8, 2 * NY)
    from_y = np.concatenate([from_y, np.zeros((HIGH, CHUNK - 8, 2 * NY))], 1)
    from_y = from_y.reshape(HIGH * CHUNK, 2 * NY)
    pick = np.zeros((SLAB, 32))
    owner = np.arange(SLAB)
    pick[owner, np.minimum(owner // SHARE, OWN)] = 1.0
    split = np.concatenate([cos_x, sin_x], 0).reshape(2 * MX, SLAB, PLANES)
    gather = np.transpose(split, (2, 0, 1)).reshape(2 * PLANES * MX, SLAB)
    quarter = NY // 4
    cos_q = np.transpose(cos_y[:, :quarter].reshape(HIGH, LOW, quarter), (1, 0, 2))
    sin_q = np.transpose(sin_y[:, :quarter].reshape(HIGH, LOW, quarter), (1, 0, 2))
    lines_z = from_z.reshape(2 * MZ, NZ)
    pair_from_z = np.kron(np.eye(2), lines_z)
    plain_z = np.stack([cos_z, -sin_z], 1).reshape(2 * MZ, NZ)
    pair_to_z = np.kron(np.eye(2), plain_z)
    real = np.stack([cos_q, sin_q], -1)
    imag = np.stack([-sin_q, cos_q], -1)
    own_from_y = np.stack([real, imag], 2).reshape(2 * MY, 2 * quarter)
    real = np.stack([cos_q, -sin_q], -1)
    imag = np.stack([sin_q, cos_q], -1)
    own_to_y = np.stack([real, imag], 1)
    own_to_y = np.pad(own_to_y, ((0, 0), (0, 0), (0, 0), (0, 0), (0, BACK - 2)))
    own_to_y = np.transpose(own_to_y, (0, 1, 3, 2, 4)).reshape(LOW * 2 * quarter, HIGH * BACK)
    parts = dict(
        to_y=to_y, to_z=to_z, from_z=from_z, from_y=from_y, pick=pick,
        gather=gather, spread=gather.T, pair_to_z=pair_to_z, own_to_y=own_to_y,
    )
    early = dict(pair_from_z=pair_from_z, own_from_y=own_from_y)
    places = {}
    packed = []
    for group in (early, parts):
        rows = []
        start = 0
        for name, part in group.items():
            places[name] = (start, part.shape[0], part.shape[1])
            start += part.shape[0]
            rows.append(np.pad(part, ((0, 0), (0, LANES - part.shape[1]))))
        packed.append(np.concatenate(rows, 0))
    return places, packed[0], packed[1]


PLACES, EARLY, PACKED = pack_tables()


def get(tables, name):
    start, rows, lanes = PLACES[name]
    return tables[start : start + rows, :lanes]


def mm(left, right):
    return jnp.dot(left, right, preferred_element_type=F32)


def swap(values):
    return pltpu.roll(values, HALF, 1)


def turn(values, shift):
    return pltpu.roll(values, shift, 1)


def quarter_turns(real, imag, forward):
    lane = lane_of(real.shape)
    even = (lane // 32) % 2 == 0
    sign = jnp.where(lane < HALF, 1.0, -1.0)
    sums, gaps = [], []
    for part in (real, imag):
        other = swap(part)
        sums.append(part + other)
        gaps.append(part - other)
    if forward:
        cross = (gaps[1], -gaps[0])
    else:
        cross = (-gaps[1], gaps[0])
    return [
        jnp.where(even, e + sign * turn(e, 96), sign * turn(d, 32) + c)
        for e, d, c in zip(sums, gaps, cross)
    ]


def by_group(blocks):
    group = lane_of(blocks[0].shape) // 32
    out = blocks[0]
    for index in range(1, 4):
        out = jnp.where(group == index, blocks[index], out)
    return out


def lane_of(shape):
    return lax.broadcasted_iota(jnp.int32, shape, 1)


def gelu_grad(pre_act):
    normal_cdf = 0.5 * (1.0 + lax.erf(pre_act * (1.0 / math.sqrt(2.0))))
    normal_pdf = jnp.exp(-0.5 * pre_act * pre_act) * (1.0 / math.sqrt(2.0 * math.pi))
    return normal_cdf + pre_act * normal_pdf


def two_words(values):
    head = values.astype(BF16).astype(F32)
    rest = values - head
    return jnp.where(lane_of(values.shape) < HALF, head, swap(rest))


def middle_kernel(
    modes, bases, cots, owns, tables, grad_out, out,
    up, flat, down, rows, grad, packed, base, cot, own, sem
):
    loads = [
        pltpu.make_async_copy(source, target, sem.at[index + 3])
        for index, (source, target) in enumerate(((bases, base), (cots, cot), (owns, own)))
    ]
    for load in loads:
        load.start()

    @pl.loop(0, MZ, unroll=4)
    def _(kz):
        start = pl.multiple_of(kz * 64, 64)
        up[pl.ds(pl.multiple_of(kz * 128, 128), 128), :] = mm(
            get(tables, "to_y"), modes[pl.ds(start, 64), :]
        )

    loads[0].wait()

    @pl.loop(0, NY // 2, unroll=4)
    def _(pair):
        left = up[pl.ds(pair * 2, 2 * MZ, stride=NY), :]
        right = up[pl.ds(pair * 2 + 1, 2 * MZ, stride=NY), :]
        both = jnp.concatenate([left, right], 1).astype(BF16)
        grid = mm(get(tables, "to_z"), both)
        start = pl.multiple_of(pair * 128, 128)
        flat[pl.ds(start, 64), :] = grid[:, :LANES] + base[pl.ds(start, 64), :]
        start = pl.multiple_of(pair * 128 + 64, 64)
        flat[pl.ds(start, 64), :] = grid[:, LANES:] + base[pl.ds(start, 64), :]

    loads[1].wait()

    def block_of(block, total):
        here = pl.ds(pl.multiple_of(block * 64, 64), 64)
        values = cot[here, :].astype(F32) * gelu_grad(flat[here, :])
        values = values.astype(BF16)
        grad[here, :] = values
        return total + jnp.sum(values.astype(F32).reshape(8, 8, LANES), 0)

    bias = lax.fori_loop(0, CELLS // 64, block_of, jnp.zeros((8, LANES), F32), unroll=2)
    bias = jnp.broadcast_to(jnp.sum(bias, 0, keepdims=True), (8, LANES))
    save = pltpu.make_async_copy(grad, grad_out, sem.at[0])
    save.start()

    @pl.loop(0, NY // 2, unroll=4)
    def _(pair):
        start = pl.multiple_of(pair * 128, 128)
        left = grad[pl.ds(start, 64), :]
        right = grad[pl.ds(pl.multiple_of(start + 64, 64), 64), :]
        lines = mm(get(tables, "from_z"), jnp.concatenate([left, right], 1))
        start = pl.multiple_of(pair * 64, 64)
        down[pl.ds(start, 32), :] = lines[:, :LANES]
        down[pl.ds(pl.multiple_of(start + 32, 32), 32), :] = lines[:, LANES:]

    loads[2].wait()
    sums = jnp.zeros((2 * OWN, LANES), F32)
    for quarter in range(4):
        cells = pl.ds(quarter * 1024, 1024)
        sums += mm(own[quarter * 32 : quarter * 32 + 32, :], grad[cells, :])
    lower = sums[:OWN] + swap(sums[OWN:])
    bias = bias + swap(bias)
    words = two_words(jnp.concatenate([lower, bias, jnp.zeros_like(bias)], 0)).astype(BF16)

    flat[:SLAB, :] = mm(get(tables, "pick"), words)
    sends = []
    half_rows = SLAB * CHUNK // 2
    for half in range(2):

        @pl.loop(half * MZ // 2, (half + 1) * MZ // 2, unroll=4)
        def _(kz):
            lines = down[pl.ds(kz, 2 * NY, stride=MZ), :].astype(BF16)
            start = pl.multiple_of(kz * HIGH * CHUNK, HIGH * CHUNK)
            rows[pl.ds(start, HIGH * CHUNK), :] = mm(get(tables, "from_y"), lines)

        here = pl.ds(half * half_rows, half_rows)
        rows[pl.ds(half * half_rows + 8, SLAB // 2, stride=CHUNK), :] = flat[
            half * SLAB // 2 : (half + 1) * SLAB // 2, :
        ]
        packed[here, :] = rows[here, :].astype(BF16)
        sends.append(pltpu.make_async_copy(packed.at[here, :], out.at[here, :], sem.at[half + 1]))
        sends[half].start()
    for send in sends + [save]:
        send.wait()


def places(count, anywhere):
    kinds = [pltpu.HBM if index in anywhere else pltpu.VMEM for index in range(count)]
    return [pl.BlockSpec(memory_space=kind) for kind in kinds]


def call(kernel, shapes, scratch, flops, room, *operands, anywhere=(), anywhere_out=()):
    moved = sum(s.size * s.dtype.itemsize for s in list(operands) + list(shapes))
    return pl.pallas_call(
        kernel,
        out_shape=shapes,
        in_specs=places(len(operands), anywhere),
        out_specs=places(len(shapes), anywhere_out),
        scratch_shapes=scratch,
        cost_estimate=pl.CostEstimate(flops=flops, bytes_accessed=moved, transcendentals=0),
        compiler_params=pltpu.CompilerParams(vmem_limit_bytes=room * 2**20),
    )(*operands)


def middle(modes, base, cot, own, tables):
    shapes = (
        jax.ShapeDtypeStruct((CELLS, LANES), BF16),
        jax.ShapeDtypeStruct((SLAB * CHUNK, LANES), BF16),
    )
    scratch = [
        pltpu.VMEM((2 * NY * MZ, LANES), F32),
        pltpu.VMEM((CELLS, LANES), F32),
        pltpu.VMEM((2 * NY * MZ, LANES), F32),
        pltpu.VMEM((SLAB * CHUNK, LANES), F32),
        pltpu.VMEM((CELLS, LANES), BF16),
        pltpu.VMEM((SLAB * CHUNK, LANES), BF16),
        pltpu.VMEM((CELLS, LANES), F32),
        pltpu.VMEM((CELLS, LANES), BF16),
        pltpu.VMEM((LANES, CELLS // 4), BF16),
        pltpu.SemaphoreType.DMA((6,)),
    ]
    return call(
        middle_kernel, shapes, scratch, 400_000_000, 52, modes, base, cot, own, tables,
        anywhere=(1, 2, 3), anywhere_out=(0, 1),
    )


def own_kernel(field, tables, out, lines):
    for pair in range(8):
        part = lax.dot_general(
            get(tables, "pair_from_z"),
            field[:, pair * LANES : (pair + 1) * LANES],
            (((1,), (1,)), ((), ())),
            preferred_element_type=F32,
        )
        for half in range(2):
            top = half * 32
            real, imag = quarter_turns(part[top : top + 16], part[top + 16 : top + 32], True)
            start = (pair * 2 + half) * 32
            lines[start : start + 16, :] = real
            lines[start + 16 : start + 32, :] = imag
    for pair in range(MZ // 2):
        left = lines[pl.ds(2 * pair, 32, stride=MZ), :]
        right = lines[pl.ds(2 * pair + 1, 32, stride=MZ), :]
        both = jnp.concatenate([left, right], 1).astype(BF16)
        both = mm(get(tables, "own_from_y"), both)
        for half in range(2):
            part = both[:, half * LANES : (half + 1) * LANES]
            part = by_group([part[low * 16 : low * 16 + 16] for low in range(LOW)])
            start = (2 * pair + half) * 16
            out[start : start + 16, :] = part.astype(BF16)


def own_modes(own, tables):
    shapes = (jax.ShapeDtypeStruct((2 * SLAB, LANES), BF16),)
    scratch = [pltpu.VMEM((NY // 4 * 2 * MZ, LANES), F32)]
    return call(own_kernel, shapes, scratch, 4_000_000, 8, own, tables)[0]


def grid_kernel(modes, point, tables, out, sums, bias, lines, wide):
    wide[...] = modes[...].astype(F32)
    for kz in range(MZ):
        both = mm(get(tables, "own_to_y"), modes[kz * 32 : kz * 32 + 32, :])
        both = by_group([both[low * 32 : low * 32 + 32] for low in range(LOW)])
        real, imag = quarter_turns(both[:16], both[16:], False)
        lines[kz * 32 : kz * 32 + 16, :] = real
        lines[kz * 32 + 16 : kz * 32 + 32, :] = imag
    for pair in range(8):
        left = lines[pl.ds(2 * pair, 2 * MZ, stride=16), :]
        right = lines[pl.ds(2 * pair + 1, 2 * MZ, stride=16), :]
        both = jnp.concatenate([left, right], 0).T.astype(BF16)
        both = mm(both, get(tables, "pair_to_z"))
        for quarter in range(4):
            start = quarter * 1024 + pair * LANES
            here = both[quarter * 32 : quarter * 32 + 32] + point[:, start : start + LANES]
            out[:, start : start + LANES] = here.astype(BF16)
    words = wide[pl.ds(2, OWN, stride=BACK * SHARE), :]
    sums[...] = (words + swap(words))[:, :HALF]
    words = wide[pl.ds(BACK * SHARE * OWN + 2, 8, stride=1), :]
    bias[...] = (words + swap(words))[:1, :HALF]


def own_grid(modes, point, tables):
    shapes = (
        jax.ShapeDtypeStruct((2 * OWN, CELLS), BF16),
        jax.ShapeDtypeStruct((OWN, C), F32),
        jax.ShapeDtypeStruct((1, C), F32),
    )
    scratch = [pltpu.VMEM((2 * NY // 4 * MZ, LANES), F32), pltpu.VMEM((SLAB * BACK, LANES), F32)]
    return call(grid_kernel, shapes, scratch, 8_000_000, 8, modes, point, tables)


def along_x(tables, left, right):
    both = mm(get(tables, "gather"), jnp.concatenate([left, right], 1).astype(BF16))
    return both[: 2 * MX], both[2 * MX :]


def mix_kernel(pencils, weight, tables, coeff, out, wide):
    wide[...] = pencils[...].astype(F32)
    left = wide[pl.ds(0, SLAB, stride=2), :]
    right = wide[pl.ds(1, SLAB, stride=2), :]
    near, far = along_x(tables, left, right)
    near = near + jnp.concatenate([turn(far[:, :LANES], 112), turn(far[:, LANES:], 112)], 1)
    modes_real = (near[:MX, :LANES] + near[MX:, LANES:]).astype(BF16).astype(F32)
    modes_imag = (near[:MX, LANES:] - near[MX:, :LANES]).astype(BF16).astype(F32)
    coeff[0] = modes_real
    coeff[1] = modes_imag
    for m in range(LOW):
        rows = pl.ds(m * MX, MX)
        real = jnp.zeros((MX, C), F32)
        imag = jnp.zeros((MX, C), F32)
        for i in range(OWN):
            at = m * 32 + i
            left = jnp.broadcast_to(modes_real[:, at : at + 1], (MX, C))
            right = jnp.broadcast_to(modes_imag[:, at : at + 1], (MX, C))
            weight_real = weight[0, i, rows, :].astype(F32)
            weight_imag = weight[1, i, rows, :].astype(F32)
            real += left * weight_real - right * weight_imag
            imag += left * weight_imag + right * weight_real
        part = jnp.concatenate([real, imag], 1).astype(BF16)
        for peer in range(4):
            out[peer, rows, :] = part


def mix(pencils, weight, tables):
    shapes = (
        jax.ShapeDtypeStruct((2, MX, LANES), F32),
        jax.ShapeDtypeStruct((4, LOW * MX, LANES), BF16),
    )
    scratch = [pltpu.VMEM((2 * SLAB, LANES), F32)]
    return call(mix_kernel, shapes, scratch, 4_000_000, 8, pencils, weight, tables)


def spread_kernel(parts, tables, out, rows):
    total = parts[0].astype(F32)
    for peer in range(1, 4):
        total += parts[peer].astype(F32)
    lane = lane_of((MX, LANES))
    for m in range(LOW):
        here = total[m * MX : (m + 1) * MX]
        there = swap(here)
        zero = jnp.zeros_like(here)
        a = jnp.where(lane < HALF, here, zero)
        b = jnp.where(lane < HALF, there, zero)
        c = jnp.where(lane < HALF, zero, there)
        d = jnp.where(lane < HALF, zero, here)
        top = jnp.concatenate([a, b], 1)
        second = jnp.concatenate([-b, a], 1)
        third = jnp.concatenate([c, d], 1)
        last = jnp.concatenate([-d, c], 1)
        block = jnp.concatenate([top, second, third, last], 0).astype(BF16)
        planes = mm(get(tables, "spread"), block)
        rows[pl.ds(m, SLAB, stride=8), :] = planes[:, :LANES]
        rows[pl.ds(LOW + m, SLAB, stride=8), :] = planes[:, LANES:]
    out[...] = rows[...].astype(BF16)


def spread_planes(parts, tables):
    shapes = (jax.ShapeDtypeStruct((SLAB * 8, LANES), BF16),)
    scratch = [pltpu.VMEM((SLAB * 8, LANES), F32)]
    return call(spread_kernel, shapes, scratch, 40_000_000, 8, parts, tables)[0]


def adjoint_kernel(pencils, weights, tables, scale, hat, out, wide, rows, weight, sem):
    load = pltpu.make_async_copy(weights, weight, sem)
    load.start()
    wide[...] = pencils[...].astype(F32)
    lane = lane_of((MX, LANES))
    near_real = jnp.zeros((MX, LANES), F32)
    near_imag = jnp.zeros((MX, LANES), F32)
    factor = scale[0:1, :]
    for m in range(LOW):
        left = wide[pl.ds(m, SLAB, stride=CHUNK), :]
        right = wide[pl.ds(LOW + m, SLAB, stride=CHUNK), :]
        near, far = along_x(tables, left, right)
        first = near[:, :LANES] + swap(far[:, :LANES])
        second = near[:, LANES:] + swap(far[:, LANES:])
        real = (first[:MX] + second[MX:]) * factor
        imag = (second[:MX] - first[MX:]) * factor
        hat[0, pl.ds(m * MX, MX), :] = real.astype(BF16).astype(F32)[:, :C]
        hat[1, pl.ds(m * MX, MX), :] = imag.astype(BF16).astype(F32)[:, :C]
    load.wait()
    for m in range(LOW):
        at_m = pl.ds(m * MX, MX)
        real = hat[0, at_m, :]
        imag = hat[1, at_m, :]
        for i in range(OWN):
            weight_real = weight[0, i, at_m, :].astype(F32)
            weight_imag = weight[1, i, at_m, :].astype(F32)
            sum_real = jnp.sum(real * weight_real + imag * weight_imag, 1, keepdims=True)
            sum_imag = jnp.sum(imag * weight_real - real * weight_imag, 1, keepdims=True)
            near_real = jnp.where(lane == m * 32 + i, sum_real, near_real)
            near_imag = jnp.where(lane == m * 32 + i, sum_imag, near_imag)
    far_real = turn(near_real, 16)
    far_imag = turn(near_imag, 16)
    top = jnp.concatenate([near_real, near_imag], 1)
    second = jnp.concatenate([-near_imag, near_real], 1)
    third = jnp.concatenate([far_real, far_imag], 1)
    last = jnp.concatenate([-far_imag, far_real], 1)
    block = jnp.concatenate([top, second, third, last], 0).astype(BF16)
    planes = mm(get(tables, "spread"), block)
    rows[pl.ds(0, SLAB, stride=BACK), :] = planes[:, :LANES]
    rows[pl.ds(1, SLAB, stride=BACK), :] = planes[:, LANES:]
    rider = wide[pl.ds(8, SLAB, stride=CHUNK), :]
    total = jnp.sum(rider, 0, keepdims=True)
    total = jnp.broadcast_to(total, (8, LANES))
    total = two_words((total + swap(total)) * INVERSE_ROOT)
    rows[pl.ds(2, SLAB, stride=BACK), :] = jnp.broadcast_to(total[:1], (SLAB, LANES))
    rows[pl.ds(3, SLAB, stride=BACK), :] = jnp.zeros((SLAB, LANES), F32)
    out[...] = rows[...].astype(BF16)


def adjoint_planes(pencils, weight, tables, scale):
    shapes = (
        jax.ShapeDtypeStruct((2, LOW * MX, C), F32),
        jax.ShapeDtypeStruct((SLAB * BACK, LANES), BF16),
    )
    scratch = [
        pltpu.VMEM((SLAB * CHUNK, LANES), F32),
        pltpu.VMEM((SLAB * BACK, LANES), F32),
        pltpu.VMEM((2, OWN, LOW * MX, C), BF16),
        pltpu.SemaphoreType.DMA,
    ]
    return call(
        adjoint_kernel, shapes, scratch, 40_000_000, 50, pencils, weight, tables, scale, anywhere=(1,)
    )


def outer_kernel(coeff, hat, out):
    modes_real = coeff[0]
    modes_imag = coeff[1]
    for m in range(LOW):
        rows = pl.ds(m * MX, MX)
        real = hat[0, rows, :]
        imag = hat[1, rows, :]
        for i in range(OWN):
            at = m * 32 + i
            left = jnp.broadcast_to(modes_real[:, at : at + 1], (MX, C))
            right = jnp.broadcast_to(modes_imag[:, at : at + 1], (MX, C))
            out[0, i, rows, :] = left * real + right * imag
            out[1, i, rows, :] = left * imag - right * real


def outer(coeff, hat):
    shapes = (jax.ShapeDtypeStruct((2, OWN, LOW * MX, C), F32),)
    return call(outer_kernel, shapes, [], 8_000_000, 8, coeff, hat)[0]


def over(values, axis):
    return lax.all_to_all(values, axis, split_axis=0, concat_axis=0, tiled=True)


def paired(matrix):
    zero = jnp.zeros_like(matrix)
    upper = jnp.concatenate([matrix, zero], 1)
    lower = jnp.concatenate([zero, matrix], 1)
    return jnp.concatenate([upper, lower], 0)


def body(field, cotangent, spectral_weight, point_weight, point_bias):
    chan_start = lax.axis_index("chan") * OWN
    own = lax.dynamic_slice_in_dim(field, chan_start, OWN, 0)
    own = jnp.transpose(own.reshape(OWN, PLANES, 4, CELLS // 4), (2, 1, 0, 3))
    own = own.reshape(LANES, CELLS // 4)
    own_rows = lax.dynamic_slice_in_dim(point_weight, chan_start, OWN, 0)
    weight = jnp.transpose(spectral_weight, (0, 1, 3, 4, 2)).reshape(2, OWN, LOW * MX, C)
    tables = table(PACKED)
    first = own_modes(own, table(EARLY))
    field, cotangent, first = lax.optimization_barrier((field, cotangent, first))
    pencils = over(first.reshape(SLAB, PLANES, LANES), "slab").reshape(NX, LANES)

    cells = jnp.transpose(field, (2, 1, 0)).reshape(CELLS, LANES)
    cot = jnp.transpose(cotangent, (2, 1, 0)).reshape(CELLS, LANES)
    bias = jnp.tile(point_bias.astype(F32), 2)[None]
    base = mm(cells, paired(point_weight)) + bias
    coeff, parts = mix(pencils, weight, tables)
    parts = over(parts, "chan")
    planes = spread_planes(parts, tables)
    modes = over(planes.reshape(SLAB, 8, LANES), "slab").reshape(SLAB * 8, LANES)
    grad, rows = middle(modes, base, cot, own, tables)
    arrived = over(rows.reshape(SLAB * CHUNK // 2, 2, LANES), "slab").reshape(SLAB * CHUNK, LANES)
    point_back = mm(paired(own_rows), grad.T)
    kz_weight = jnp.where(lax.axis_index("slab") < HIGH, 1.0, 2.0) / (NX * NY * NZ)
    scale = jnp.full((8, LANES), kz_weight, F32)
    hat, rows = adjoint_planes(arrived, weight, tables, scale)
    final = over(rows.reshape(SLAB, BACK, LANES), "slab").reshape(SLAB * BACK, LANES)
    outer_part = outer(coeff, hat).reshape(2, OWN, LOW, MX, C)
    grad_spectral = jnp.transpose(outer_part, (0, 1, 4, 2, 3))
    planes, grad_pointwise, grad_bias = own_grid(final, point_back, tables)
    grad_input = jnp.transpose(planes.reshape(PLANES, OWN, CELLS), (1, 0, 2))
    return grad_input, grad_spectral, grad_pointwise, grad_bias[0]


def solution(mesh):
    placed = (
        P(None, "slab", None),
        P(None, "slab", None),
        P(None, "chan", None, "slab", None),
        P(),
        P(),
    )
    return jax.shard_map(
        body,
        mesh=mesh,
        in_specs=placed,
        out_specs=(
            P("chan", "slab", None),
            P(None, "chan", None, "slab", None),
            P("chan", None),
            P(),
        ),
        check_vma=False,
    )
```

time: 131 us -> 122 us (0.931)
  local copies, waits for them, and re-layouts: 16.6 us -> 10.3 us
  waiting for transfers between devices: 36.3 us -> 33.4 us
  Pallas kernels: 13.3 us -> 16.1 us
  matrix products: 4.12 us -> 2.27 us
  other arithmetic: 1.32 us -> 0 us
    unnamed x44 -> x12, local copies, waits for them, and re-layouts: 7.74 us -> 0.78 us
    all_to_all x3, waiting for transfers between devices: 36.3 us -> 33.4 us  [over(): return lax.all_to_all(values, axis, split_axis=0, concat_axis=0, tiled=True)]
    pallas_call x5 -> x7, Pallas kernels: 13.3 us -> 16.1 us  [call(): pl.pallas_call(kernel, out_shape=shapes, in_specs=places(len(operands), a...]
    optimization_barrier x3 -> x2, local copies, waits for them, and re-layouts: 2.26 us -> 4.6 us  [body(): lax.optimization_barrier((field, cotangent, first))]
    dot_general x4 -> x0, matrix products: 1.95 us -> none  [the longest x1 1.28 us: own_modes(): jnp.einsum('cxyz,zpk->cxkpy', grid_view, forward_z, preferred_element_typ...]
    reshape x1, local copies, waits for them, and re-layouts: 0.66 us -> 2.26 us  [body(): cot = jnp.transpose(cotangent, (2, 1, 0)).reshape(CELLS, LANES)]
  transfers between devices with their start and end apart: 3 -> 3, of which waited for: 3 -> 3; matrix products, arithmetic and copies ran while one was open for 5% -> 8% of each run, Pallas kernels for 2% -> 2%
where the time goes in v2:
time: 122 us; the launch traced here: 121 us
  blocking collectives  38.3 us (31%)
  waiting for transfers between devices  33.4 us (27%)
  starting transfers between devices  20.3 us (17%)
  Pallas kernels  16.1 us (13%)
  local copies, waits for them, and re-layouts  10.3 us (8%)
  matrix products  2.27 us (2%)
    all_to_all x2, blocking collectives, over(): return lax.all_to_all(values, axis, split_axis=0, concat_axis=0, tiled=True)  38.3 us
    all_to_all x3, waiting for transfers between devices, over(): return lax.all_to_all(values, axis, split_axis=0, concat_axis=0, tiled=True)  33.4 us
    all_to_all x3, starting transfers between devices, over(): return lax.all_to_all(values, axis, split_axis=0, concat_axis=0, tiled=True)  20.3 us
    pallas_call x7, Pallas kernels, call(): pl.pallas_call(kernel, out_shape=shapes, in_specs=places(len(operands), a...  16.1 us
    optimization_barrier x2, local copies, waits for them, and re-layouts, body(): lax.optimization_barrier((field, cotangent, first))  4.6 us
  transfers between devices with their start and end apart: 3, of which 3 were waited for; matrix products, arithmetic and copies ran while one was open for 8% of the time, Pallas kernels for 2%

profile of v2, /device:TPU:1, one launch (start us, length us, event | category | flops | bytes accessed | tf_op | source)
XLA Modules:
  0.0 121.5 jit_solution(13291431211218383806)
XLA Ops:
  0.6 0.0 copy-start
  0.6 0.0 copy-start.1
  0.7 1.2 %constant_dynamic-slice_fusion.1 = bf16[16,2,4096]{2,1,0:T(2,128)(2,1)S(1)} fusion(bf16[64,2,4096]{2,1,0:T(2,128)(2,1)} %param.7, s32[]{:T(128)S(6)} %select_n.8), kind=kLoop, calls=%fused_computation.22 | loop fusion | bytes 524292 | tf_op jit(solution)/shard_map/dynamic_slice | solution.py:536
  1.9 0.2 reshape.70
  2.1 0.2 copy.14
  2.2 0.0 copy-start.2
  2.3 0.7 copy-done.2
  3.0 0.7 shard_map.102
  3.7 29.7 %all_to_all.25 = bf16[128,2,128]{2,1,0:T(2,128)(2,1)S(1)} all-to-all(bf16[128,2,128]{2,1,0:T(2,128)(2,1)S(1)} %bitcast.38), channel_id=1, replica_groups=mesh['slab'=128,'chan'=4] {'slab'}, dimensions={0} | all-to-all | bytes 131072 | tf_op jit(solution)/shard_map/all_to_all | solution.py:524
  33.4 0.0 copy-done
  33.4 0.0 copy-done.1
  33.4 0.0 copy-start.5
  33.4 1.0 shard_map.103
  34.4 8.6 %all_to_all.26.parts = bf16[4,128,128]{2,1,0:T(8,128)(2,1)S(1)} all-to-all(bf16[4,128,128]{2,1,0:T(8,128)(2,1)S(1)} %get-tuple-element.17), channel_id=1, replica_groups=mesh['slab'=128,'chan'=4] {'chan'}, dimensions={0} | all-to-all | bytes 262144 | tf_op jit(solution)/shard_map/all_to_all | solution.py:524
  43.0 1.0 shard_map.104
  44.0 7.2 %all-to-all-start.2 = ((bf16[128,8,128]{2,1,0:T(8,128)(2,1)}), bf16[128,8,128]{2,1,0:T(8,128)(2,1)S(1)}, u32[]{:S(2)}, u32[]{:S(2)}) async-start(bf16[128,8,128]{2,1,0:T(8,128)(2,1)} %bitcast.7), calls=%async_computation.2 | async-start | bytes 524288 | tf_op jit(solution)/shard_map/all_to_all | solution.py:524
  51.2 1.8 %copy.15 = bf16[64,2,4096]{2,0,1:T(8,128)(2,1)S(1)} copy(bf16[64,2,4096]{2,1,0:T(2,128)(2,1)} %param.7) | data formatting | bytes 2097152 | tf_op jit(solution)/shard_map/optimization_barrier | solution.py:543
  53.0 0.0 copy-done.5
  53.0 0.1 add.23
  53.1 0.0 copy-start.4
  53.1 2.8 %copy.16 = bf16[64,2,4096]{2,0,1:T(8,128)(2,1)} copy(bf16[64,2,4096]{2,1,0:T(2,128)(2,1)} %param.8) | data formatting | bytes 2097152 | tf_op jit(solution)/shard_map/optimization_barrier | solution.py:543
  55.9 2.3 %copy.17.cots = bf16[4096,128]{1,0:T(8,128)(2,1)} copy(bf16[4096,128]{0,1:T(8,128)(2,1)} %bitcast.41) | data formatting | bytes 2097152 | tf_op jit(solution)/shard_map/reshape | solution.py:547
  58.2 0.0 copy-done.4
  58.2 1.8 %convolution_add_fusion.bases = f32[4096,128]{1,0:T(8,128)} fusion(bf16[4096,128]{0,1:T(8,128)(2,1)S(1)} %bitcast.40, f32[128]{0:T(128)S(1)} %add.23, bf16[64,64]{1,0:T(8,128)(2,1)S(1)} %copy-done.4), kind=kOutput, calls=%fused_computation | convolution fusion | flops 134873088 | bytes 3154432 | tf_op jit(solution)/shard_map/dot_general | solution.py:121
  60.0 6.5 %all-to-all-done.2 = bf16[128,8,128]{2,1,0:T(8,128)(2,1)S(1)} async-done(((bf16[128,8,128]{2,1,0:T(8,128)(2,1)}), bf16[128,8,128]{2,1,0:T(8,128)(2,1)S(1)}, u32[]{:S(2)}, u32[]{:S(2)}) %all-to-all-start.2) | async-done | bytes 262176 | tf_op jit(solution)/shard_map/all_to_all | solution.py:524
  66.5 8.1 %shard_map.105 = (bf16[4096,128]{1,0:T(8,128)(2,1)}, bf16[1280,128]{1,0:T(8,128)(2,1)}) custom-call(bf16[1024,128]{1,0:T(8,128)(2,1)S(1)} %bitcast.35, f32[4096,128]{1,0:T(8,128)} %convolution_add_fusion.bases, bf16[4096,128]{1,0:T(8,128)(2,1)} %copy.17.cots, bf16[128,1024]{1,0:T(8,128)(2,1)S(1)} %bitcast.33, bf16[880,128]{1,0:T(8,128)(2,1)S(1)} %copy-done), custom_call_target="tpu_custom_call" | custom-call | flops 400000000 | bytes 5271552 | tf_op jit(solution)/shard_map/pallas_call | solution.py:268
  74.7 0.0 copy-start.3
  74.7 7.4 %all-to-all-start.3 = ((bf16[640,2,128]{2,1,0:T(2,128)(2,1)}), bf16[640,2,128]{2,1,0:T(2,128)(2,1)S(1)}, u32[]{:S(2)}, u32[]{:S(2)}) async-start(bf16[640,2,128]{2,1,0:T(2,128)(2,1)} %bitcast.13), calls=%async_computation.3 | async-start | bytes 655360 | tf_op jit(solution)/shard_map/all_to_all | solution.py:524
  82.2 16.5 %all-to-all-done.3 = bf16[640,2,128]{2,1,0:T(2,128)(2,1)S(1)} async-done(((bf16[640,2,128]{2,1,0:T(2,128)(2,1)}), bf16[640,2,128]{2,1,0:T(2,128)(2,1)S(1)}, u32[]{:S(2)}, u32[]{:S(2)}) %all-to-all-start.3) | async-done | bytes 327712 | tf_op jit(solution)/shard_map/all_to_all | solution.py:524
  98.7 2.0 %shard_map.106 = (f32[2,128,64]{2,1,0:T(8,128)S(1)}, bf16[512,128]{1,0:T(8,128)(2,1)}) custom-call(bf16[1280,128]{1,0:T(8,128)(2,1)S(1)} %bitcast.34, bf16[2,16,128,64]{3,2,1,0:T(8,128)(2,1)S(1)} %bitcast.31, bf16[880,128]{1,0:T(8,128)(2,1)S(1)} %copy-done, f32[8,128]{1,0:T(8,128)S(1)} %broadcast_in_dim.2.scale), custom_call_target="tpu_custom_call" | custom-call | flops 40000000 | bytes 1277952 | tf_op jit(solution)/shard_map/pallas_call | solution.py:268
  100.7 5.7 %all-to-all-start.4 = ((bf16[128,4,128]{2,1,0:T(4,128)(2,1)}), bf16[128,4,128]{2,1,0:T(4,128)(2,1)S(1)}, u32[]{:S(2)}, u32[]{:S(2)}) async-start(bf16[128,4,128]{2,1,0:T(4,128)(2,1)} %bitcast.15), calls=%async_computation.4 | async-start | bytes 262144 | tf_op jit(solution)/shard_map/all_to_all | solution.py:524
  106.4 0.0 copy-done.3
  106.4 0.4 fusion.12.point
  106.8 2.0 %shard_map.108 = f32[2,16,128,64]{3,2,1,0:T(8,128)} custom-call(f32[2,32,128]{2,1,0:T(8,128)S(1)} %get-tuple-element.24.coeff, f32[2,128,64]{2,1,0:T(8,128)S(1)} %get-tuple-element.25.hat), custom_call_target="tpu_custom_call" | custom-call | flops 8000000 | bytes 1146880 | tf_op jit(solution)/shard_map/pallas_call | solution.py:268
  108.9 10.3 %all-to-all-done.4 = bf16[128,4,128]{2,1,0:T(4,128)(2,1)S(1)} async-done(((bf16[128,4,128]{2,1,0:T(4,128)(2,1)}), bf16[128,4,128]{2,1,0:T(4,128)(2,1)S(1)}, u32[]{:S(2)}, u32[]{:S(2)}) %all-to-all-start.4) | async-done | bytes 131104 | tf_op jit(solution)/shard_map/all_to_all | solution.py:524
  119.2 1.3 %shard_map.107 = (bf16[32,4096]{1,0:T(8,128)(2,1)S(1)}, f32[16,64]{1,0:T(8,128)}, f32[1,64]{1,0:T(1,128)}) custom-call(bf16[512,128]{1,0:T(8,128)(2,1)S(1)} %bitcast.36, f32[32,4096]{1,0:T(8,128)S(1)} %fusion.12.point, bf16[880,128]{1,0:T(8,128)(2,1)S(1)} %copy-done), custom_call_target="tpu_custom_call" | custom-call | flops 8000000 | bytes 1147136 | tf_op jit(solution)/shard_map/pallas_call | solution.py:268
  120.5 1.0 copy.22
  (3 shorter events, 0.0 us)
Async XLA Ops:
  0.6 32.8 %copy-start = (bf16[880,128]{1,0:T(8,128)(2,1)S(1)}, bf16[880,128]{1,0:T(8,128)(2,1)}, u32[]{:S(2)}) copy-start(bf16[880,128]{1,0:T(8,128)(2,1)} %constant.45.tables) | copy-start | bytes 675844
  0.6 32.7 %copy-start.1 = (bf16[2,16,64,4,32]{2,4,3,1,0:T(8,128)(2,1)S(1)}, bf16[2,16,64,4,32]{2,4,3,1,0:T(8,128)(2,1)}, u32[]{:S(2)}) copy-start(bf16[2,16,64,4,32]{2,4,3,1,0:T(8,128)(2,1)} %param.9) | copy-start | bytes 1572868
  2.2 0.8 copy-start.2
  33.4 19.6 %copy-start.5 = (bf16[64]{0:T(256)(128)(2,1)S(1)}, bf16[64]{0:T(256)(128)(2,1)}, u32[]{:S(2)}) copy-start(bf16[64]{0:T(256)(128)(2,1)} %param.11) | copy-start | bytes 388
  44.0 22.5 %all-to-all-start.2 = ((bf16[128,8,128]{2,1,0:T(8,128)(2,1)}), bf16[128,8,128]{2,1,0:T(8,128)(2,1)S(1)}, u32[]{:S(2)}, u32[]{:S(2)}) async-start(bf16[128,8,128]{2,1,0:T(8,128)(2,1)} %bitcast.7), calls=%async_computation.2 | async-start | bytes 524288 | tf_op jit(solution)/shard_map/all_to_all | solution.py:524
  53.1 5.1 %copy-start.4 = (bf16[64,64]{1,0:T(8,128)(2,1)S(1)}, bf16[64,64]{1,0:T(8,128)(2,1)}, u32[]{:S(2)}) copy-start(bf16[64,64]{1,0:T(8,128)(2,1)} %param.10) | copy-start | bytes 24580
  74.7 31.7 %copy-start.3 = (bf16[4096,128]{1,0:T(8,128)(2,1)S(1)}, bf16[4096,128]{1,0:T(8,128)(2,1)}, u32[]{:S(2)}) copy-start(bf16[4096,128]{1,0:T(8,128)(2,1)} %get-tuple-element.22) | copy-start | bytes 3145732
  74.7 24.0 %all-to-all-start.3 = ((bf16[640,2,128]{2,1,0:T(2,128)(2,1)}), bf16[640,2,128]{2,1,0:T(2,128)(2,1)S(1)}, u32[]{:S(2)}, u32[]{:S(2)}) async-start(bf16[640,2,128]{2,1,0:T(2,128)(2,1)} %bitcast.13), calls=%async_computation.3 | async-start | bytes 655360 | tf_op jit(solution)/shard_map/all_to_all | solution.py:524
  100.7 18.5 %all-to-all-start.4 = ((bf16[128,4,128]{2,1,0:T(4,128)(2,1)}), bf16[128,4,128]{2,1,0:T(4,128)(2,1)S(1)}, u32[]{:S(2)}, u32[]{:S(2)}) async-start(bf16[128,4,128]{2,1,0:T(4,128)(2,1)} %bitcast.15), calls=%async_computation.4 | async-start | bytes 262144 | tf_op jit(solution)/shard_map/all_to_all | solution.py:524

commit v3 on v2

--- a/solution.py
+++ b/solution.py
@@ -61,13 +61,13 @@
 def pack_tables():
     cos_z, sin_z, cos_y, sin_y, cos_x, sin_x = axis_tables()
     weight = (np.where(np.arange(MZ) == 0, 1.0, 2.0) / (NX * NY * NZ))[:, None]
-    to_z = np.stack([weight * cos_z, -weight * sin_z], 1).reshape(2 * MZ, NZ).T
-    from_z = np.concatenate([cos_z, -sin_z], 0)
+    plain_z = np.stack([cos_z, -sin_z], 1)
+    wide = plain_z[:, :, None, None, :] * np.eye(8)[None, None, :, :, None]
+    tall = (weight[:, :, None, None, None] * wide).reshape(256, 512).T
+    wide = wide.reshape(256, 512)
     real = np.stack([cos_y, sin_y], 1).reshape(MY, 2 * NY)
     imag = np.stack([-sin_y, cos_y], 1).reshape(MY, 2 * NY)
     to_y = rows_of_ky(real, imag).reshape(2 * MY, 2 * NY).T
-    real = np.stack([cos_y, sin_y], 2).reshape(MY, 2 * NY)
-    imag = np.stack([-sin_y, cos_y], 2).reshape(MY, 2 * NY)
     from_y = rows_of_ky(real, imag).reshape(HIGH, 8, 2 * NY)
     from_y = np.concatenate([from_y, np.zeros((HIGH, CHUNK - 8, 2 * NY))], 1)
     from_y = from_y.reshape(HIGH * CHUNK, 2 * NY)
@@ -79,12 +79,8 @@
     quarter = NY // 4
     cos_q = np.transpose(cos_y[:, :quarter].reshape(HIGH, LOW, quarter), (1, 0, 2))
     sin_q = np.transpose(sin_y[:, :quarter].reshape(HIGH, LOW, quarter), (1, 0, 2))
-    lines_z = from_z.reshape(2 * MZ, NZ)
-    pair_from_z = np.kron(np.eye(2), lines_z)
-    plain_z = np.stack([cos_z, -sin_z], 1).reshape(2 * MZ, NZ)
-    pair_to_z = np.kron(np.eye(2), plain_z)
-    real = np.stack([cos_q, sin_q], -1)
-    imag = np.stack([-sin_q, cos_q], -1)
+    real = np.stack([cos_q, sin_q], 2)
+    imag = np.stack([-sin_q, cos_q], 2)
     own_from_y = np.stack([real, imag], 2).reshape(2 * MY, 2 * quarter)
     real = np.stack([cos_q, -sin_q], -1)
     imag = np.stack([sin_q, cos_q], -1)
@@ -92,24 +88,35 @@
     own_to_y = np.pad(own_to_y, ((0, 0), (0, 0), (0, 0), (0, 0), (0, BACK - 2)))
     own_to_y = np.transpose(own_to_y, (0, 1, 3, 2, 4)).reshape(LOW * 2 * quarter, HIGH * BACK)
     parts = dict(
-        to_y=to_y, to_z=to_z, from_z=from_z, from_y=from_y, pick=pick,
-        gather=gather, spread=gather.T, pair_to_z=pair_to_z, own_to_y=own_to_y,
-    )
-    early = dict(pair_from_z=pair_from_z, own_from_y=own_from_y)
+        to_y=to_y, from_y=from_y, pick=pick, gather=gather, spread=gather.T,
+    )
+    side = np.zeros((256, LANES))
+    side[: 2 * MY, : 2 * quarter] = own_from_y
+    side[2 * MY : 2 * MY + 8 * quarter, : HIGH * BACK] = own_to_y
+    wide = np.concatenate([wide, side], 1)
     places = {}
-    packed = []
-    for group in (early, parts):
-        rows = []
-        start = 0
-        for name, part in group.items():
-            places[name] = (start, part.shape[0], part.shape[1])
-            start += part.shape[0]
-            rows.append(np.pad(part, ((0, 0), (0, LANES - part.shape[1]))))
-        packed.append(np.concatenate(rows, 0))
-    return places, packed[0], packed[1]
-
-
-PLACES, EARLY, PACKED = pack_tables()
+    rows = []
+    start = 0
+    for name, part in parts.items():
+        places[name] = (start, part.shape[0], part.shape[1])
+        start += part.shape[0]
+        rows.append(np.pad(part, ((0, 0), (0, LANES - part.shape[1]))))
+    return places, np.concatenate(rows, 0), wide, tall
+
+
+PLACES, PACKED, WIDE, TALL = pack_tables()
+
+
+def wide_part(wide):
+    return wide[:, :512]
+
+
+def own_from_y(wide):
+    return wide[:64, 512:544]
+
+
+def own_to_y(wide):
+    return wide[64:192, 512:544]
 
 
 def get(tables, name):
@@ -161,9 +168,9 @@
 
 
 def gelu_grad(pre_act):
-    normal_cdf = 0.5 * (1.0 + lax.erf(pre_act * (1.0 / math.sqrt(2.0))))
-    normal_pdf = jnp.exp(-0.5 * pre_act * pre_act) * (1.0 / math.sqrt(2.0 * math.pi))
-    return normal_cdf + pre_act * normal_pdf
+    normal_cdf = 0.5 + 0.5 * lax.erf(pre_act * (1.0 / math.sqrt(2.0)))
+    bell = jnp.exp2(pre_act * pre_act * (-0.5 * math.log2(math.e)))
+    return normal_cdf + (pre_act * (1.0 / math.sqrt(2.0 * math.pi))) * bell
 
 
 def two_words(values):
@@ -173,12 +180,13 @@
 
 
 def middle_kernel(
-    modes, bases, cots, owns, tables, grad_out, out,
-    up, flat, down, rows, grad, packed, base, cot, own, sem
+    modes, bases, cots, own, wide, tall, tables, grad_out, out,
+    up, flat, down, rows, grad, packed, base, cot, sem
 ):
+    pairs = ((bases, base), (cots, cot))
     loads = [
         pltpu.make_async_copy(source, target, sem.at[index + 3])
-        for index, (source, target) in enumerate(((bases, base), (cots, cot), (owns, own)))
+        for index, (source, target) in enumerate(pairs)
     ]
     for load in loads:
         load.start()
@@ -186,54 +194,43 @@
     @pl.loop(0, MZ, unroll=4)
     def _(kz):
         start = pl.multiple_of(kz * 64, 64)
-        up[pl.ds(pl.multiple_of(kz * 128, 128), 128), :] = mm(
-            get(tables, "to_y"), modes[pl.ds(start, 64), :]
-        )
+        lines = mm(get(tables, "to_y"), modes[pl.ds(start, 64), :])
+        up[pl.ds(2 * kz, 2), :, :] = lines.reshape(2, NY, LANES)
 
     loads[0].wait()
-
-    @pl.loop(0, NY // 2, unroll=4)
-    def _(pair):
-        left = up[pl.ds(pair * 2, 2 * MZ, stride=NY), :]
-        right = up[pl.ds(pair * 2 + 1, 2 * MZ, stride=NY), :]
-        both = jnp.concatenate([left, right], 1).astype(BF16)
-        grid = mm(get(tables, "to_z"), both)
-        start = pl.multiple_of(pair * 128, 128)
-        flat[pl.ds(start, 64), :] = grid[:, :LANES] + base[pl.ds(start, 64), :]
-        start = pl.multiple_of(pair * 128 + 64, 64)
-        flat[pl.ds(start, 64), :] = grid[:, LANES:] + base[pl.ds(start, 64), :]
-
+    for pair in range(4):
+        sides = [
+            up[:, (2 * pair + side) * 8 : (2 * pair + side) * 8 + 8, :].reshape(256, LANES)
+            for side in range(2)
+        ]
+        grid = mm(tall[...], jnp.concatenate(sides, 1).astype(BF16))
+        for side in range(2):
+            cells = pl.ds((2 * pair + side) * 512, 512)
+            flat[cells, :] = grid[:, side * LANES : (side + 1) * LANES] + base[cells, :]
     loads[1].wait()
 
-    def block_of(block, total):
+    @pl.loop(0, CELLS // 64, unroll=4)
+    def _(block):
         here = pl.ds(pl.multiple_of(block * 64, 64), 64)
-        values = cot[here, :].astype(F32) * gelu_grad(flat[here, :])
-        values = values.astype(BF16)
-        grad[here, :] = values
-        return total + jnp.sum(values.astype(F32).reshape(8, 8, LANES), 0)
-
-    bias = lax.fori_loop(0, CELLS // 64, block_of, jnp.zeros((8, LANES), F32), unroll=2)
-    bias = jnp.broadcast_to(jnp.sum(bias, 0, keepdims=True), (8, LANES))
+        grad[here, :] = (cot[here, :].astype(F32) * gelu_grad(flat[here, :])).astype(BF16)
+
     save = pltpu.make_async_copy(grad, grad_out, sem.at[0])
     save.start()
-
-    @pl.loop(0, NY // 2, unroll=4)
-    def _(pair):
-        start = pl.multiple_of(pair * 128, 128)
-        left = grad[pl.ds(start, 64), :]
-        right = grad[pl.ds(pl.multiple_of(start + 64, 64), 64), :]
-        lines = mm(get(tables, "from_z"), jnp.concatenate([left, right], 1))
-        start = pl.multiple_of(pair * 64, 64)
-        down[pl.ds(start, 32), :] = lines[:, :LANES]
-        down[pl.ds(pl.multiple_of(start + 32, 32), 32), :] = lines[:, LANES:]
-
-    loads[2].wait()
-    sums = jnp.zeros((2 * OWN, LANES), F32)
+    for pair in range(4):
+        sides = [grad[(2 * pair + side) * 512 : (2 * pair + side) * 512 + 512, :] for side in range(2)]
+        lines = mm(wide_part(wide), jnp.concatenate(sides, 1)).reshape(2 * MZ, 8, 2 * LANES)
+        for side in range(2):
+            group = (2 * pair + side) * 8
+            down[:, group : group + 8, :] = lines[:, :, side * LANES : (side + 1) * LANES]
+
+    sums = jnp.zeros((3 * OWN, LANES), F32)
     for quarter in range(4):
         cells = pl.ds(quarter * 1024, 1024)
-        sums += mm(own[quarter * 32 : quarter * 32 + 32, :], grad[cells, :])
-    lower = sums[:OWN] + swap(sums[OWN:])
-    bias = bias + swap(bias)
+        left = own[quarter * 32 : quarter * 32 + 32, :]
+        left = jnp.concatenate([left, jnp.ones((OWN, CELLS // 4), BF16)], 0)
+        sums += mm(left, grad[cells, :])
+    lower = sums[:OWN] + swap(sums[OWN : 2 * OWN])
+    bias = sums[2 * OWN : 2 * OWN + 8] + swap(sums[2 * OWN : 2 * OWN + 8])
     words = two_words(jnp.concatenate([lower, bias, jnp.zeros_like(bias)], 0)).astype(BF16)
 
     flat[:SLAB, :] = mm(get(tables, "pick"), words)
@@ -243,7 +240,7 @@
 
         @pl.loop(half * MZ // 2, (half + 1) * MZ // 2, unroll=4)
         def _(kz):
-            lines = down[pl.ds(kz, 2 * NY, stride=MZ), :].astype(BF16)
+            lines = down[pl.ds(2 * kz, 2), :, :].reshape(2 * NY, LANES).astype(BF16)
             start = pl.multiple_of(kz * HIGH * CHUNK, HIGH * CHUNK)
             rows[pl.ds(start, HIGH * CHUNK), :] = mm(get(tables, "from_y"), lines)
 
@@ -276,48 +273,47 @@
     )(*operands)
 
 
-def middle(modes, base, cot, own, tables):
+def middle(modes, base, cot, own, wide, tables):
     shapes = (
         jax.ShapeDtypeStruct((CELLS, LANES), BF16),
         jax.ShapeDtypeStruct((SLAB * CHUNK, LANES), BF16),
     )
     scratch = [
-        pltpu.VMEM((2 * NY * MZ, LANES), F32),
+        pltpu.VMEM((2 * MZ, NY, LANES), F32),
         pltpu.VMEM((CELLS, LANES), F32),
-        pltpu.VMEM((2 * NY * MZ, LANES), F32),
+        pltpu.VMEM((2 * MZ, NY, LANES), F32),
         pltpu.VMEM((SLAB * CHUNK, LANES), F32),
         pltpu.VMEM((CELLS, LANES), BF16),
         pltpu.VMEM((SLAB * CHUNK, LANES), BF16),
         pltpu.VMEM((CELLS, LANES), F32),
         pltpu.VMEM((CELLS, LANES), BF16),
-        pltpu.VMEM((LANES, CELLS // 4), BF16),
-        pltpu.SemaphoreType.DMA((6,)),
+        pltpu.SemaphoreType.DMA((5,)),
     ]
     return call(
-        middle_kernel, shapes, scratch, 400_000_000, 52, modes, base, cot, own, tables,
-        anywhere=(1, 2, 3), anywhere_out=(0, 1),
-    )
-
-
-def own_kernel(field, tables, out, lines):
-    for pair in range(8):
+        middle_kernel, shapes, scratch, 400_000_000, 52,
+        modes, base, cot, own, wide, table(TALL), tables,
+        anywhere=(1, 2), anywhere_out=(0, 1),
+    )
+
+
+def own_kernel(field, wide, out, lines):
+    for group in range(2):
         part = lax.dot_general(
-            get(tables, "pair_from_z"),
-            field[:, pair * LANES : (pair + 1) * LANES],
+            wide_part(wide),
+            field[:, group * 512 : (group + 1) * 512],
             (((1,), (1,)), ((), ())),
             preferred_element_type=F32,
-        )
-        for half in range(2):
-            top = half * 32
-            real, imag = quarter_turns(part[top : top + 16], part[top + 16 : top + 32], True)
-            start = (pair * 2 + half) * 32
-            lines[start : start + 16, :] = real
-            lines[start + 16 : start + 32, :] = imag
+        ).reshape(MZ, 2, 8, LANES)
+        real = part[:, 0].reshape(MZ * 8, LANES)
+        imag = part[:, 1].reshape(MZ * 8, LANES)
+        real, imag = quarter_turns(real, imag, True)
+        lines[:, 0, group * 8 : group * 8 + 8, :] = real.reshape(MZ, 8, LANES)
+        lines[:, 1, group * 8 : group * 8 + 8, :] = imag.reshape(MZ, 8, LANES)
     for pair in range(MZ // 2):
-        left = lines[pl.ds(2 * pair, 32, stride=MZ), :]
-        right = lines[pl.ds(2 * pair + 1, 32, stride=MZ), :]
+        left = lines[2 * pair].reshape(32, LANES)
+        right = lines[2 * pair + 1].reshape(32, LANES)
         both = jnp.concatenate([left, right], 1).astype(BF16)
-        both = mm(get(tables, "own_from_y"), both)
+        both = mm(own_from_y(wide), both)
         for half in range(2):
             part = both[:, half * LANES : (half + 1) * LANES]
             part = by_group([part[low * 16 : low * 16 + 16] for low in range(LOW)])
@@ -325,43 +321,41 @@
             out[start : start + 16, :] = part.astype(BF16)
 
 
-def own_modes(own, tables):
+def own_modes(own, wide):
     shapes = (jax.ShapeDtypeStruct((2 * SLAB, LANES), BF16),)
-    scratch = [pltpu.VMEM((NY // 4 * 2 * MZ, LANES), F32)]
-    return call(own_kernel, shapes, scratch, 4_000_000, 8, own, tables)[0]
-
-
-def grid_kernel(modes, point, tables, out, sums, bias, lines, wide):
+    scratch = [pltpu.VMEM((MZ, 2, NY // 4, LANES), F32)]
+    return call(own_kernel, shapes, scratch, 4_000_000, 8, own, wide)[0]
+
+
+def grid_kernel(modes, point, wide_z, out, sums, bias, lines, wide):
     wide[...] = modes[...].astype(F32)
     for kz in range(MZ):
-        both = mm(get(tables, "own_to_y"), modes[kz * 32 : kz * 32 + 32, :])
+        both = mm(own_to_y(wide_z), modes[kz * 32 : kz * 32 + 32, :])
         both = by_group([both[low * 32 : low * 32 + 32] for low in range(LOW)])
         real, imag = quarter_turns(both[:16], both[16:], False)
-        lines[kz * 32 : kz * 32 + 16, :] = real
-        lines[kz * 32 + 16 : kz * 32 + 32, :] = imag
-    for pair in range(8):
-        left = lines[pl.ds(2 * pair, 2 * MZ, stride=16), :]
-        right = lines[pl.ds(2 * pair + 1, 2 * MZ, stride=16), :]
-        both = jnp.concatenate([left, right], 0).T.astype(BF16)
-        both = mm(both, get(tables, "pair_to_z"))
+        lines[kz, 0] = real
+        lines[kz, 1] = imag
+    for group in range(2):
+        both = lines[:, :, group * 8 : group * 8 + 8, :].reshape(256, LANES)
+        both = mm(both.T.astype(BF16), wide_part(wide_z))
         for quarter in range(4):
-            start = quarter * 1024 + pair * LANES
-            here = both[quarter * 32 : quarter * 32 + 32] + point[:, start : start + LANES]
-            out[:, start : start + LANES] = here.astype(BF16)
+            cells = pl.ds(quarter * 1024 + group * 512, 512)
+            here = both[quarter * 32 : quarter * 32 + 32] + point[:, cells]
+            out[:, cells] = here.astype(BF16)
     words = wide[pl.ds(2, OWN, stride=BACK * SHARE), :]
     sums[...] = (words + swap(words))[:, :HALF]
     words = wide[pl.ds(BACK * SHARE * OWN + 2, 8, stride=1), :]
     bias[...] = (words + swap(words))[:1, :HALF]
 
 
-def own_grid(modes, point, tables):
+def own_grid(modes, point, wide):
     shapes = (
         jax.ShapeDtypeStruct((2 * OWN, CELLS), BF16),
         jax.ShapeDtypeStruct((OWN, C), F32),
         jax.ShapeDtypeStruct((1, C), F32),
     )
-    scratch = [pltpu.VMEM((2 * NY // 4 * MZ, LANES), F32), pltpu.VMEM((SLAB * BACK, LANES), F32)]
-    return call(grid_kernel, shapes, scratch, 8_000_000, 8, modes, point, tables)
+    scratch = [pltpu.VMEM((MZ, 2, NY // 4, LANES), F32), pltpu.VMEM((SLAB * BACK, LANES), F32)]
+    return call(grid_kernel, shapes, scratch, 8_000_000, 8, modes, point, wide)
 
 
 def along_x(tables, left, right):
@@ -539,7 +533,8 @@
     own_rows = lax.dynamic_slice_in_dim(point_weight, chan_start, OWN, 0)
     weight = jnp.transpose(spectral_weight, (0, 1, 3, 4, 2)).reshape(2, OWN, LOW * MX, C)
     tables = table(PACKED)
-    first = own_modes(own, table(EARLY))
+    wide = table(WIDE)
+    first = own_modes(own, wide)
     field, cotangent, first = lax.optimization_barrier((field, cotangent, first))
     pencils = over(first.reshape(SLAB, PLANES, LANES), "slab").reshape(NX, LANES)
 
@@ -551,7 +546,7 @@
     parts = over(parts, "chan")
     planes = spread_planes(parts, tables)
     modes = over(planes.reshape(SLAB, 8, LANES), "slab").reshape(SLAB * 8, LANES)
-    grad, rows = middle(modes, base, cot, own, tables)
+    grad, rows = middle(modes, base, cot, own, wide, tables)
     arrived = over(rows.reshape(SLAB * CHUNK // 2, 2, LANES), "slab").reshape(SLAB * CHUNK, LANES)
     point_back = mm(paired(own_rows), grad.T)
     kz_weight = jnp.where(lax.axis_index("slab") < HIGH, 1.0, 2.0) / (NX * NY * NZ)
@@ -560,7 +555,7 @@
     final = over(rows.reshape(SLAB, BACK, LANES), "slab").reshape(SLAB * BACK, LANES)
     outer_part = outer(coeff, hat).reshape(2, OWN, LOW, MX, C)
     grad_spectral = jnp.transpose(outer_part, (0, 1, 4, 2, 3))
-    planes, grad_pointwise, grad_bias = own_grid(final, point_back, tables)
+    planes, grad_pointwise, grad_bias = own_grid(final, point_back, wide)
     grad_input = jnp.transpose(planes.reshape(PLANES, OWN, CELLS), (1, 0, 2))
     return grad_input, grad_spectral, grad_pointwise, grad_bias[0]
 

time: 122 us -> 119 us (0.975)
  Pallas kernels: 16.1 us -> 13.2 us
    pallas_call x7, Pallas kernels: 16.1 us -> 13.2 us  [call(): pl.pallas_call(kernel, out_shape=shapes, in_specs=places(len(operands), a...]
where the time goes in v3:
time: 119 us
  blocking collectives  38.3 us (32%)
  waiting for transfers between devices  33.4 us (28%)
  starting transfers between devices  20.2 us (17%)
  Pallas kernels  13.2 us (11%)
  local copies, waits for them, and re-layouts  10.5 us (9%)
  matrix products  2.27 us (2%)
    all_to_all x2, blocking collectives, over(): return lax.all_to_all(values, axis, split_axis=0, concat_axis=0, tiled=True)  38.3 us
    all_to_all x3, waiting for transfers between devices, over(): return lax.all_to_all(values, axis, split_axis=0, concat_axis=0, tiled=True)  33.4 us
    all_to_all x3, starting transfers between devices, over(): return lax.all_to_all(values, axis, split_axis=0, concat_axis=0, tiled=True)  20.2 us
    pallas_call x7, Pallas kernels, call(): pl.pallas_call(kernel, out_shape=shapes, in_specs=places(len(operands), a...  13.2 us
    optimization_barrier x2, local copies, waits for them, and re-layouts, body(): lax.optimization_barrier((field, cotangent, first))  4.6 us
  transfers between devices with their start and end apart: 3, of which 3 were waited for; matrix products, arithmetic and copies ran while one was open for 8% of the time, Pallas kernels for 2%

profile of v3, /device:TPU:1, one launch (start us, length us, event | category | flops | bytes accessed | tf_op | source)
XLA Modules:
  0.0 118.6 jit_solution(6054369838098420248)
XLA Ops:
  0.6 0.0 copy-start.3
  0.6 0.0 copy-start
  0.7 1.2 %constant_dynamic-slice_fusion.1 = bf16[16,2,4096]{2,1,0:T(2,128)(2,1)S(1)} fusion(bf16[64,2,4096]{2,1,0:T(2,128)(2,1)} %param.8, s32[]{:T(128)S(6)} %select_n.8), kind=kLoop, calls=%fused_computation.22 | loop fusion | bytes 524292 | tf_op jit(solution)/shard_map/dynamic_slice | solution.py:530
  1.9 0.2 reshape.70
  2.1 0.2 copy.15
  2.2 0.0 copy-start.1
  2.3 1.0 copy-done.1
  3.2 0.7 shard_map.111
  3.9 29.7 %all_to_all.25 = bf16[128,2,128]{2,1,0:T(2,128)(2,1)S(1)} all-to-all(bf16[128,2,128]{2,1,0:T(2,128)(2,1)S(1)} %bitcast.38), channel_id=1, replica_groups=mesh['slab'=128,'chan'=4] {'slab'}, dimensions={0} | all-to-all | bytes 131072 | tf_op jit(solution)/shard_map/all_to_all | solution.py:518
  33.6 0.0 copy-done.3
  33.6 0.0 copy-done
  33.6 0.0 copy-start.7
  33.6 1.0 shard_map.112
  34.6 8.6 %all_to_all.26.parts = bf16[4,128,128]{2,1,0:T(8,128)(2,1)S(1)} all-to-all(bf16[4,128,128]{2,1,0:T(8,128)(2,1)S(1)} %get-tuple-element.17), channel_id=1, replica_groups=mesh['slab'=128,'chan'=4] {'chan'}, dimensions={0} | all-to-all | bytes 262144 | tf_op jit(solution)/shard_map/all_to_all | solution.py:518
  43.2 1.0 shard_map.113
  44.2 7.2 %all-to-all-start.2 = ((bf16[128,8,128]{2,1,0:T(8,128)(2,1)}), bf16[128,8,128]{2,1,0:T(8,128)(2,1)S(1)}, u32[]{:S(2)}, u32[]{:S(2)}) async-start(bf16[128,8,128]{2,1,0:T(8,128)(2,1)} %bitcast.7), calls=%async_computation.2 | async-start | bytes 524288 | tf_op jit(solution)/shard_map/all_to_all | solution.py:518
  51.4 1.8 %copy.16 = bf16[64,2,4096]{2,0,1:T(8,128)(2,1)S(1)} copy(bf16[64,2,4096]{2,1,0:T(2,128)(2,1)} %param.8) | data formatting | bytes 2097152 | tf_op jit(solution)/shard_map/optimization_barrier | solution.py:538
  53.2 0.0 copy-done.7
  53.2 0.1 add.23
  53.3 0.0 copy-start.6
  53.3 2.8 %copy.17 = bf16[64,2,4096]{2,0,1:T(8,128)(2,1)} copy(bf16[64,2,4096]{2,1,0:T(2,128)(2,1)} %param.9) | data formatting | bytes 2097152 | tf_op jit(solution)/shard_map/optimization_barrier | solution.py:538
  56.1 2.3 %copy.18.cots = bf16[4096,128]{1,0:T(8,128)(2,1)} copy(bf16[4096,128]{0,1:T(8,128)(2,1)} %bitcast.41) | data formatting | bytes 2097152 | tf_op jit(solution)/shard_map/reshape | solution.py:542
  58.4 0.0 copy-start.2
  58.4 0.0 copy-start.4
  58.4 0.0 copy-done.6
  58.4 1.8 %convolution_add_fusion.bases = f32[4096,128]{1,0:T(8,128)} fusion(bf16[4096,128]{0,1:T(8,128)(2,1)S(1)} %bitcast.40, f32[128]{0:T(128)S(1)} %add.23, bf16[64,64]{1,0:T(8,128)(2,1)S(1)} %copy-done.6), kind=kOutput, calls=%fused_computation | convolution fusion | flops 134873088 | bytes 3154432 | tf_op jit(solution)/shard_map/dot_general | solution.py:128
  60.2 6.5 %all-to-all-done.2 = bf16[128,8,128]{2,1,0:T(8,128)(2,1)S(1)} async-done(((bf16[128,8,128]{2,1,0:T(8,128)(2,1)}), bf16[128,8,128]{2,1,0:T(8,128)(2,1)S(1)}, u32[]{:S(2)}, u32[]{:S(2)}) %all-to-all-start.2) | async-done | bytes 262176 | tf_op jit(solution)/shard_map/all_to_all | solution.py:518
  66.7 0.0 copy-done.2
  66.7 0.0 copy-done.4
  66.7 5.4 %shard_map.114 = (bf16[4096,128]{1,0:T(8,128)(2,1)}, bf16[1280,128]{1,0:T(8,128)(2,1)}) custom-call(bf16[1024,128]{1,0:T(8,128)(2,1)S(1)} %bitcast.35, f32[4096,128]{1,0:T(8,128)} %convolution_add_fusion.bases, bf16[4096,128]{1,0:T(8,128)(2,1)} %copy.18.cots, bf16[128,1024]{1,0:T(8,128)(2,1)S(1)} %bitcast.33, bf16[256,640]{1,0:T(8,128)(2,1)S(1)} %copy-done.2, ...), custom_call_target="tpu_custom_call" | custom-call | flops 400000000 | bytes 5787648 | tf_op jit(solution)/shard_map/pallas_call | solution.py:265
  72.1 0.0 copy-start.5
  72.1 7.5 %all-to-all-start.3 = ((bf16[640,2,128]{2,1,0:T(2,128)(2,1)}), bf16[640,2,128]{2,1,0:T(2,128)(2,1)S(1)}, u32[]{:S(2)}, u32[]{:S(2)}) async-start(bf16[640,2,128]{2,1,0:T(2,128)(2,1)} %bitcast.13), calls=%async_computation.3 | async-start | bytes 655360 | tf_op jit(solution)/shard_map/all_to_all | solution.py:518
  79.6 16.5 %all-to-all-done.3 = bf16[640,2,128]{2,1,0:T(2,128)(2,1)S(1)} async-done(((bf16[640,2,128]{2,1,0:T(2,128)(2,1)}), bf16[640,2,128]{2,1,0:T(2,128)(2,1)S(1)}, u32[]{:S(2)}, u32[]{:S(2)}) %all-to-all-start.3) | async-done | bytes 327712 | tf_op jit(solution)/shard_map/all_to_all | solution.py:518
  96.1 2.0 %shard_map.115 = (f32[2,128,64]{2,1,0:T(8,128)S(1)}, bf16[512,128]{1,0:T(8,128)(2,1)}) custom-call(bf16[1280,128]{1,0:T(8,128)(2,1)S(1)} %bitcast.34, bf16[2,16,128,64]{3,2,1,0:T(8,128)(2,1)S(1)} %bitcast.31, bf16[592,128]{1,0:T(8,128)(2,1)S(1)} %copy-done.3, f32[8,128]{1,0:T(8,128)S(1)} %broadcast_in_dim.2.scale), custom_call_target="tpu_custom_call" | custom-call | flops 40000000 | bytes 1204224 | tf_op jit(solution)/shard_map/pallas_call | solution.py:265
  98.1 5.5 %all-to-all-start.4 = ((bf16[128,4,128]{2,1,0:T(4,128)(2,1)}), bf16[128,4,128]{2,1,0:T(4,128)(2,1)S(1)}, u32[]{:S(2)}, u32[]{:S(2)}) async-start(bf16[128,4,128]{2,1,0:T(4,128)(2,1)} %bitcast.15), calls=%async_computation.4 | async-start | bytes 262144 | tf_op jit(solution)/shard_map/all_to_all | solution.py:518
  103.7 0.0 copy-done.5
  103.7 0.4 fusion.12.point
  104.1 2.0 %shard_map.117 = f32[2,16,128,64]{3,2,1,0:T(8,128)} custom-call(f32[2,32,128]{2,1,0:T(8,128)S(1)} %get-tuple-element.24.coeff, f32[2,128,64]{2,1,0:T(8,128)S(1)} %get-tuple-element.25.hat), custom_call_target="tpu_custom_call" | custom-call | flops 8000000 | bytes 1146880 | tf_op jit(solution)/shard_map/pallas_call | solution.py:265
  106.1 10.3 %all-to-all-done.4 = bf16[128,4,128]{2,1,0:T(4,128)(2,1)S(1)} async-done(((bf16[128,4,128]{2,1,0:T(4,128)(2,1)}), bf16[128,4,128]{2,1,0:T(4,128)(2,1)S(1)}, u32[]{:S(2)}, u32[]{:S(2)}) %all-to-all-start.4) | async-done | bytes 131104 | tf_op jit(solution)/shard_map/all_to_all | solution.py:518
  116.5 1.2 shard_map.116
  117.6 1.0 copy.23
  (3 shorter events, 0.0 us)
Async XLA Ops:
  0.6 33.0 %copy-start.3 = (bf16[592,128]{1,0:T(8,128)(2,1)S(1)}, bf16[592,128]{1,0:T(8,128)(2,1)}, u32[]{:S(2)}) copy-start(bf16[592,128]{1,0:T(8,128)(2,1)} %constant.48.tables) | copy-start | bytes 454660
  0.6 33.0 %copy-start = (bf16[2,16,64,4,32]{2,4,3,1,0:T(8,128)(2,1)S(1)}, bf16[2,16,64,4,32]{2,4,3,1,0:T(8,128)(2,1)}, u32[]{:S(2)}) copy-start(bf16[2,16,64,4,32]{2,4,3,1,0:T(8,128)(2,1)} %param.10) | copy-start | bytes 1572868
  2.2 1.0 copy-start.1
  33.6 19.6 %copy-start.7 = (bf16[64]{0:T(256)(128)(2,1)S(1)}, bf16[64]{0:T(256)(128)(2,1)}, u32[]{:S(2)}) copy-start(bf16[64]{0:T(256)(128)(2,1)} %param.12) | copy-start | bytes 388
  44.2 22.5 %all-to-all-start.2 = ((bf16[128,8,128]{2,1,0:T(8,128)(2,1)}), bf16[128,8,128]{2,1,0:T(8,128)(2,1)S(1)}, u32[]{:S(2)}, u32[]{:S(2)}) async-start(bf16[128,8,128]{2,1,0:T(8,128)(2,1)} %bitcast.7), calls=%async_computation.2 | async-start | bytes 524288 | tf_op jit(solution)/shard_map/all_to_all | solution.py:518
  53.3 5.1 %copy-start.6 = (bf16[64,64]{1,0:T(8,128)(2,1)S(1)}, bf16[64,64]{1,0:T(8,128)(2,1)}, u32[]{:S(2)}) copy-start(bf16[64,64]{1,0:T(8,128)(2,1)} %param.11) | copy-start | bytes 24580
  58.4 8.4 %copy-start.2 = (bf16[256,640]{1,0:T(8,128)(2,1)S(1)}, bf16[256,640]{1,0:T(8,128)(2,1)}, u32[]{:S(2)}) copy-start(bf16[256,640]{1,0:T(8,128)(2,1)} %constant.47.wide.wide_z) | copy-start | bytes 983044
  58.4 8.4 %copy-start.4 = (bf16[512,256]{1,0:T(8,128)(2,1)S(1)}, bf16[512,256]{1,0:T(8,128)(2,1)}, u32[]{:S(2)}) copy-start(bf16[512,256]{1,0:T(8,128)(2,1)} %constant.49.tall) | copy-start | bytes 786436
  72.1 31.5 %copy-start.5 = (bf16[4096,128]{1,0:T(8,128)(2,1)S(1)}, bf16[4096,128]{1,0:T(8,128)(2,1)}, u32[]{:S(2)}) copy-start(bf16[4096,128]{1,0:T(8,128)(2,1)} %get-tuple-element.22) | copy-start | bytes 3145732
  72.1 24.0 %all-to-all-start.3 = ((bf16[640,2,128]{2,1,0:T(2,128)(2,1)}), bf16[640,2,128]{2,1,0:T(2,128)(2,1)S(1)}, u32[]{:S(2)}, u32[]{:S(2)}) async-start(bf16[640,2,128]{2,1,0:T(2,128)(2,1)} %bitcast.13), calls=%async_computation.3 | async-start | bytes 655360 | tf_op jit(solution)/shard_map/all_to_all | solution.py:518
  98.1 18.4 %all-to-all-start.4 = ((bf16[128,4,128]{2,1,0:T(4,128)(2,1)}), bf16[128,4,128]{2,1,0:T(4,128)(2,1)S(1)}, u32[]{:S(2)}, u32[]{:S(2)}) async-start(bf16[128,4,128]{2,1,0:T(4,128)(2,1)} %bitcast.15), calls=%async_computation.4 | async-start | bytes 262144 | tf_op jit(solution)/shard_map/all_to_all | solution.py:518

commit v4 on v3

--- a/solution.py
+++ b/solution.py
@@ -26,6 +26,8 @@
 CHUNK = 10
 BACK = 4
 SHARE = 7
+PITCH = 66
+OWN_ROOM = 56
 INVERSE_ROOT = 1.0 / math.sqrt(NX * NY * NZ)
 F32 = jnp.float32
 BF16 = jnp.bfloat16
@@ -88,7 +90,7 @@
     own_to_y = np.pad(own_to_y, ((0, 0), (0, 0), (0, 0), (0, 0), (0, BACK - 2)))
     own_to_y = np.transpose(own_to_y, (0, 1, 3, 2, 4)).reshape(LOW * 2 * quarter, HIGH * BACK)
     parts = dict(
-        to_y=to_y, from_y=from_y, pick=pick, gather=gather, spread=gather.T,
+        to_y=to_y, from_y=from_y, pick=pick,
     )
     side = np.zeros((256, LANES))
     side[: 2 * MY, : 2 * quarter] = own_from_y
@@ -101,10 +103,13 @@
         places[name] = (start, part.shape[0], part.shape[1])
         start += part.shape[0]
         rows.append(np.pad(part, ((0, 0), (0, LANES - part.shape[1]))))
-    return places, np.concatenate(rows, 0), wide, tall
-
-
-PLACES, PACKED, WIDE, TALL = pack_tables()
+    places["gather"] = (0, SLAB, SLAB)
+    places["spread"] = (SLAB, SLAB, SLAB)
+    pencil = np.concatenate([gather, gather.T], 0)
+    return places, np.concatenate(rows, 0), pencil, wide, tall
+
+
+PLACES, PACKED, PENCIL, WIDE, TALL = pack_tables()
 
 
 def wide_part(wide):
@@ -296,11 +301,27 @@
     )
 
 
-def own_kernel(field, wide, out, lines):
+def own_kernel(field, wides, out, own, raw, spread, lines, wide, sem):
+    start = pl.multiple_of(lax.axis_index("chan") * (OWN * HALF), OWN * HALF)
+    fetch = pltpu.make_async_copy(field.at[pl.ds(start, OWN * HALF), :], raw, sem.at[0])
+    fetch.start()
+    load = pltpu.make_async_copy(wides, wide, sem.at[1])
+    load.start()
+    fetch.wait()
+    for c in range(OWN):
+        spread[c * PITCH : c * PITCH + HALF, :] = raw[c * HALF : (c + 1) * HALF, :].astype(F32)
+    for tile in range(8):
+        parts = [
+            spread[pl.ds((quarter * 8 + tile) * 2 + plane, OWN, stride=PITCH), :]
+            for quarter in range(4)
+            for plane in range(PLANES)
+        ]
+        own[:, tile * LANES : (tile + 1) * LANES] = jnp.concatenate(parts, 0).astype(BF16)
+    load.wait()
     for group in range(2):
         part = lax.dot_general(
             wide_part(wide),
-            field[:, group * 512 : (group + 1) * 512],
+            own[:, group * 512 : (group + 1) * 512],
             (((1,), (1,)), ((), ())),
             preferred_element_type=F32,
         ).reshape(MZ, 2, 8, LANES)
@@ -321,13 +342,22 @@
             out[start : start + 16, :] = part.astype(BF16)
 
 
-def own_modes(own, wide):
-    shapes = (jax.ShapeDtypeStruct((2 * SLAB, LANES), BF16),)
-    scratch = [pltpu.VMEM((MZ, 2, NY // 4, LANES), F32)]
-    return call(own_kernel, shapes, scratch, 4_000_000, 8, own, wide)[0]
-
-
-def grid_kernel(modes, point, wide_z, out, sums, bias, lines, wide):
+def own_modes(field, wide):
+    shapes = (
+        jax.ShapeDtypeStruct((2 * SLAB, LANES), BF16),
+        jax.ShapeDtypeStruct((LANES, CELLS // 4), BF16),
+    )
+    scratch = [
+        pltpu.VMEM((OWN * HALF, LANES), BF16),
+        pltpu.VMEM((OWN * PITCH, LANES), F32),
+        pltpu.VMEM((MZ, 2, NY // 4, LANES), F32),
+        pltpu.VMEM((256, 640), BF16),
+        pltpu.SemaphoreType.DMA((2,)),
+    ]
+    return call(own_kernel, shapes, scratch, 4_000_000, OWN_ROOM, field, wide, anywhere=(0, 1))
+
+
+def grid_kernel(modes, point, wide_z, out, sums, bias, lines, wide, spread):
     wide[...] = modes[...].astype(F32)
     for kz in range(MZ):
         both = mm(own_to_y(wide_z), modes[kz * 32 : kz * 32 + 32, :])
@@ -341,7 +371,14 @@
         for quarter in range(4):
             cells = pl.ds(quarter * 1024 + group * 512, 512)
             here = both[quarter * 32 : quarter * 32 + 32] + point[:, cells]
-            out[:, cells] = here.astype(BF16)
+            for plane in range(PLANES):
+                for tile in range(4):
+                    first = (quarter * 8 + group * 4 + tile) * 2 + plane
+                    spread[pl.ds(first, OWN, stride=PITCH), :] = here[
+                        plane * OWN : (plane + 1) * OWN, tile * LANES : (tile + 1) * LANES
+                    ]
+    for i in range(OWN):
+        out[i * HALF : (i + 1) * HALF, :] = spread[i * PITCH : i * PITCH + HALF, :].astype(BF16)
     words = wide[pl.ds(2, OWN, stride=BACK * SHARE), :]
     sums[...] = (words + swap(words))[:, :HALF]
     words = wide[pl.ds(BACK * SHARE * OWN + 2, 8, stride=1), :]
@@ -350,11 +387,15 @@
 
 def own_grid(modes, point, wide):
     shapes = (
-        jax.ShapeDtypeStruct((2 * OWN, CELLS), BF16),
+        jax.ShapeDtypeStruct((OWN * HALF, LANES), BF16),
         jax.ShapeDtypeStruct((OWN, C), F32),
         jax.ShapeDtypeStruct((1, C), F32),
     )
-    scratch = [pltpu.VMEM((MZ, 2, NY // 4, LANES), F32), pltpu.VMEM((SLAB * BACK, LANES), F32)]
+    scratch = [
+        pltpu.VMEM((MZ, 2, NY // 4, LANES), F32),
+        pltpu.VMEM((SLAB * BACK, LANES), F32),
+        pltpu.VMEM((OWN * PITCH, LANES), F32),
+    ]
     return call(grid_kernel, shapes, scratch, 8_000_000, 8, modes, point, wide)
 
 
@@ -527,14 +568,12 @@
 
 def body(field, cotangent, spectral_weight, point_weight, point_bias):
     chan_start = lax.axis_index("chan") * OWN
-    own = lax.dynamic_slice_in_dim(field, chan_start, OWN, 0)
-    own = jnp.transpose(own.reshape(OWN, PLANES, 4, CELLS // 4), (2, 1, 0, 3))
-    own = own.reshape(LANES, CELLS // 4)
     own_rows = lax.dynamic_slice_in_dim(point_weight, chan_start, OWN, 0)
     weight = jnp.transpose(spectral_weight, (0, 1, 3, 4, 2)).reshape(2, OWN, LOW * MX, C)
-    tables = table(PACKED)
+    tables = table(PENCIL)
     wide = table(WIDE)
-    first = own_modes(own, wide)
+    rows = jnp.transpose(field.reshape(C, PLANES, 32, LANES), (0, 2, 1, 3)).reshape(CELLS, LANES)
+    first, own = own_modes(rows, wide)
     field, cotangent, first = lax.optimization_barrier((field, cotangent, first))
     pencils = over(first.reshape(SLAB, PLANES, LANES), "slab").reshape(NX, LANES)
 
@@ -542,11 +581,12 @@
     cot = jnp.transpose(cotangent, (2, 1, 0)).reshape(CELLS, LANES)
     bias = jnp.tile(point_bias.astype(F32), 2)[None]
     base = mm(cells, paired(point_weight)) + bias
+    pencils, base, cot = lax.optimization_barrier((pencils, base, cot))
     coeff, parts = mix(pencils, weight, tables)
     parts = over(parts, "chan")
     planes = spread_planes(parts, tables)
     modes = over(planes.reshape(SLAB, 8, LANES), "slab").reshape(SLAB * 8, LANES)
-    grad, rows = middle(modes, base, cot, own, wide, tables)
+    grad, rows = middle(modes, base, cot, own, wide, table(PACKED))
     arrived = over(rows.reshape(SLAB * CHUNK // 2, 2, LANES), "slab").reshape(SLAB * CHUNK, LANES)
     point_back = mm(paired(own_rows), grad.T)
     kz_weight = jnp.where(lax.axis_index("slab") < HIGH, 1.0, 2.0) / (NX * NY * NZ)
@@ -556,7 +596,8 @@
     outer_part = outer(coeff, hat).reshape(2, OWN, LOW, MX, C)
     grad_spectral = jnp.transpose(outer_part, (0, 1, 4, 2, 3))
     planes, grad_pointwise, grad_bias = own_grid(final, point_back, wide)
-    grad_input = jnp.transpose(planes.reshape(PLANES, OWN, CELLS), (1, 0, 2))
+    grad_input = jnp.transpose(planes.reshape(OWN, 32, PLANES, LANES), (0, 2, 1, 3))
+    grad_input = grad_input.reshape(OWN, PLANES, CELLS)
     return grad_input, grad_spectral, grad_pointwise, grad_bias[0]
 
 

time: 119 us -> 117 us (0.983)
  blocking collectives: 38.3 us -> 8.63 us
  starting transfers between devices: 20.2 us -> 37.9 us
  waiting for transfers between devices: 33.4 us -> 48 us
  local copies, waits for them, and re-layouts: 10.5 us -> 3.84 us
  Pallas kernels: 13.2 us -> 15.3 us
    all_to_all x2 -> x1, blocking collectives: 38.3 us -> 8.63 us  [over(): return lax.all_to_all(values, axis, split_axis=0, concat_axis=0, tiled=True)]
    all_to_all x3 -> x4, starting transfers between devices: 20.2 us -> 37.9 us  [over(): return lax.all_to_all(values, axis, split_axis=0, concat_axis=0, tiled=True)]
    all_to_all x3 -> x4, waiting for transfers between devices: 33.4 us -> 48 us  [over(): return lax.all_to_all(values, axis, split_axis=0, concat_axis=0, tiled=True)]
    reshape x3 -> x0, local copies, waits for them, and re-layouts: 3.41 us -> none  [the longest x1 2.27 us: body(): cot = jnp.transpose(cotangent, (2, 1, 0)).reshape(CELLS, LANES)]
    optimization_barrier x2, local copies, waits for them, and re-layouts: 4.6 us -> 2.39 us  [body(): lax.optimization_barrier((field, cotangent, first))]
    pallas_call x7, Pallas kernels: 13.2 us -> 15.3 us  [call(): pl.pallas_call(kernel, out_shape=shapes, in_specs=places(len(operands), a...]
    optimization_barrier x0 -> x1, local copies, waits for them, and re-layouts: none -> 1.31 us  [body(): pencils, base, cot = lax.optimization_barrier((pencils, base, cot))]
    dynamic_slice x1 -> x0, local copies, waits for them, and re-layouts: 1.24 us -> none  [body(): own = lax.dynamic_slice_in_dim(field, chan_start, OWN, 0)]
  transfers between devices with their start and end apart: 3 -> 4, of which waited for: 3 -> 4; matrix products, arithmetic and copies ran while one was open for 8% -> 5% of each run, Pallas kernels for 2% -> 2%
where the time goes in v4:
time: 117 us
  waiting for transfers between devices  48 us (41%)
  starting transfers between devices  37.9 us (32%)
  Pallas kernels  15.3 us (13%)
  blocking collectives  8.63 us (7%)
  local copies, waits for them, and re-layouts  3.84 us (3%)
  matrix products  2.26 us (2%)
    all_to_all x4, waiting for transfers between devices, over(): return lax.all_to_all(values, axis, split_axis=0, concat_axis=0, tiled=True)  48 us
    all_to_all x4, starting transfers between devices, over(): return lax.all_to_all(values, axis, split_axis=0, concat_axis=0, tiled=True)  37.9 us
    pallas_call x7, Pallas kernels, call(): pl.pallas_call(kernel, out_shape=shapes, in_specs=places(len(operands), a...  15.3 us
    all_to_all x1, blocking collectives, over(): return lax.all_to_all(values, axis, split_axis=0, concat_axis=0, tiled=True)  8.63 us
    optimization_barrier x2, local copies, waits for them, and re-layouts, body(): lax.optimization_barrier((field, cotangent, first))  2.39 us
  transfers between devices with their start and end apart: 4, of which 4 were waited for; matrix products, arithmetic and copies ran while one was open for 5% of the time, Pallas kernels for 2%

profile of v4, /device:TPU:1, one launch (start us, length us, event | category | flops | bytes accessed | tf_op | source)
XLA Modules:
  0.0 116.7 jit_solution(12063674397271339347)
XLA Ops:
  0.6 0.0 copy-start.6
  0.6 0.0 copy-start.9
  0.7 0.0 copy-start.8
  0.7 2.5 %shard_map.120 = (bf16[256,128]{1,0:T(8,128)(2,1)}, bf16[128,1024]{1,0:T(8,128)(2,1)}) custom-call(bf16[4096,128]{1,0:T(8,128)(2,1)} %bitcast.39, bf16[256,640]{1,0:T(8,128)(2,1)} %constant.50.wides.wide.wide_z), custom_call_target="tpu_custom_call" | custom-call | flops 4000000 | bytes 1703936 | tf_op jit(solution)/shard_map/pallas_call | solution.py:270
  3.1 18.4 %all-to-all-start = ((bf16[128,2,128]{2,1,0:T(2,128)(2,1)}), bf16[128,2,128]{2,1,0:T(2,128)(2,1)S(1)}, u32[]{:S(2)}, u32[]{:S(2)}) async-start(bf16[128,2,128]{2,1,0:T(2,128)(2,1)} %bitcast.43), calls=%async_computation | async-start | bytes 131072 | tf_op jit(solution)/shard_map/all_to_all | solution.py:559
  21.6 0.0 copy-done.6
  21.6 0.6 copy.17
  22.2 0.0 copy-done.9
  22.2 0.1 add.21
  22.3 0.0 copy-done.8
  22.3 0.0 copy-start
  22.3 0.0 copy-start.2
  22.3 1.8 %convolution_add_fusion.bases = f32[4096,128]{1,0:T(8,128)} fusion(bf16[4096,128]{0,1:T(8,128)(2,1)S(1)} %bitcast.41, f32[128]{0:T(128)S(1)} %add.21, bf16[64,64]{1,0:T(8,128)(2,1)S(1)} %copy-done.8), kind=kOutput, calls=%fused_computation | convolution fusion | flops 134873088 | bytes 3154432 | tf_op jit(solution)/shard_map/dot_general | solution.py:133
  24.1 1.8 %copy.18 = bf16[64,2,4096]{2,0,1:T(8,128)(2,1)S(1)} copy(bf16[64,2,4096]{2,1,0:T(2,128)(2,1)} %param.10) | data formatting | bytes 2097152 | tf_op jit(solution)/shard_map/optimization_barrier | solution.py:577
  25.9 7.1 %all-to-all-done = bf16[128,2,128]{2,1,0:T(2,128)(2,1)S(1)} async-done(((bf16[128,2,128]{2,1,0:T(2,128)(2,1)}), bf16[128,2,128]{2,1,0:T(2,128)(2,1)S(1)}, u32[]{:S(2)}, u32[]{:S(2)}) %all-to-all-start) | async-done | bytes 65568 | tf_op jit(solution)/shard_map/all_to_all | solution.py:559
  33.0 0.0 copy-done
  33.0 0.0 copy-done.2
  33.0 0.0 copy-start.1
  33.0 0.0 copy-start.3
  33.1 0.0 copy-start.4
  33.1 0.0 copy-start.5
  33.1 1.0 shard_map.121
  34.0 8.6 %all_to_all.25.parts = bf16[4,128,128]{2,1,0:T(8,128)(2,1)S(1)} all-to-all(bf16[4,128,128]{2,1,0:T(8,128)(2,1)S(1)} %get-tuple-element.26), channel_id=1, replica_groups=mesh['slab'=128,'chan'=4] {'chan'}, dimensions={0} | all-to-all | bytes 262144 | tf_op jit(solution)/shard_map/all_to_all | solution.py:559
  42.7 1.0 shard_map.122
  43.7 8.1 %all-to-all-start.2 = ((bf16[128,8,128]{2,1,0:T(8,128)(2,1)}), bf16[128,8,128]{2,1,0:T(8,128)(2,1)S(1)}, u32[]{:S(2)}, u32[]{:S(2)}) async-start(bf16[128,8,128]{2,1,0:T(8,128)(2,1)} %bitcast.11), calls=%async_computation.2 | async-start | bytes 524288 | tf_op jit(solution)/shard_map/all_to_all | solution.py:559
  51.8 1.3 %copy.19.cots = bf16[4096,128]{1,0:T(8,128)(2,1)} copy(bf16[4096,128]{0,1:T(8,128)(2,1)S(1)} %bitcast.40) | data formatting | bytes 2097152 | tf_op jit(solution)/shard_map/optimization_barrier | solution.py:584
  53.1 13.9 %all-to-all-done.2 = bf16[128,8,128]{2,1,0:T(8,128)(2,1)S(1)} async-done(((bf16[128,8,128]{2,1,0:T(8,128)(2,1)}), bf16[128,8,128]{2,1,0:T(8,128)(2,1)S(1)}, u32[]{:S(2)}, u32[]{:S(2)}) %all-to-all-start.2) | async-done | bytes 262176 | tf_op jit(solution)/shard_map/all_to_all | solution.py:559
  67.0 0.0 copy-done.1
  67.0 0.0 copy-done.3
  67.0 0.0 copy-done.4
  67.0 0.0 copy-done.5
  67.0 5.4 %shard_map.123 = (bf16[4096,128]{1,0:T(8,128)(2,1)}, bf16[1280,128]{1,0:T(8,128)(2,1)}) custom-call(bf16[1024,128]{1,0:T(8,128)(2,1)S(1)} %bitcast.36, f32[4096,128]{1,0:T(8,128)} %convolution_add_fusion.bases, bf16[4096,128]{1,0:T(8,128)(2,1)} %copy.19.cots, bf16[128,1024]{1,0:T(8,128)(2,1)S(1)} %copy-done.4, bf16[256,640]{1,0:T(8,128)(2,1)S(1)} %copy-done.1, ...), custom_call_target="tpu_custom_call" | custom-call | flops 400000000 | bytes 5722112 | tf_op jit(solution)/shard_map/pallas_call | solution.py:270
  72.4 0.0 copy-start.7
  72.4 5.7 %all-to-all-start.3 = ((bf16[640,2,128]{2,1,0:T(2,128)(2,1)}), bf16[640,2,128]{2,1,0:T(2,128)(2,1)S(1)}, u32[]{:S(2)}, u32[]{:S(2)}) async-start(bf16[640,2,128]{2,1,0:T(2,128)(2,1)} %bitcast.13), calls=%async_computation.3 | async-start | bytes 655360 | tf_op jit(solution)/shard_map/all_to_all | solution.py:559
  78.1 16.6 %all-to-all-done.3 = bf16[640,2,128]{2,1,0:T(2,128)(2,1)S(1)} async-done(((bf16[640,2,128]{2,1,0:T(2,128)(2,1)}), bf16[640,2,128]{2,1,0:T(2,128)(2,1)S(1)}, u32[]{:S(2)}, u32[]{:S(2)}) %all-to-all-start.3) | async-done | bytes 327712 | tf_op jit(solution)/shard_map/all_to_all | solution.py:559
  94.7 2.0 %shard_map.124 = (f32[2,128,64]{2,1,0:T(8,128)S(1)}, bf16[512,128]{1,0:T(8,128)(2,1)}) custom-call(bf16[1280,128]{1,0:T(8,128)(2,1)S(1)} %bitcast.35, bf16[2,16,128,64]{3,2,1,0:T(8,128)(2,1)S(1)} %bitcast.34, bf16[256,128]{1,0:T(8,128)(2,1)S(1)} %copy-done.2, f32[8,128]{1,0:T(8,128)S(1)} %broadcast_in_dim.2.scale), custom_call_target="tpu_custom_call" | custom-call | flops 40000000 | bytes 1118208 | tf_op jit(solution)/shard_map/pallas_call | solution.py:270
  96.7 5.7 %all-to-all-start.4 = ((bf16[128,4,128]{2,1,0:T(4,128)(2,1)}), bf16[128,4,128]{2,1,0:T(4,128)(2,1)S(1)}, u32[]{:S(2)}, u32[]{:S(2)}) async-start(bf16[128,4,128]{2,1,0:T(4,128)(2,1)} %bitcast.15), calls=%async_computation.4 | async-start | bytes 262144 | tf_op jit(solution)/shard_map/all_to_all | solution.py:559
  102.4 0.0 copy-done.7
  102.4 0.4 fusion.12.point
  102.9 2.0 %shard_map.126 = f32[2,16,128,64]{3,2,1,0:T(8,128)} custom-call(f32[2,32,128]{2,1,0:T(8,128)S(1)} %get-tuple-element.34.coeff, f32[2,128,64]{2,1,0:T(8,128)S(1)} %get-tuple-element.35.hat), custom_call_target="tpu_custom_call" | custom-call | flops 8000000 | bytes 1146880 | tf_op jit(solution)/shard_map/pallas_call | solution.py:270
  104.9 10.3 %all-to-all-done.4 = bf16[128,4,128]{2,1,0:T(4,128)(2,1)S(1)} async-done(((bf16[128,4,128]{2,1,0:T(4,128)(2,1)}), bf16[128,4,128]{2,1,0:T(4,128)(2,1)S(1)}, u32[]{:S(2)}, u32[]{:S(2)}) %all-to-all-start.4) | async-done | bytes 131104 | tf_op jit(solution)/shard_map/all_to_all | solution.py:559
  115.2 1.5 %shard_map.125 = (bf16[1024,128]{1,0:T(8,128)(2,1)}, f32[16,64]{1,0:T(8,128)}, f32[1,64]{1,0:T(1,128)}) custom-call(bf16[512,128]{1,0:T(8,128)(2,1)S(1)} %bitcast.37, f32[32,4096]{1,0:T(8,128)S(1)} %fusion.12.point, bf16[256,640]{1,0:T(8,128)(2,1)S(1)} %copy-done.1), custom_call_target="tpu_custom_call" | custom-call | flops 8000000 | bytes 1249536 | tf_op jit(solution)/shard_map/pallas_call | solution.py:270
  (3 shorter events, 0.0 us)
Async XLA Ops:
  0.6 20.9 %copy-start.6 = (bf16[64,2,4096]{2,1,0:T(2,128)(2,1)S(1)}, bf16[64,2,4096]{2,1,0:T(2,128)(2,1)}, u32[]{:S(2)}) copy-start(bf16[64,2,4096]{2,1,0:T(2,128)(2,1)} %param.9) | copy-start | bytes 3145732
  0.6 21.5 %copy-start.9 = (bf16[64]{0:T(256)(128)(2,1)S(1)}, bf16[64]{0:T(256)(128)(2,1)}, u32[]{:S(2)}) copy-start(bf16[64]{0:T(256)(128)(2,1)} %param.13) | copy-start | bytes 388
  0.7 21.6 %copy-start.8 = (bf16[64,64]{1,0:T(8,128)(2,1)S(1)}, bf16[64,64]{1,0:T(8,128)(2,1)}, u32[]{:S(2)}) copy-start(bf16[64,64]{1,0:T(8,128)(2,1)} %param.12) | copy-start | bytes 24580
  3.1 29.9 %all-to-all-start = ((bf16[128,2,128]{2,1,0:T(2,128)(2,1)}), bf16[128,2,128]{2,1,0:T(2,128)(2,1)S(1)}, u32[]{:S(2)}, u32[]{:S(2)}) async-start(bf16[128,2,128]{2,1,0:T(2,128)(2,1)} %bitcast.43), calls=%async_computation | async-start | bytes 131072 | tf_op jit(solution)/shard_map/all_to_all | solution.py:559
  22.3 10.8 %copy-start = (bf16[2,16,64,4,32]{2,4,3,1,0:T(8,128)(2,1)S(1)}, bf16[2,16,64,4,32]{2,4,3,1,0:T(8,128)(2,1)}, u32[]{:S(2)}) copy-start(bf16[2,16,64,4,32]{2,4,3,1,0:T(8,128)(2,1)} %param.11) | copy-start | bytes 1572868
  22.3 10.8 %copy-start.2 = (bf16[256,128]{1,0:T(8,128)(2,1)S(1)}, bf16[256,128]{1,0:T(8,128)(2,1)}, u32[]{:S(2)}) copy-start(bf16[256,128]{1,0:T(8,128)(2,1)} %constant.51.tables) | copy-start | bytes 196612
  33.0 34.0 %copy-start.1 = (bf16[256,640]{1,0:T(8,128)(2,1)S(1)}, bf16[256,640]{1,0:T(8,128)(2,1)}, u32[]{:S(2)}) copy-start(bf16[256,640]{1,0:T(8,128)(2,1)} %constant.50.wides.wide.wide_z) | copy-start | bytes 983044
  33.0 34.0 %copy-start.3 = (bf16[512,256]{1,0:T(8,128)(2,1)S(1)}, bf16[512,256]{1,0:T(8,128)(2,1)}, u32[]{:S(2)}) copy-start(bf16[512,256]{1,0:T(8,128)(2,1)} %constant.52.tall) | copy-start | bytes 786436
  33.1 33.9 %copy-start.4 = (bf16[128,1024]{1,0:T(8,128)(2,1)S(1)}, bf16[128,1024]{1,0:T(8,128)(2,1)}, u32[]{:S(2)}) copy-start(bf16[128,1024]{1,0:T(8,128)(2,1)} %get-tuple-element.29.own) | copy-start | bytes 786436
  33.1 33.9 %copy-start.5 = (bf16[336,128]{1,0:T(8,128)(2,1)S(1)}, bf16[336,128]{1,0:T(8,128)(2,1)}, u32[]{:S(2)}) copy-start(bf16[336,128]{1,0:T(8,128)(2,1)} %constant.53.tables) | copy-start | bytes 258052
  43.7 23.3 %all-to-all-start.2 = ((bf16[128,8,128]{2,1,0:T(8,128)(2,1)}), bf16[128,8,128]{2,1,0:T(8,128)(2,1)S(1)}, u32[]{:S(2)}, u32[]{:S(2)}) async-start(bf16[128,8,128]{2,1,0:T(8,128)(2,1)} %bitcast.11), calls=%async_computation.2 | async-start | bytes 524288 | tf_op jit(solution)/shard_map/all_to_all | solution.py:559
  72.4 30.0 %copy-start.7 = (bf16[4096,128]{1,0:T(8,128)(2,1)S(1)}, bf16[4096,128]{1,0:T(8,128)(2,1)}, u32[]{:S(2)}) copy-start(bf16[4096,128]{1,0:T(8,128)(2,1)} %get-tuple-element.32) | copy-start | bytes 3145732
  72.4 22.3 %all-to-all-start.3 = ((bf16[640,2,128]{2,1,0:T(2,128)(2,1)}), bf16[640,2,128]{2,1,0:T(2,128)(2,1)S(1)}, u32[]{:S(2)}, u32[]{:S(2)}) async-start(bf16[640,2,128]{2,1,0:T(2,128)(2,1)} %bitcast.13), calls=%async_computation.3 | async-start | bytes 655360 | tf_op jit(solution)/shard_map/all_to_all | solution.py:559
  96.7 18.5 %all-to-all-start.4 = ((bf16[128,4,128]{2,1,0:T(4,128)(2,1)}), bf16[128,4,128]{2,1,0:T(4,128)(2,1)S(1)}, u32[]{:S(2)}, u32[]{:S(2)}) async-start(bf16[128,4,128]{2,1,0:T(4,128)(2,1)} %bitcast.15), calls=%async_computation.4 | async-start | bytes 262144 | tf_op jit(solution)/shard_map/all_to_all | solution.py:559

commit v5 on v4

--- a/solution.py
+++ b/solution.py
@@ -172,10 +172,10 @@
     return lax.broadcasted_iota(jnp.int32, shape, 1)
 
 
-def gelu_grad(pre_act):
-    normal_cdf = 0.5 + 0.5 * lax.erf(pre_act * (1.0 / math.sqrt(2.0)))
+def twice_gelu_grad(pre_act):
     bell = jnp.exp2(pre_act * pre_act * (-0.5 * math.log2(math.e)))
-    return normal_cdf + (pre_act * (1.0 / math.sqrt(2.0 * math.pi))) * bell
+    bell = (pre_act * math.sqrt(2.0 / math.pi)) * bell
+    return (1.0 + lax.erf(pre_act * (1.0 / math.sqrt(2.0)))) + bell
 
 
 def two_words(values):
@@ -186,11 +186,11 @@
 
 def middle_kernel(
     modes, bases, cots, own, wide, tall, tables, grad_out, out,
-    up, flat, down, rows, grad, packed, base, cot, sem
+    up, flat, down, rows, grad, base, cot, sem
 ):
     pairs = ((bases, base), (cots, cot))
     loads = [
-        pltpu.make_async_copy(source, target, sem.at[index + 3])
+        pltpu.make_async_copy(source, target, sem.at[index + 1])
         for index, (source, target) in enumerate(pairs)
     ]
     for load in loads:
@@ -217,7 +217,7 @@
     @pl.loop(0, CELLS // 64, unroll=4)
     def _(block):
         here = pl.ds(pl.multiple_of(block * 64, 64), 64)
-        grad[here, :] = (cot[here, :].astype(F32) * gelu_grad(flat[here, :])).astype(BF16)
+        grad[here, :] = (cot[here, :].astype(F32) * twice_gelu_grad(flat[here, :])).astype(BF16)
 
     save = pltpu.make_async_copy(grad, grad_out, sem.at[0])
     save.start()
@@ -239,7 +239,6 @@
     words = two_words(jnp.concatenate([lower, bias, jnp.zeros_like(bias)], 0)).astype(BF16)
 
     flat[:SLAB, :] = mm(get(tables, "pick"), words)
-    sends = []
     half_rows = SLAB * CHUNK // 2
     for half in range(2):
 
@@ -253,11 +252,8 @@
         rows[pl.ds(half * half_rows + 8, SLAB // 2, stride=CHUNK), :] = flat[
             half * SLAB // 2 : (half + 1) * SLAB // 2, :
         ]
-        packed[here, :] = rows[here, :].astype(BF16)
-        sends.append(pltpu.make_async_copy(packed.at[here, :], out.at[here, :], sem.at[half + 1]))
-        sends[half].start()
-    for send in sends + [save]:
-        send.wait()
+        out[here, :] = rows[here, :].astype(BF16)
+    save.wait()
 
 
 def places(count, anywhere):
@@ -289,15 +285,14 @@
         pltpu.VMEM((2 * MZ, NY, LANES), F32),
         pltpu.VMEM((SLAB * CHUNK, LANES), F32),
         pltpu.VMEM((CELLS, LANES), BF16),
-        pltpu.VMEM((SLAB * CHUNK, LANES), BF16),
         pltpu.VMEM((CELLS, LANES), F32),
         pltpu.VMEM((CELLS, LANES), BF16),
-        pltpu.SemaphoreType.DMA((5,)),
+        pltpu.SemaphoreType.DMA((3,)),
     ]
     return call(
         middle_kernel, shapes, scratch, 400_000_000, 52,
         modes, base, cot, own, wide, table(TALL), tables,
-        anywhere=(1, 2), anywhere_out=(0, 1),
+        anywhere=(1, 2), anywhere_out=(0,),
     )
 
 
@@ -412,21 +407,21 @@
     near = near + jnp.concatenate([turn(far[:, :LANES], 112), turn(far[:, LANES:], 112)], 1)
     modes_real = (near[:MX, :LANES] + near[MX:, LANES:]).astype(BF16).astype(F32)
     modes_imag = (near[:MX, LANES:] - near[MX:, :LANES]).astype(BF16).astype(F32)
+    lane = lane_of((MX, LANES))
     coeff[0] = modes_real
     coeff[1] = modes_imag
     for m in range(LOW):
         rows = pl.ds(m * MX, MX)
-        real = jnp.zeros((MX, C), F32)
-        imag = jnp.zeros((MX, C), F32)
+        straight = jnp.zeros((MX, LANES), F32)
+        crossed = jnp.zeros((MX, LANES), F32)
         for i in range(OWN):
             at = m * 32 + i
-            left = jnp.broadcast_to(modes_real[:, at : at + 1], (MX, C))
-            right = jnp.broadcast_to(modes_imag[:, at : at + 1], (MX, C))
-            weight_real = weight[0, i, rows, :].astype(F32)
-            weight_imag = weight[1, i, rows, :].astype(F32)
-            real += left * weight_real - right * weight_imag
-            imag += left * weight_imag + right * weight_real
-        part = jnp.concatenate([real, imag], 1).astype(BF16)
+            here = weight[i, rows, :].astype(F32)
+            straight += jnp.broadcast_to(modes_real[:, at : at + 1], (MX, LANES)) * here
+            crossed += jnp.broadcast_to(modes_imag[:, at : at + 1], (MX, LANES)) * here
+        crossed = swap(crossed)
+        part = straight + jnp.where(lane < HALF, -crossed, crossed)
+        part = part.astype(BF16)
         for peer in range(4):
             out[peer, rows, :] = part
 
@@ -478,6 +473,7 @@
     near_real = jnp.zeros((MX, LANES), F32)
     near_imag = jnp.zeros((MX, LANES), F32)
     factor = scale[0:1, :]
+    both_hats = []
     for m in range(LOW):
         left = wide[pl.ds(m, SLAB, stride=CHUNK), :]
         right = wide[pl.ds(LOW + m, SLAB, stride=CHUNK), :]
@@ -486,18 +482,23 @@
         second = near[:, LANES:] + swap(far[:, LANES:])
         real = (first[:MX] + second[MX:]) * factor
         imag = (second[:MX] - first[MX:]) * factor
-        hat[0, pl.ds(m * MX, MX), :] = real.astype(BF16).astype(F32)[:, :C]
-        hat[1, pl.ds(m * MX, MX), :] = imag.astype(BF16).astype(F32)[:, :C]
+        real = real.astype(BF16).astype(F32)
+        imag = imag.astype(BF16).astype(F32)
+        hat[0, pl.ds(m * MX, MX), :] = real[:, :C]
+        hat[1, pl.ds(m * MX, MX), :] = imag[:, :C]
+        both_hats.append(
+            (
+                jnp.where(lane < HALF, real, swap(imag)),
+                jnp.where(lane < HALF, imag, -swap(real)),
+            )
+        )
     load.wait()
     for m in range(LOW):
-        at_m = pl.ds(m * MX, MX)
-        real = hat[0, at_m, :]
-        imag = hat[1, at_m, :]
+        straight, crossed = both_hats[m]
         for i in range(OWN):
-            weight_real = weight[0, i, at_m, :].astype(F32)
-            weight_imag = weight[1, i, at_m, :].astype(F32)
-            sum_real = jnp.sum(real * weight_real + imag * weight_imag, 1, keepdims=True)
-            sum_imag = jnp.sum(imag * weight_real - real * weight_imag, 1, keepdims=True)
+            here = weight[i, pl.ds(m * MX, MX), :].astype(F32)
+            sum_real = jnp.sum(straight * here, 1, keepdims=True)
+            sum_imag = jnp.sum(crossed * here, 1, keepdims=True)
             near_real = jnp.where(lane == m * 32 + i, sum_real, near_real)
             near_imag = jnp.where(lane == m * 32 + i, sum_imag, near_imag)
     far_real = turn(near_real, 16)
@@ -527,7 +528,7 @@
     scratch = [
         pltpu.VMEM((SLAB * CHUNK, LANES), F32),
         pltpu.VMEM((SLAB * BACK, LANES), F32),
-        pltpu.VMEM((2, OWN, LOW * MX, C), BF16),
+        pltpu.VMEM((OWN, LOW * MX, LANES), BF16),
         pltpu.SemaphoreType.DMA,
     ]
     return call(
@@ -570,27 +571,34 @@
     chan_start = lax.axis_index("chan") * OWN
     own_rows = lax.dynamic_slice_in_dim(point_weight, chan_start, OWN, 0)
     weight = jnp.transpose(spectral_weight, (0, 1, 3, 4, 2)).reshape(2, OWN, LOW * MX, C)
+    own_rows_of = paired(own_rows)
     tables = table(PENCIL)
     wide = table(WIDE)
     rows = jnp.transpose(field.reshape(C, PLANES, 32, LANES), (0, 2, 1, 3)).reshape(CELLS, LANES)
     first, own = own_modes(rows, wide)
-    field, cotangent, first = lax.optimization_barrier((field, cotangent, first))
+    field, cotangent, weight, first = lax.optimization_barrier(
+        (field, cotangent, weight, first)
+    )
     pencils = over(first.reshape(SLAB, PLANES, LANES), "slab").reshape(NX, LANES)
 
     cells = jnp.transpose(field, (2, 1, 0)).reshape(CELLS, LANES)
     cot = jnp.transpose(cotangent, (2, 1, 0)).reshape(CELLS, LANES)
+    cot = mm(cot, 0.5 * jnp.eye(LANES, dtype=BF16)).astype(BF16)
+    weight = jnp.concatenate([weight[0], weight[1]], -1)
     bias = jnp.tile(point_bias.astype(F32), 2)[None]
     base = mm(cells, paired(point_weight)) + bias
-    pencils, base, cot = lax.optimization_barrier((pencils, base, cot))
+    kz_weight = jnp.where(lax.axis_index("slab") < HIGH, 1.0, 2.0) / (NX * NY * NZ)
+    scale = jnp.full((8, LANES), kz_weight, F32)
+    pencils, base, cot, weight, own_rows_of, scale = lax.optimization_barrier(
+        (pencils, base, cot, weight, own_rows_of, scale)
+    )
     coeff, parts = mix(pencils, weight, tables)
     parts = over(parts, "chan")
     planes = spread_planes(parts, tables)
     modes = over(planes.reshape(SLAB, 8, LANES), "slab").reshape(SLAB * 8, LANES)
     grad, rows = middle(modes, base, cot, own, wide, table(PACKED))
     arrived = over(rows.reshape(SLAB * CHUNK // 2, 2, LANES), "slab").reshape(SLAB * CHUNK, LANES)
-    point_back = mm(paired(own_rows), grad.T)
-    kz_weight = jnp.where(lax.axis_index("slab") < HIGH, 1.0, 2.0) / (NX * NY * NZ)
-    scale = jnp.full((8, LANES), kz_weight, F32)
+    point_back = mm(own_rows_of, grad.T)
     hat, rows = adjoint_planes(arrived, weight, tables, scale)
     final = over(rows.reshape(SLAB, BACK, LANES), "slab").reshape(SLAB * BACK, LANES)
     outer_part = outer(coeff, hat).reshape(2, OWN, LOW, MX, C)

time: 117 us -> 118 us (level)
  blocking collectives: 8.63 us -> 57.3 us
  waiting for transfers between devices: 48 us -> 13.6 us
  starting transfers between devices: 37.9 us -> 24 us
  Pallas kernels: 15.3 us -> 13.8 us
  other arithmetic: 0 us -> 1.48 us
  matrix products: 2.26 us -> 3.72 us
    all_to_all x1 -> x3, blocking collectives: 8.63 us -> 57.3 us  [over(): return lax.all_to_all(values, axis, split_axis=0, concat_axis=0, tiled=True)]
    all_to_all x4 -> x2, waiting for transfers between devices: 48 us -> 13.6 us  [over(): return lax.all_to_all(values, axis, split_axis=0, concat_axis=0, tiled=True)]
    all_to_all x4 -> x2, starting transfers between devices: 37.9 us -> 24 us  [over(): return lax.all_to_all(values, axis, split_axis=0, concat_axis=0, tiled=True)]
    optimization_barrier x3 -> x2, local copies, waits for them, and re-layouts: 3.7 us -> 1.16 us  [body(): lax.optimization_barrier((field, cotangent, weight, first))]
    pallas_call x7, Pallas kernels: 15.3 us -> 13.8 us  [call(): pl.pallas_call(kernel, out_shape=shapes, in_specs=places(len(operands), a...]
    concatenate x0 -> x2, other arithmetic: none -> 1.48 us  [the longest x1 1.4 us: body(): weight = jnp.concatenate([weight[0], weight[1]], -1)]
    dot_general x2 -> x3, matrix products: 2.26 us -> 3.72 us  [mm(): return jnp.dot(left, right, preferred_element_type=F32)]
  transfers between devices with their start and end apart: 4 -> 2, of which waited for: 4 -> 2; matrix products, arithmetic and copies ran while one was open for 5% -> 7% of each run, Pallas kernels for 2% -> 2%
where the time goes in v5:
time: 118 us
  blocking collectives  57.3 us (49%)
  starting transfers between devices  24 us (20%)
  Pallas kernels  13.8 us (12%)
  waiting for transfers between devices  13.6 us (12%)
  matrix products  3.72 us (3%)
  local copies, waits for them, and re-layouts  3.47 us (3%)
  other arithmetic  1.48 us (1%)
    all_to_all x3, blocking collectives, over(): return lax.all_to_all(values, axis, split_axis=0, concat_axis=0, tiled=True)  57.3 us
    all_to_all x2, starting transfers between devices, over(): return lax.all_to_all(values, axis, split_axis=0, concat_axis=0, tiled=True)  24 us
    pallas_call x7, Pallas kernels, call(): pl.pallas_call(kernel, out_shape=shapes, in_specs=places(len(operands), a...  13.8 us
    all_to_all x2, waiting for transfers between devices, over(): return lax.all_to_all(values, axis, split_axis=0, concat_axis=0, tiled=True)  13.6 us
    dot_general x3, matrix products, mm(): return jnp.dot(left, right, preferred_element_type=F32)  3.72 us
  transfers between devices with their start and end apart: 2, of which 2 were waited for; matrix products, arithmetic and copies ran while one was open for 7% of the time, Pallas kernels for 2%

profile of v5, /device:TPU:1, one launch (start us, length us, event | category | flops | bytes accessed | tf_op | source)
XLA Modules:
  0.0 118.0 jit_solution(10737531585440687489)
XLA Ops:
  0.6 0.0 copy-start.5
  0.6 2.5 %shard_map.120 = (bf16[256,128]{1,0:T(8,128)(2,1)}, bf16[128,1024]{1,0:T(8,128)(2,1)}) custom-call(bf16[4096,128]{1,0:T(8,128)(2,1)} %bitcast.45, bf16[256,640]{1,0:T(8,128)(2,1)} %constant.53.wides.wide.wide_z), custom_call_target="tpu_custom_call" | custom-call | flops 4000000 | bytes 1703936 | tf_op jit(solution)/shard_map/pallas_call | solution.py:266
  3.1 18.4 %all-to-all-start = ((bf16[128,2,128]{2,1,0:T(2,128)(2,1)}), bf16[128,2,128]{2,1,0:T(2,128)(2,1)S(1)}, u32[]{:S(2)}, u32[]{:S(2)}) async-start(bf16[128,2,128]{2,1,0:T(2,128)(2,1)} %bitcast.50), calls=%async_computation | async-start | bytes 131072 | tf_op jit(solution)/shard_map/all_to_all | solution.py:560
  21.5 0.7 tile.2
  22.2 0.1 add.21
  22.3 0.0 copy-done.5
  22.3 0.0 copy-start.7
  22.3 0.6 copy.16
  22.9 0.6 copy-done.7
  23.5 0.0 copy-start.8
  23.5 0.6 copy.17
  24.1 0.0 copy-start.9
  24.1 1.4 %convolution_convert_fusion.cots = bf16[4096,128]{1,0:T(8,128)(2,1)} fusion(bf16[4096,128]{0,1:T(8,128)(2,1)S(1)} %bitcast.47), kind=kOutput, calls=%fused_computation.1 | convolution fusion | flops 134774784 | bytes 2097152 | tf_op jit(solution)/shard_map/dot_general | solution.py:133
  25.6 0.0 copy-done.8
  25.6 0.9 slice_bitcast_fusion.1
  26.5 0.0 copy-done.9
  26.5 0.0 copy-start.1
  26.5 1.8 %convolution_add_fusion.bases = f32[4096,128]{1,0:T(8,128)} fusion(bf16[4096,128]{0,1:T(8,128)(2,1)S(1)} %bitcast.46, f32[128]{0:T(128)S(1)} %add.21, bf16[64,64]{1,0:T(8,128)(2,1)S(1)} %copy-done.9), kind=kOutput, calls=%fused_computation | convolution fusion | flops 134873088 | bytes 3154432 | tf_op jit(solution)/shard_map/dot_general | solution.py:133
  28.3 0.0 copy-start
  28.3 0.0 copy-start.2
  28.3 0.0 copy-start.3
  28.3 0.0 copy-start.4
  28.3 0.1 fusion.15
  28.4 1.4 %pad_maximum_fusion.weight.weights = bf16[16,128,128]{2,1,0:T(8,128)(2,1)S(1)} fusion(bf16[16,128,64]{2,1,0:T(8,128)(2,1)} %get-tuple-element.47, bf16[16,128,64]{2,1,0:T(8,128)(2,1)S(1)} %get-tuple-element.46), kind=kLoop, calls=%fused_computation.2 | loop fusion | flops 1048576 | bytes 1048576 | tf_op jit(solution)/shard_map/concatenate | solution.py:587
  29.8 3.2 %all-to-all-done = bf16[128,2,128]{2,1,0:T(2,128)(2,1)S(1)} async-done(((bf16[128,2,128]{2,1,0:T(2,128)(2,1)}), bf16[128,2,128]{2,1,0:T(2,128)(2,1)S(1)}, u32[]{:S(2)}, u32[]{:S(2)}) %all-to-all-start) | async-done | bytes 65568 | tf_op jit(solution)/shard_map/all_to_all | solution.py:560
  33.0 0.0 copy-done.1
  33.0 0.8 shard_map.121
  33.9 8.6 %all_to_all.25.parts = bf16[4,128,128]{2,1,0:T(8,128)(2,1)S(1)} all-to-all(bf16[4,128,128]{2,1,0:T(8,128)(2,1)S(1)} %get-tuple-element.32), channel_id=1, replica_groups=mesh['slab'=128,'chan'=4] {'chan'}, dimensions={0} | all-to-all | bytes 262144 | tf_op jit(solution)/shard_map/all_to_all | solution.py:560
  42.5 0.3 shard_map.122
  42.8 27.0 %all_to_all.26 = bf16[128,8,128]{2,1,0:T(8,128)(2,1)S(1)} all-to-all(bf16[128,8,128]{2,1,0:T(8,128)(2,1)S(1)} %bitcast.41), channel_id=1, replica_groups=mesh['slab'=128,'chan'=4] {'slab'}, dimensions={0} | all-to-all | bytes 524288 | tf_op jit(solution)/shard_map/all_to_all | solution.py:560
  69.8 0.0 copy-done
  69.8 0.0 copy-done.2
  69.8 0.0 copy-done.3
  69.8 0.0 copy-done.4
  69.8 4.7 %shard_map.123 = (bf16[4096,128]{1,0:T(8,128)(2,1)}, bf16[1280,128]{1,0:T(8,128)(2,1)S(1)}) custom-call(bf16[1024,128]{1,0:T(8,128)(2,1)S(1)} %bitcast.40, f32[4096,128]{1,0:T(8,128)} %convolution_add_fusion.bases, bf16[4096,128]{1,0:T(8,128)(2,1)} %convolution_convert_fusion.cots, bf16[128,1024]{1,0:T(8,128)(2,1)S(1)} %copy-done.3, ...), custom_call_target="tpu_custom_call" | custom-call | flops 400000000 | bytes 5722112 | tf_op jit(solution)/shard_map/pallas_call | solution.py:266
  74.5 0.0 copy-start.6
  74.5 21.7 %all_to_all.27 = bf16[640,2,128]{2,1,0:T(2,128)(2,1)S(1)} all-to-all(bf16[640,2,128]{2,1,0:T(2,128)(2,1)S(1)} %bitcast.43), channel_id=1, replica_groups=mesh['slab'=128,'chan'=4] {'slab'}, dimensions={0} | all-to-all | bytes 655360 | tf_op jit(solution)/shard_map/all_to_all | solution.py:560
  96.2 2.0 %shard_map.124 = (f32[2,128,64]{2,1,0:T(8,128)S(1)}, bf16[512,128]{1,0:T(8,128)(2,1)}) custom-call(bf16[1280,128]{1,0:T(8,128)(2,1)S(1)} %bitcast.39, bf16[16,128,128]{2,1,0:T(8,128)(2,1)S(1)} %pad_maximum_fusion.weight.weights, bf16[256,128]{1,0:T(8,128)(2,1)S(1)} %copy-done.1, f32[8,128]{1,0:T(8,128)S(1)} %broadcast_in_dim.2.scale), custom_call_target="tpu_custom_call" | custom-call | flops 40000000 | bytes 1118208 | tf_op jit(solution)/shard_map/pallas_call | solution.py:266
  98.2 5.5 %all-to-all-start.4 = ((bf16[128,4,128]{2,1,0:T(4,128)(2,1)}), bf16[128,4,128]{2,1,0:T(4,128)(2,1)S(1)}, u32[]{:S(2)}, u32[]{:S(2)}) async-start(bf16[128,4,128]{2,1,0:T(4,128)(2,1)} %bitcast.17), calls=%async_computation.4 | async-start | bytes 262144 | tf_op jit(solution)/shard_map/all_to_all | solution.py:560
  103.7 0.0 copy-done.6
  103.7 0.4 fusion.21.point
  104.2 2.0 %shard_map.126 = f32[2,16,128,64]{3,2,1,0:T(8,128)} custom-call(f32[2,32,128]{2,1,0:T(8,128)S(1)} %get-tuple-element.42.coeff, f32[2,128,64]{2,1,0:T(8,128)S(1)} %get-tuple-element.43.hat), custom_call_target="tpu_custom_call" | custom-call | flops 8000000 | bytes 1146880 | tf_op jit(solution)/shard_map/pallas_call | solution.py:266
  106.2 10.3 %all-to-all-done.4 = bf16[128,4,128]{2,1,0:T(4,128)(2,1)S(1)} async-done(((bf16[128,4,128]{2,1,0:T(4,128)(2,1)}), bf16[128,4,128]{2,1,0:T(4,128)(2,1)S(1)}, u32[]{:S(2)}, u32[]{:S(2)}) %all-to-all-start.4) | async-done | bytes 131104 | tf_op jit(solution)/shard_map/all_to_all | solution.py:560
  116.5 1.5 %shard_map.125 = (bf16[1024,128]{1,0:T(8,128)(2,1)}, f32[16,64]{1,0:T(8,128)}, f32[1,64]{1,0:T(1,128)}) custom-call(bf16[512,128]{1,0:T(8,128)(2,1)S(1)} %bitcast.42, f32[32,4096]{1,0:T(8,128)S(1)} %fusion.21.point, bf16[256,640]{1,0:T(8,128)(2,1)S(1)} %copy-done), custom_call_target="tpu_custom_call" | custom-call | flops 8000000 | bytes 1249536 | tf_op jit(solution)/shard_map/pallas_call | solution.py:266
  (2 shorter events, 0.0 us)
Async XLA Ops:
  0.6 21.7 %copy-start.5 = (bf16[64,2,4096]{2,1,0:T(2,128)(2,1)S(1)}, bf16[64,2,4096]{2,1,0:T(2,128)(2,1)}, u32[]{:S(2)}) copy-start(bf16[64,2,4096]{2,1,0:T(2,128)(2,1)} %param.9) | copy-start | bytes 3145732
  3.1 29.9 %all-to-all-start = ((bf16[128,2,128]{2,1,0:T(2,128)(2,1)}), bf16[128,2,128]{2,1,0:T(2,128)(2,1)S(1)}, u32[]{:S(2)}, u32[]{:S(2)}) async-start(bf16[128,2,128]{2,1,0:T(2,128)(2,1)} %bitcast.50), calls=%async_computation | async-start | bytes 131072 | tf_op jit(solution)/shard_map/all_to_all | solution.py:560
  22.3 1.2 %copy-start.7 = (bf16[64,2,4096]{2,1,0:T(2,128)(2,1)S(1)}, bf16[64,2,4096]{2,1,0:T(2,128)(2,1)}, u32[]{:S(2)}) copy-start(bf16[64,2,4096]{2,1,0:T(2,128)(2,1)} %param.10) | copy-start | bytes 3145732
  23.5 2.1 %copy-start.8 = (bf16[2,16,64,4,32]{2,4,3,1,0:T(8,128)(2,1)S(1)}, bf16[2,16,64,4,32]{2,4,3,1,0:T(8,128)(2,1)}, u32[]{:S(2)}) copy-start(bf16[2,16,64,4,32]{2,4,3,1,0:T(8,128)(2,1)} %param.11) | copy-start | bytes 1572868
  24.1 2.4 %copy-start.9 = (bf16[64,64]{1,0:T(8,128)(2,1)S(1)}, bf16[64,64]{1,0:T(8,128)(2,1)}, u32[]{:S(2)}) copy-start(bf16[64,64]{1,0:T(8,128)(2,1)} %param.12) | copy-start | bytes 24580
  26.5 6.6 %copy-start.1 = (bf16[256,128]{1,0:T(8,128)(2,1)S(1)}, bf16[256,128]{1,0:T(8,128)(2,1)}, u32[]{:S(2)}) copy-start(bf16[256,128]{1,0:T(8,128)(2,1)} %constant.54.tables) | copy-start | bytes 196612
  28.3 41.5 %copy-start = (bf16[256,640]{1,0:T(8,128)(2,1)S(1)}, bf16[256,640]{1,0:T(8,128)(2,1)}, u32[]{:S(2)}) copy-start(bf16[256,640]{1,0:T(8,128)(2,1)} %constant.53.wides.wide.wide_z) | copy-start | bytes 983044
  28.3 41.5 %copy-start.2 = (bf16[512,256]{1,0:T(8,128)(2,1)S(1)}, bf16[512,256]{1,0:T(8,128)(2,1)}, u32[]{:S(2)}) copy-start(bf16[512,256]{1,0:T(8,128)(2,1)} %constant.55.tall) | copy-start | bytes 786436
  28.3 41.5 %copy-start.3 = (bf16[128,1024]{1,0:T(8,128)(2,1)S(1)}, bf16[128,1024]{1,0:T(8,128)(2,1)}, u32[]{:S(2)}) copy-start(bf16[128,1024]{1,0:T(8,128)(2,1)} %get-tuple-element.35.own) | copy-start | bytes 786436
  28.3 41.5 %copy-start.4 = (bf16[336,128]{1,0:T(8,128)(2,1)S(1)}, bf16[336,128]{1,0:T(8,128)(2,1)}, u32[]{:S(2)}) copy-start(bf16[336,128]{1,0:T(8,128)(2,1)} %constant.56.tables) | copy-start | bytes 258052
  74.5 29.2 %copy-start.6 = (bf16[4096,128]{1,0:T(8,128)(2,1)S(1)}, bf16[4096,128]{1,0:T(8,128)(2,1)}, u32[]{:S(2)}) copy-start(bf16[4096,128]{1,0:T(8,128)(2,1)} %get-tuple-element.40) | copy-start | bytes 3145732
  98.2 18.4 %all-to-all-start.4 = ((bf16[128,4,128]{2,1,0:T(4,128)(2,1)}), bf16[128,4,128]{2,1,0:T(4,128)(2,1)S(1)}, u32[]{:S(2)}, u32[]{:S(2)}) async-start(bf16[128,4,128]{2,1,0:T(4,128)(2,1)} %bitcast.17), calls=%async_computation.4 | async-start | bytes 262144 | tf_op jit(solution)/shard_map/all_to_all | solution.py:560

commit v6 on v4

--- a/solution.py
+++ b/solution.py
@@ -172,10 +172,10 @@
     return lax.broadcasted_iota(jnp.int32, shape, 1)
 
 
-def gelu_grad(pre_act):
-    normal_cdf = 0.5 + 0.5 * lax.erf(pre_act * (1.0 / math.sqrt(2.0)))
+def twice_gelu_grad(pre_act):
     bell = jnp.exp2(pre_act * pre_act * (-0.5 * math.log2(math.e)))
-    return normal_cdf + (pre_act * (1.0 / math.sqrt(2.0 * math.pi))) * bell
+    bell = (pre_act * math.sqrt(2.0 / math.pi)) * bell
+    return (1.0 + lax.erf(pre_act * (1.0 / math.sqrt(2.0)))) + bell
 
 
 def two_words(values):
@@ -186,11 +186,11 @@
 
 def middle_kernel(
     modes, bases, cots, own, wide, tall, tables, grad_out, out,
-    up, flat, down, rows, grad, packed, base, cot, sem
+    up, flat, down, rows, grad, base, cot, sem
 ):
     pairs = ((bases, base), (cots, cot))
     loads = [
-        pltpu.make_async_copy(source, target, sem.at[index + 3])
+        pltpu.make_async_copy(source, target, sem.at[index + 1])
         for index, (source, target) in enumerate(pairs)
     ]
     for load in loads:
@@ -217,7 +217,7 @@
     @pl.loop(0, CELLS // 64, unroll=4)
     def _(block):
         here = pl.ds(pl.multiple_of(block * 64, 64), 64)
-        grad[here, :] = (cot[here, :].astype(F32) * gelu_grad(flat[here, :])).astype(BF16)
+        grad[here, :] = (cot[here, :].astype(F32) * twice_gelu_grad(flat[here, :])).astype(BF16)
 
     save = pltpu.make_async_copy(grad, grad_out, sem.at[0])
     save.start()
@@ -239,7 +239,6 @@
     words = two_words(jnp.concatenate([lower, bias, jnp.zeros_like(bias)], 0)).astype(BF16)
 
     flat[:SLAB, :] = mm(get(tables, "pick"), words)
-    sends = []
     half_rows = SLAB * CHUNK // 2
     for half in range(2):
 
@@ -253,11 +252,8 @@
         rows[pl.ds(half * half_rows + 8, SLAB // 2, stride=CHUNK), :] = flat[
             half * SLAB // 2 : (half + 1) * SLAB // 2, :
         ]
-        packed[here, :] = rows[here, :].astype(BF16)
-        sends.append(pltpu.make_async_copy(packed.at[here, :], out.at[here, :], sem.at[half + 1]))
-        sends[half].start()
-    for send in sends + [save]:
-        send.wait()
+        out[here, :] = rows[here, :].astype(BF16)
+    save.wait()
 
 
 def places(count, anywhere):
@@ -289,15 +285,14 @@
         pltpu.VMEM((2 * MZ, NY, LANES), F32),
         pltpu.VMEM((SLAB * CHUNK, LANES), F32),
         pltpu.VMEM((CELLS, LANES), BF16),
-        pltpu.VMEM((SLAB * CHUNK, LANES), BF16),
         pltpu.VMEM((CELLS, LANES), F32),
         pltpu.VMEM((CELLS, LANES), BF16),
-        pltpu.SemaphoreType.DMA((5,)),
+        pltpu.SemaphoreType.DMA((3,)),
     ]
     return call(
         middle_kernel, shapes, scratch, 400_000_000, 52,
         modes, base, cot, own, wide, table(TALL), tables,
-        anywhere=(1, 2), anywhere_out=(0, 1),
+        anywhere=(1, 2), anywhere_out=(0,),
     )
 
 
@@ -568,31 +563,37 @@
 
 def body(field, cotangent, spectral_weight, point_weight, point_bias):
     chan_start = lax.axis_index("chan") * OWN
-    own_rows = lax.dynamic_slice_in_dim(point_weight, chan_start, OWN, 0)
+    own_rows = paired(lax.dynamic_slice_in_dim(point_weight, chan_start, OWN, 0))
     weight = jnp.transpose(spectral_weight, (0, 1, 3, 4, 2)).reshape(2, OWN, LOW * MX, C)
     tables = table(PENCIL)
     wide = table(WIDE)
     rows = jnp.transpose(field.reshape(C, PLANES, 32, LANES), (0, 2, 1, 3)).reshape(CELLS, LANES)
     first, own = own_modes(rows, wide)
-    field, cotangent, first = lax.optimization_barrier((field, cotangent, first))
     pencils = over(first.reshape(SLAB, PLANES, LANES), "slab").reshape(NX, LANES)
-
+    coeff, parts = mix(pencils, weight, tables)
+
+    field, cotangent, own_rows, parts = lax.optimization_barrier(
+        (field, cotangent, own_rows, parts)
+    )
+    kz_weight = jnp.where(lax.axis_index("slab") < HIGH, 1.0, 2.0) / (NX * NY * NZ)
+    scale = jnp.full((8, LANES), kz_weight, F32)
     cells = jnp.transpose(field, (2, 1, 0)).reshape(CELLS, LANES)
     cot = jnp.transpose(cotangent, (2, 1, 0)).reshape(CELLS, LANES)
+    cot = mm(cot, 0.5 * jnp.eye(LANES, dtype=BF16)).astype(BF16)
     bias = jnp.tile(point_bias.astype(F32), 2)[None]
     base = mm(cells, paired(point_weight)) + bias
-    pencils, base, cot = lax.optimization_barrier((pencils, base, cot))
-    coeff, parts = mix(pencils, weight, tables)
     parts = over(parts, "chan")
+    parts, base, cot, own_rows, scale = lax.optimization_barrier(
+        (parts, base, cot, own_rows, scale)
+    )
+
     planes = spread_planes(parts, tables)
     modes = over(planes.reshape(SLAB, 8, LANES), "slab").reshape(SLAB * 8, LANES)
     grad, rows = middle(modes, base, cot, own, wide, table(PACKED))
-    arrived = over(rows.reshape(SLAB * CHUNK // 2, 2, LANES), "slab").reshape(SLAB * CHUNK, LANES)
-    point_back = mm(paired(own_rows), grad.T)
-    kz_weight = jnp.where(lax.axis_index("slab") < HIGH, 1.0, 2.0) / (NX * NY * NZ)
-    scale = jnp.full((8, LANES), kz_weight, F32)
-    hat, rows = adjoint_planes(arrived, weight, tables, scale)
+    arrived = over(rows.reshape(SLAB * CHUNK // 2, 2, LANES), "slab")
+    hat, rows = adjoint_planes(arrived.reshape(SLAB * CHUNK, LANES), weight, tables, scale)
     final = over(rows.reshape(SLAB, BACK, LANES), "slab").reshape(SLAB * BACK, LANES)
+    point_back = mm(own_rows, grad.T)
     outer_part = outer(coeff, hat).reshape(2, OWN, LOW, MX, C)
     grad_spectral = jnp.transpose(outer_part, (0, 1, 4, 2, 3))
     planes, grad_pointwise, grad_bias = own_grid(final, point_back, wide)

time: 117 us -> 115 us (0.983)
  blocking collectives: 8.63 us -> 43.2 us
  waiting for transfers between devices: 48 us -> 20.2 us
  starting transfers between devices: 37.9 us -> 28.1 us
  matrix products: 2.26 us -> 3.74 us
    all_to_all x1 -> x2, blocking collectives: 8.63 us -> 43.2 us  [over(): return lax.all_to_all(values, axis, split_axis=0, concat_axis=0, tiled=True)]
    all_to_all x4 -> x3, waiting for transfers between devices: 48 us -> 20.2 us  [over(): return lax.all_to_all(values, axis, split_axis=0, concat_axis=0, tiled=True)]
    all_to_all x4 -> x3, starting transfers between devices: 37.9 us -> 28.1 us  [over(): return lax.all_to_all(values, axis, split_axis=0, concat_axis=0, tiled=True)]
    optimization_barrier x3 -> x2, local copies, waits for them, and re-layouts: 3.7 us -> 1.17 us  [body(): lax.optimization_barrier((field, cotangent, own_rows, parts))]
    dot_general x2 -> x3, matrix products: 2.26 us -> 3.74 us  [mm(): return jnp.dot(left, right, preferred_element_type=F32)]
    unnamed x20 -> x22, local copies, waits for them, and re-layouts: 0.04 us -> 1.5 us
  transfers between devices with their start and end apart: 4 -> 3, of which waited for: 4 -> 2; matrix products, arithmetic and copies ran while one was open for 5% -> 6% of each run, Pallas kernels for 2% -> 2%
where the time goes in v6:
time: 115 us
  blocking collectives  43.2 us (38%)
  starting transfers between devices  28.1 us (24%)
  waiting for transfers between devices  20.2 us (18%)
  Pallas kernels  14.5 us (13%)
  local copies, waits for them, and re-layouts  4.1 us (4%)
  matrix products  3.74 us (3%)
    all_to_all x2, blocking collectives, over(): return lax.all_to_all(values, axis, split_axis=0, concat_axis=0, tiled=True)  43.2 us
    all_to_all x3, starting transfers between devices, over(): return lax.all_to_all(values, axis, split_axis=0, concat_axis=0, tiled=True)  28.1 us
    all_to_all x3, waiting for transfers between devices, over(): return lax.all_to_all(values, axis, split_axis=0, concat_axis=0, tiled=True)  20.2 us
    pallas_call x7, Pallas kernels, call(): pl.pallas_call(kernel, out_shape=shapes, in_specs=places(len(operands), a...  14.5 us
    dot_general x3, matrix products, mm(): return jnp.dot(left, right, preferred_element_type=F32)  3.74 us
  transfers between devices with their start and end apart: 3, of which 2 were waited for; matrix products, arithmetic and copies ran while one was open for 6% of the time, Pallas kernels for 2%

profile of v6, /device:TPU:1, one launch (start us, length us, event | category | flops | bytes accessed | tf_op | source)
XLA Modules:
  0.0 114.8 jit_solution(5529565952373571289)
XLA Ops:
  0.6 0.0 copy-start
  0.6 2.5 %shard_map.120 = (bf16[256,128]{1,0:T(8,128)(2,1)}, bf16[128,1024]{1,0:T(8,128)(2,1)}) custom-call(bf16[4096,128]{1,0:T(8,128)(2,1)} %bitcast.43, bf16[256,640]{1,0:T(8,128)(2,1)} %constant.53.wides.wide.wide_z), custom_call_target="tpu_custom_call" | custom-call | flops 4000000 | bytes 1703936 | tf_op jit(solution)/shard_map/pallas_call | solution.py:266
  3.1 18.4 %all-to-all-start = ((bf16[128,2,128]{2,1,0:T(2,128)(2,1)}), bf16[128,2,128]{2,1,0:T(2,128)(2,1)S(1)}, u32[]{:S(2)}, u32[]{:S(2)}) async-start(bf16[128,2,128]{2,1,0:T(2,128)(2,1)} %bitcast.47), calls=%async_computation | async-start | bytes 131072 | tf_op jit(solution)/shard_map/all_to_all | solution.py:554
  21.6 0.7 constant_dynamic-slice_fusion
  22.2 0.7 tile.2
  22.9 0.1 add.22
  23.0 0.1 fusion.15
  23.1 9.9 %all-to-all-done = bf16[128,2,128]{2,1,0:T(2,128)(2,1)S(1)} async-done(((bf16[128,2,128]{2,1,0:T(2,128)(2,1)}), bf16[128,2,128]{2,1,0:T(2,128)(2,1)S(1)}, u32[]{:S(2)}, u32[]{:S(2)}) %all-to-all-start) | async-done | bytes 65568 | tf_op jit(solution)/shard_map/all_to_all | solution.py:554
  33.0 0.0 copy-done
  33.0 0.0 copy-start.2
  33.0 0.8 copy-done.2
  33.8 0.0 copy-start.7
  33.8 1.6 %shard_map.121 = (f32[2,32,128]{2,1,0:T(8,128)S(1)}, bf16[4,128,128]{2,1,0:T(8,128)(2,1)}) custom-call(bf16[256,128]{1,0:T(8,128)(2,1)S(1)} %bitcast.42, bf16[2,16,128,64]{3,2,1,0:T(8,128)(2,1)S(1)} %bitcast.35, bf16[256,128]{1,0:T(8,128)(2,1)S(1)} %copy-done.2), custom_call_target="tpu_custom_call" | custom-call | flops 4000000 | bytes 819200 | tf_op jit(solution)/shard_map/pallas_call | solution.py:266
  35.4 4.0 %all-to-all-start.1 = ((bf16[4,128,128]{2,1,0:T(8,128)(2,1)}), bf16[4,128,128]{2,1,0:T(8,128)(2,1)S(1)}, u32[]{:S(2)}, u32[]{:S(2)}) async-start(bf16[4,128,128]{2,1,0:T(8,128)(2,1)} %get-tuple-element.26), calls=%async_computation.1 | async-start | bytes 262144 | tf_op jit(solution)/shard_map/all_to_all | solution.py:554
  39.4 0.0 copy-done.7
  39.4 0.0 copy-start.9
  39.4 0.0 copy-start.10
  39.4 0.6 copy.16
  40.0 0.6 copy-done.9
  40.7 0.6 copy.17
  41.2 0.0 copy-done.10
  41.3 0.0 copy-start.3
  41.3 1.8 %convolution_add_fusion.bases = f32[4096,128]{1,0:T(8,128)} fusion(bf16[4096,128]{0,1:T(8,128)(2,1)S(1)} %bitcast.45, f32[128]{0:T(128)S(1)} %add.22, bf16[64,64]{1,0:T(8,128)(2,1)S(1)} %copy-done.10), kind=kOutput, calls=%fused_computation | convolution fusion | flops 134873088 | bytes 3154432 | tf_op jit(solution)/shard_map/dot_general | solution.py:133
  43.1 0.0 copy-start.1
  43.1 0.0 copy-start.4
  43.1 0.0 copy-start.5
  43.1 0.0 copy-start.6
  43.1 1.5 %convolution_convert_fusion.cots = bf16[4096,128]{1,0:T(8,128)(2,1)} fusion(bf16[4096,128]{0,1:T(8,128)(2,1)S(1)} %bitcast.44), kind=kOutput, calls=%fused_computation.1 | convolution fusion | flops 134774784 | bytes 2097152 | tf_op jit(solution)/shard_map/dot_general | solution.py:133
  44.6 0.0 all-to-all-done.1.parts
  44.6 0.0 copy-done.3
  44.6 0.3 shard_map.122
  44.9 21.5 %all_to_all.25 = bf16[128,8,128]{2,1,0:T(8,128)(2,1)S(1)} all-to-all(bf16[128,8,128]{2,1,0:T(8,128)(2,1)S(1)} %bitcast.39), channel_id=1, replica_groups=mesh['slab'=128,'chan'=4] {'slab'}, dimensions={0} | all-to-all | bytes 524288 | tf_op jit(solution)/shard_map/all_to_all | solution.py:554
  66.4 0.0 copy-done.1
  66.4 0.0 copy-done.4
  66.4 0.0 copy-done.5
  66.4 0.0 copy-done.6
  66.5 4.7 %shard_map.123 = (bf16[4096,128]{1,0:T(8,128)(2,1)}, bf16[1280,128]{1,0:T(8,128)(2,1)S(1)}) custom-call(bf16[1024,128]{1,0:T(8,128)(2,1)S(1)} %bitcast.38, f32[4096,128]{1,0:T(8,128)} %convolution_add_fusion.bases, bf16[4096,128]{1,0:T(8,128)(2,1)} %convolution_convert_fusion.cots, bf16[128,1024]{1,0:T(8,128)(2,1)S(1)} %copy-done.5, ...), custom_call_target="tpu_custom_call" | custom-call | flops 400000000 | bytes 5722112 | tf_op jit(solution)/shard_map/pallas_call | solution.py:266
  71.1 0.0 copy-start.8
  71.1 21.7 %all_to_all.26 = bf16[640,2,128]{2,1,0:T(2,128)(2,1)S(1)} all-to-all(bf16[640,2,128]{2,1,0:T(2,128)(2,1)S(1)} %bitcast.41), channel_id=1, replica_groups=mesh['slab'=128,'chan'=4] {'slab'}, dimensions={0} | all-to-all | bytes 655360 | tf_op jit(solution)/shard_map/all_to_all | solution.py:554
  92.8 2.0 %shard_map.124 = (f32[2,128,64]{2,1,0:T(8,128)S(1)}, bf16[512,128]{1,0:T(8,128)(2,1)}) custom-call(bf16[1280,128]{1,0:T(8,128)(2,1)S(1)} %bitcast.37, bf16[2,16,128,64]{3,2,1,0:T(8,128)(2,1)S(1)} %bitcast.36, bf16[256,128]{1,0:T(8,128)(2,1)S(1)} %copy-done.3, f32[8,128]{1,0:T(8,128)S(1)} %broadcast_in_dim.2.scale), custom_call_target="tpu_custom_call" | custom-call | flops 40000000 | bytes 1118208 | tf_op jit(solution)/shard_map/pallas_call | solution.py:266
  94.8 5.7 %all-to-all-start.4 = ((bf16[128,4,128]{2,1,0:T(4,128)(2,1)}), bf16[128,4,128]{2,1,0:T(4,128)(2,1)S(1)}, u32[]{:S(2)}, u32[]{:S(2)}) async-start(bf16[128,4,128]{2,1,0:T(4,128)(2,1)} %bitcast.15), calls=%async_computation.4 | async-start | bytes 262144 | tf_op jit(solution)/shard_map/all_to_all | solution.py:554
  100.5 0.0 copy-done.8
  100.5 0.4 fusion.21.point
  101.0 2.0 %shard_map.126 = f32[2,16,128,64]{3,2,1,0:T(8,128)} custom-call(f32[2,32,128]{2,1,0:T(8,128)S(1)} %get-tuple-element.40.coeff, f32[2,128,64]{2,1,0:T(8,128)S(1)} %get-tuple-element.41.hat), custom_call_target="tpu_custom_call" | custom-call | flops 8000000 | bytes 1146880 | tf_op jit(solution)/shard_map/pallas_call | solution.py:266
  103.0 10.3 %all-to-all-done.4 = bf16[128,4,128]{2,1,0:T(4,128)(2,1)S(1)} async-done(((bf16[128,4,128]{2,1,0:T(4,128)(2,1)}), bf16[128,4,128]{2,1,0:T(4,128)(2,1)S(1)}, u32[]{:S(2)}, u32[]{:S(2)}) %all-to-all-start.4) | async-done | bytes 131104 | tf_op jit(solution)/shard_map/all_to_all | solution.py:554
  113.3 1.5 %shard_map.125 = (bf16[1024,128]{1,0:T(8,128)(2,1)}, f32[16,64]{1,0:T(8,128)}, f32[1,64]{1,0:T(1,128)}) custom-call(bf16[512,128]{1,0:T(8,128)(2,1)S(1)} %bitcast.40, f32[32,4096]{1,0:T(8,128)S(1)} %fusion.21.point, bf16[256,640]{1,0:T(8,128)(2,1)S(1)} %copy-done.1), custom_call_target="tpu_custom_call" | custom-call | flops 8000000 | bytes 1249536 | tf_op jit(solution)/shard_map/pallas_call | solution.py:266
  (1 shorter events, 0.0 us)
Async XLA Ops:
  0.6 32.3 %copy-start = (bf16[2,16,64,4,32]{2,4,3,1,0:T(8,128)(2,1)S(1)}, bf16[2,16,64,4,32]{2,4,3,1,0:T(8,128)(2,1)}, u32[]{:S(2)}) copy-start(bf16[2,16,64,4,32]{2,4,3,1,0:T(8,128)(2,1)} %param.11) | copy-start | bytes 1572868
  3.1 29.8 %all-to-all-start = ((bf16[128,2,128]{2,1,0:T(2,128)(2,1)}), bf16[128,2,128]{2,1,0:T(2,128)(2,1)S(1)}, u32[]{:S(2)}, u32[]{:S(2)}) async-start(bf16[128,2,128]{2,1,0:T(2,128)(2,1)} %bitcast.47), calls=%async_computation | async-start | bytes 131072 | tf_op jit(solution)/shard_map/all_to_all | solution.py:554
  33.0 0.8 copy-start.2
  33.8 5.6 %copy-start.7 = (bf16[64,2,4096]{2,1,0:T(2,128)(2,1)S(1)}, bf16[64,2,4096]{2,1,0:T(2,128)(2,1)}, u32[]{:S(2)}) copy-start(bf16[64,2,4096]{2,1,0:T(2,128)(2,1)} %param.9) | copy-start | bytes 3145732
  35.4 9.1 %all-to-all-start.1 = ((bf16[4,128,128]{2,1,0:T(8,128)(2,1)}), bf16[4,128,128]{2,1,0:T(8,128)(2,1)S(1)}, u32[]{:S(2)}, u32[]{:S(2)}) async-start(bf16[4,128,128]{2,1,0:T(8,128)(2,1)} %get-tuple-element.26), calls=%async_computation.1 | async-start | bytes 262144 | tf_op jit(solution)/shard_map/all_to_all | solution.py:554
  39.4 1.2 %copy-start.9 = (bf16[64,2,4096]{2,1,0:T(2,128)(2,1)S(1)}, bf16[64,2,4096]{2,1,0:T(2,128)(2,1)}, u32[]{:S(2)}) copy-start(bf16[64,2,4096]{2,1,0:T(2,128)(2,1)} %param.10) | copy-start | bytes 3145732
  39.4 1.8 %copy-start.10 = (bf16[64,64]{1,0:T(8,128)(2,1)S(1)}, bf16[64,64]{1,0:T(8,128)(2,1)}, u32[]{:S(2)}) copy-start(bf16[64,64]{1,0:T(8,128)(2,1)} %param.12) | copy-start | bytes 24580
  41.3 3.3 %copy-start.3 = (bf16[256,128]{1,0:T(8,128)(2,1)S(1)}, bf16[256,128]{1,0:T(8,128)(2,1)}, u32[]{:S(2)}) copy-start(bf16[256,128]{1,0:T(8,128)(2,1)} %constant.54.tables) | copy-start | bytes 196612
  43.1 23.3 %copy-start.1 = (bf16[256,640]{1,0:T(8,128)(2,1)S(1)}, bf16[256,640]{1,0:T(8,128)(2,1)}, u32[]{:S(2)}) copy-start(bf16[256,640]{1,0:T(8,128)(2,1)} %constant.53.wides.wide.wide_z) | copy-start | bytes 983044
  43.1 23.3 %copy-start.4 = (bf16[512,256]{1,0:T(8,128)(2,1)S(1)}, bf16[512,256]{1,0:T(8,128)(2,1)}, u32[]{:S(2)}) copy-start(bf16[512,256]{1,0:T(8,128)(2,1)} %constant.55.tall) | copy-start | bytes 786436
  43.1 23.3 %copy-start.5 = (bf16[128,1024]{1,0:T(8,128)(2,1)S(1)}, bf16[128,1024]{1,0:T(8,128)(2,1)}, u32[]{:S(2)}) copy-start(bf16[128,1024]{1,0:T(8,128)(2,1)} %get-tuple-element.33.own) | copy-start | bytes 786436
  43.1 23.3 %copy-start.6 = (bf16[336,128]{1,0:T(8,128)(2,1)S(1)}, bf16[336,128]{1,0:T(8,128)(2,1)}, u32[]{:S(2)}) copy-start(bf16[336,128]{1,0:T(8,128)(2,1)} %constant.56.tables) | copy-start | bytes 258052
  71.1 29.4 %copy-start.8 = (bf16[4096,128]{1,0:T(8,128)(2,1)S(1)}, bf16[4096,128]{1,0:T(8,128)(2,1)}, u32[]{:S(2)}) copy-start(bf16[4096,128]{1,0:T(8,128)(2,1)} %get-tuple-element.38) | copy-start | bytes 3145732
  94.8 18.5 %all-to-all-start.4 = ((bf16[128,4,128]{2,1,0:T(4,128)(2,1)}), bf16[128,4,128]{2,1,0:T(4,128)(2,1)S(1)}, u32[]{:S(2)}, u32[]{:S(2)}) async-start(bf16[128,4,128]{2,1,0:T(4,128)(2,1)} %bitcast.15), calls=%async_computation.4 | async-start | bytes 262144 | tf_op jit(solution)/shard_map/all_to_all | solution.py:554

commit v7 on v6

--- a/solution.py
+++ b/solution.py
@@ -569,23 +569,21 @@
     wide = table(WIDE)
     rows = jnp.transpose(field.reshape(C, PLANES, 32, LANES), (0, 2, 1, 3)).reshape(CELLS, LANES)
     first, own = own_modes(rows, wide)
+    cotangent, first = lax.optimization_barrier((cotangent, first))
+    cot = jnp.transpose(cotangent, (2, 1, 0)).reshape(CELLS, LANES)
+    cot = mm(cot, 0.5 * jnp.eye(LANES, dtype=BF16)).astype(BF16)
     pencils = over(first.reshape(SLAB, PLANES, LANES), "slab").reshape(NX, LANES)
+    pencils, cot = lax.optimization_barrier((pencils, cot))
     coeff, parts = mix(pencils, weight, tables)
 
-    field, cotangent, own_rows, parts = lax.optimization_barrier(
-        (field, cotangent, own_rows, parts)
-    )
+    field, own_rows, parts = lax.optimization_barrier((field, own_rows, parts))
     kz_weight = jnp.where(lax.axis_index("slab") < HIGH, 1.0, 2.0) / (NX * NY * NZ)
     scale = jnp.full((8, LANES), kz_weight, F32)
     cells = jnp.transpose(field, (2, 1, 0)).reshape(CELLS, LANES)
-    cot = jnp.transpose(cotangent, (2, 1, 0)).reshape(CELLS, LANES)
-    cot = mm(cot, 0.5 * jnp.eye(LANES, dtype=BF16)).astype(BF16)
     bias = jnp.tile(point_bias.astype(F32), 2)[None]
     base = mm(cells, paired(point_weight)) + bias
     parts = over(parts, "chan")
-    parts, base, cot, own_rows, scale = lax.optimization_barrier(
-        (parts, base, cot, own_rows, scale)
-    )
+    parts, base, own_rows, scale = lax.optimization_barrier((parts, base, own_rows, scale))
 
     planes = spread_planes(parts, tables)
     modes = over(planes.reshape(SLAB, 8, LANES), "slab").reshape(SLAB * 8, LANES)

time: 115 us -> 114 us (level)
  local copies, waits for them, and re-layouts: 4.1 us -> 1.32 us
  waiting for transfers between devices: 20.2 us -> 21.8 us
    all_to_all x3, waiting for transfers between devices: 20.2 us -> 21.8 us  [over(): return lax.all_to_all(values, axis, split_axis=0, concat_axis=0, tiled=True)]
    unnamed x22, local copies, waits for them, and re-layouts: 1.5 us -> 0.07 us
  transfers between devices with their start and end apart: 3 -> 3, of which waited for: 2 -> 3; matrix products, arithmetic and copies ran while one was open for 6% -> 4% of each run, Pallas kernels for 2% -> 2%
where the time goes in v7:
time: 114 us
  blocking collectives  43.5 us (38%)
  starting transfers between devices  28.1 us (25%)
  waiting for transfers between devices  21.8 us (19%)
  Pallas kernels  14.5 us (13%)
  matrix products  3.73 us (3%)
  local copies, waits for them, and re-layouts  1.32 us (1%)
    all_to_all x2, blocking collectives, over(): return lax.all_to_all(values, axis, split_axis=0, concat_axis=0, tiled=True)  43.5 us
    all_to_all x3, starting transfers between devices, over(): return lax.all_to_all(values, axis, split_axis=0, concat_axis=0, tiled=True)  28.1 us
    all_to_all x3, waiting for transfers between devices, over(): return lax.all_to_all(values, axis, split_axis=0, concat_axis=0, tiled=True)  21.8 us
    pallas_call x7, Pallas kernels, call(): pl.pallas_call(kernel, out_shape=shapes, in_specs=places(len(operands), a...  14.5 us
    dot_general x3, matrix products, mm(): return jnp.dot(left, right, preferred_element_type=F32)  3.73 us
  transfers between devices with their start and end apart: 3, of which 3 were waited for; matrix products, arithmetic and copies ran while one was open for 4% of the time, Pallas kernels for 2%

profile of v7, /device:TPU:1, one launch (start us, length us, event | category | flops | bytes accessed | tf_op | source)
XLA Modules:
  0.0 114.0 jit_solution(9649225980767194646)
XLA Ops:
  0.6 0.0 copy-start.8
  0.6 2.5 %shard_map.120 = (bf16[256,128]{1,0:T(8,128)(2,1)}, bf16[128,1024]{1,0:T(8,128)(2,1)}) custom-call(bf16[4096,128]{1,0:T(8,128)(2,1)} %bitcast.43, bf16[256,640]{1,0:T(8,128)(2,1)} %constant.53.wides.wide.wide_z), custom_call_target="tpu_custom_call" | custom-call | flops 4000000 | bytes 1703936 | tf_op jit(solution)/shard_map/pallas_call | solution.py:266
  3.1 18.4 %all-to-all-start = ((bf16[128,2,128]{2,1,0:T(2,128)(2,1)}), bf16[128,2,128]{2,1,0:T(2,128)(2,1)S(1)}, u32[]{:S(2)}, u32[]{:S(2)}) async-start(bf16[128,2,128]{2,1,0:T(2,128)(2,1)} %bitcast.47), calls=%async_computation | async-start | bytes 131072 | tf_op jit(solution)/shard_map/all_to_all | solution.py:554
  21.6 0.0 copy-done.8
  21.6 0.0 copy-start.9
  21.6 0.0 copy-start.10
  21.6 0.0 copy-start
  21.6 0.0 copy-start.2
  21.6 0.6 copy.16
  22.2 0.0 copy-start.6
  22.2 1.5 %convolution_convert_fusion.cots = bf16[4096,128]{1,0:T(8,128)(2,1)} fusion(bf16[4096,128]{0,1:T(8,128)(2,1)S(1)} %bitcast.45), kind=kOutput, calls=%fused_computation.1 | convolution fusion | flops 134774784 | bytes 2097152 | tf_op jit(solution)/shard_map/dot_general | solution.py:133
  23.7 0.0 copy-done.9
  23.7 0.0 copy-done.10
  23.7 0.1 add.22
  23.8 0.1 fusion.15
  23.8 9.1 %all-to-all-done = bf16[128,2,128]{2,1,0:T(2,128)(2,1)S(1)} async-done(((bf16[128,2,128]{2,1,0:T(2,128)(2,1)}), bf16[128,2,128]{2,1,0:T(2,128)(2,1)S(1)}, u32[]{:S(2)}, u32[]{:S(2)}) %all-to-all-start) | async-done | bytes 65568 | tf_op jit(solution)/shard_map/all_to_all | solution.py:554
  33.0 0.0 copy-done
  33.0 0.0 copy-done.2
  33.0 1.6 %shard_map.121 = (f32[2,32,128]{2,1,0:T(8,128)S(1)}, bf16[4,128,128]{2,1,0:T(8,128)(2,1)}) custom-call(bf16[256,128]{1,0:T(8,128)(2,1)S(1)} %bitcast.42, bf16[2,16,128,64]{3,2,1,0:T(8,128)(2,1)S(1)} %bitcast.35, bf16[256,128]{1,0:T(8,128)(2,1)S(1)} %copy-done.2), custom_call_target="tpu_custom_call" | custom-call | flops 4000000 | bytes 819200 | tf_op jit(solution)/shard_map/pallas_call | solution.py:266
  34.6 4.0 %all-to-all-start.1 = ((bf16[4,128,128]{2,1,0:T(8,128)(2,1)}), bf16[4,128,128]{2,1,0:T(8,128)(2,1)S(1)}, u32[]{:S(2)}, u32[]{:S(2)}) async-start(bf16[4,128,128]{2,1,0:T(8,128)(2,1)} %get-tuple-element.31), calls=%async_computation.1 | async-start | bytes 262144 | tf_op jit(solution)/shard_map/all_to_all | solution.py:554
  38.6 0.0 copy-done.6
  38.6 0.6 copy.17
  39.2 0.0 copy-start.1
  39.2 0.0 copy-start.3
  39.2 0.0 copy-start.4
  39.2 0.0 copy-start.5
  39.2 1.8 %convolution_add_fusion.bases = f32[4096,128]{1,0:T(8,128)} fusion(bf16[4096,128]{0,1:T(8,128)(2,1)S(1)} %bitcast.44, f32[128]{0:T(128)S(1)} %add.22, bf16[64,64]{1,0:T(8,128)(2,1)S(1)} %copy-done.9), kind=kOutput, calls=%fused_computation | convolution fusion | flops 134873088 | bytes 3154432 | tf_op jit(solution)/shard_map/dot_general | solution.py:133
  41.1 2.4 %all-to-all-done.1.parts = bf16[4,128,128]{2,1,0:T(8,128)(2,1)S(1)} async-done(((bf16[4,128,128]{2,1,0:T(8,128)(2,1)}), bf16[4,128,128]{2,1,0:T(8,128)(2,1)S(1)}, u32[]{:S(2)}, u32[]{:S(2)}) %all-to-all-start.1) | async-done | bytes 131104 | tf_op jit(solution)/shard_map/all_to_all | solution.py:554
  43.4 0.3 shard_map.122
  43.7 21.8 %all_to_all.25 = bf16[128,8,128]{2,1,0:T(8,128)(2,1)S(1)} all-to-all(bf16[128,8,128]{2,1,0:T(8,128)(2,1)S(1)} %bitcast.39), channel_id=1, replica_groups=mesh['slab'=128,'chan'=4] {'slab'}, dimensions={0} | all-to-all | bytes 524288 | tf_op jit(solution)/shard_map/all_to_all | solution.py:554
  65.6 0.0 copy-done.1
  65.6 0.0 copy-done.3
  65.6 0.0 copy-done.4
  65.6 0.0 copy-done.5
  65.6 4.7 %shard_map.123 = (bf16[4096,128]{1,0:T(8,128)(2,1)}, bf16[1280,128]{1,0:T(8,128)(2,1)S(1)}) custom-call(bf16[1024,128]{1,0:T(8,128)(2,1)S(1)} %bitcast.38, f32[4096,128]{1,0:T(8,128)} %convolution_add_fusion.bases, bf16[4096,128]{1,0:T(8,128)(2,1)} %convolution_convert_fusion.cots, bf16[128,1024]{1,0:T(8,128)(2,1)S(1)} %copy-done.4, ...), custom_call_target="tpu_custom_call" | custom-call | flops 400000000 | bytes 5722112 | tf_op jit(solution)/shard_map/pallas_call | solution.py:266
  70.3 0.0 copy-start.7
  70.3 21.7 %all_to_all.26 = bf16[640,2,128]{2,1,0:T(2,128)(2,1)S(1)} all-to-all(bf16[640,2,128]{2,1,0:T(2,128)(2,1)S(1)} %bitcast.41), channel_id=1, replica_groups=mesh['slab'=128,'chan'=4] {'slab'}, dimensions={0} | all-to-all | bytes 655360 | tf_op jit(solution)/shard_map/all_to_all | solution.py:554
  92.0 2.0 %shard_map.124 = (f32[2,128,64]{2,1,0:T(8,128)S(1)}, bf16[512,128]{1,0:T(8,128)(2,1)}) custom-call(bf16[1280,128]{1,0:T(8,128)(2,1)S(1)} %bitcast.37, bf16[2,16,128,64]{3,2,1,0:T(8,128)(2,1)S(1)} %bitcast.36, bf16[256,128]{1,0:T(8,128)(2,1)S(1)} %copy-done.2, f32[8,128]{1,0:T(8,128)S(1)} %broadcast_in_dim.2.scale), custom_call_target="tpu_custom_call" | custom-call | flops 40000000 | bytes 1118208 | tf_op jit(solution)/shard_map/pallas_call | solution.py:266
  94.0 5.7 %all-to-all-start.4 = ((bf16[128,4,128]{2,1,0:T(4,128)(2,1)}), bf16[128,4,128]{2,1,0:T(4,128)(2,1)S(1)}, u32[]{:S(2)}, u32[]{:S(2)}) async-start(bf16[128,4,128]{2,1,0:T(4,128)(2,1)} %bitcast.15), calls=%async_computation.4 | async-start | bytes 262144 | tf_op jit(solution)/shard_map/all_to_all | solution.py:554
  99.7 0.0 copy-done.7
  99.7 0.4 fusion.21.point
  100.1 2.0 %shard_map.126 = f32[2,16,128,64]{3,2,1,0:T(8,128)} custom-call(f32[2,32,128]{2,1,0:T(8,128)S(1)} %get-tuple-element.44.coeff, f32[2,128,64]{2,1,0:T(8,128)S(1)} %get-tuple-element.45.hat), custom_call_target="tpu_custom_call" | custom-call | flops 8000000 | bytes 1146880 | tf_op jit(solution)/shard_map/pallas_call | solution.py:266
  102.2 10.3 %all-to-all-done.4 = bf16[128,4,128]{2,1,0:T(4,128)(2,1)S(1)} async-done(((bf16[128,4,128]{2,1,0:T(4,128)(2,1)}), bf16[128,4,128]{2,1,0:T(4,128)(2,1)S(1)}, u32[]{:S(2)}, u32[]{:S(2)}) %all-to-all-start.4) | async-done | bytes 131104 | tf_op jit(solution)/shard_map/all_to_all | solution.py:554
  112.5 1.5 %shard_map.125 = (bf16[1024,128]{1,0:T(8,128)(2,1)}, f32[16,64]{1,0:T(8,128)}, f32[1,64]{1,0:T(1,128)}) custom-call(bf16[512,128]{1,0:T(8,128)(2,1)S(1)} %bitcast.40, f32[32,4096]{1,0:T(8,128)S(1)} %fusion.21.point, bf16[256,640]{1,0:T(8,128)(2,1)S(1)} %copy-done.1), custom_call_target="tpu_custom_call" | custom-call | flops 8000000 | bytes 1249536 | tf_op jit(solution)/shard_map/pallas_call | solution.py:266
  (3 shorter events, 0.0 us)
Async XLA Ops:
  0.6 20.9 %copy-start.8 = (bf16[64,2,4096]{2,1,0:T(2,128)(2,1)S(1)}, bf16[64,2,4096]{2,1,0:T(2,128)(2,1)}, u32[]{:S(2)}) copy-start(bf16[64,2,4096]{2,1,0:T(2,128)(2,1)} %param.10) | copy-start | bytes 3145732
  3.1 29.8 %all-to-all-start = ((bf16[128,2,128]{2,1,0:T(2,128)(2,1)}), bf16[128,2,128]{2,1,0:T(2,128)(2,1)S(1)}, u32[]{:S(2)}, u32[]{:S(2)}) async-start(bf16[128,2,128]{2,1,0:T(2,128)(2,1)} %bitcast.47), calls=%async_computation | async-start | bytes 131072 | tf_op jit(solution)/shard_map/all_to_all | solution.py:554
  21.6 2.1 %copy-start.9 = (bf16[64,64]{1,0:T(8,128)(2,1)S(1)}, bf16[64,64]{1,0:T(8,128)(2,1)}, u32[]{:S(2)}) copy-start(bf16[64,64]{1,0:T(8,128)(2,1)} %param.12) | copy-start | bytes 24580
  21.6 2.1 %copy-start.10 = (bf16[64]{0:T(256)(128)(2,1)S(1)}, bf16[64]{0:T(256)(128)(2,1)}, u32[]{:S(2)}) copy-start(bf16[64]{0:T(256)(128)(2,1)} %param.13) | copy-start | bytes 388
  21.6 11.4 %copy-start = (bf16[2,16,64,4,32]{2,4,3,1,0:T(8,128)(2,1)S(1)}, bf16[2,16,64,4,32]{2,4,3,1,0:T(8,128)(2,1)}, u32[]{:S(2)}) copy-start(bf16[2,16,64,4,32]{2,4,3,1,0:T(8,128)(2,1)} %param.11) | copy-start | bytes 1572868
  21.6 11.4 %copy-start.2 = (bf16[256,128]{1,0:T(8,128)(2,1)S(1)}, bf16[256,128]{1,0:T(8,128)(2,1)}, u32[]{:S(2)}) copy-start(bf16[256,128]{1,0:T(8,128)(2,1)} %constant.54.tables) | copy-start | bytes 196612
  22.2 16.4 %copy-start.6 = (bf16[64,2,4096]{2,1,0:T(2,128)(2,1)S(1)}, bf16[64,2,4096]{2,1,0:T(2,128)(2,1)}, u32[]{:S(2)}) copy-start(bf16[64,2,4096]{2,1,0:T(2,128)(2,1)} %param.9) | copy-start | bytes 3145732
  34.6 8.8 %all-to-all-start.1 = ((bf16[4,128,128]{2,1,0:T(8,128)(2,1)}), bf16[4,128,128]{2,1,0:T(8,128)(2,1)S(1)}, u32[]{:S(2)}, u32[]{:S(2)}) async-start(bf16[4,128,128]{2,1,0:T(8,128)(2,1)} %get-tuple-element.31), calls=%async_computation.1 | async-start | bytes 262144 | tf_op jit(solution)/shard_map/all_to_all | solution.py:554
  39.2 26.4 %copy-start.1 = (bf16[256,640]{1,0:T(8,128)(2,1)S(1)}, bf16[256,640]{1,0:T(8,128)(2,1)}, u32[]{:S(2)}) copy-start(bf16[256,640]{1,0:T(8,128)(2,1)} %constant.53.wides.wide.wide_z) | copy-start | bytes 983044
  39.2 26.4 %copy-start.3 = (bf16[512,256]{1,0:T(8,128)(2,1)S(1)}, bf16[512,256]{1,0:T(8,128)(2,1)}, u32[]{:S(2)}) copy-start(bf16[512,256]{1,0:T(8,128)(2,1)} %constant.55.tall) | copy-start | bytes 786436
  39.2 26.4 %copy-start.4 = (bf16[128,1024]{1,0:T(8,128)(2,1)S(1)}, bf16[128,1024]{1,0:T(8,128)(2,1)}, u32[]{:S(2)}) copy-start(bf16[128,1024]{1,0:T(8,128)(2,1)} %get-tuple-element.37.own) | copy-start | bytes 786436
  39.2 26.4 %copy-start.5 = (bf16[336,128]{1,0:T(8,128)(2,1)S(1)}, bf16[336,128]{1,0:T(8,128)(2,1)}, u32[]{:S(2)}) copy-start(bf16[336,128]{1,0:T(8,128)(2,1)} %constant.56.tables) | copy-start | bytes 258052
  70.3 29.4 %copy-start.7 = (bf16[4096,128]{1,0:T(8,128)(2,1)S(1)}, bf16[4096,128]{1,0:T(8,128)(2,1)}, u32[]{:S(2)}) copy-start(bf16[4096,128]{1,0:T(8,128)(2,1)} %get-tuple-element.42) | copy-start | bytes 3145732
  94.0 18.5 %all-to-all-start.4 = ((bf16[128,4,128]{2,1,0:T(4,128)(2,1)}), bf16[128,4,128]{2,1,0:T(4,128)(2,1)S(1)}, u32[]{:S(2)}, u32[]{:S(2)}) async-start(bf16[128,4,128]{2,1,0:T(4,128)(2,1)} %bitcast.15), calls=%async_computation.4 | async-start | bytes 262144 | tf_op jit(solution)/shard_map/all_to_all | solution.py:554
